TPU v7x, 512 devices: a whole 4x8x8 slice. The times are simulated.
512 devices in a mesh: run: 8 (over z), space: 64 (over x, y, core).
Axes of the slice: x: 4, y: 8, z: 8, core: 2. Of those that a mesh axis runs over, the one named last changes fastest.
Arguments:
- start_field: float32 [8, 64, 256, 512], P('run', 'space'), may hold values from -19 to 19
- viscosity: float32 [64, 256, 512], P('space'), may hold values from 0.5 to 1
- diffusivity: float32 [8], replicated, may hold values from 0.04 to 0.1
- velocity: float32 [8, 3], replicated, may hold values from -0.13 to 0.13
- assignment: int32 [8], replicated, may hold values from 0 to 7, each once
- child_order: int32 [7, 8], replicated, may hold values from 0 to 7, each once within a row
- keep_ranks: int32 [7], replicated, may hold values from 2 to 4
Outputs:
- root_factor: float32 [4, 64, 256, 512], P(None, 'space', 'run')
Inputs may be any that keep to these rules, and one draw needn't show every extreme that they name: `assignment`: each sample appears once; runs read the first 8 entries. `child_order`: each row holds every number once.
All inputs are finite; a program needn't handle non-finite values.
Results may differ from a plain program's by a relative error of at most 0.0003.
Values sent between devices are 32-bit elements; how exact they have to be, the bound alone decides.
No kernel may reach another device: no remote copies, remote signals or barrier semaphores. Data moves between devices by JAX's collectives and lax.ppermute only.
A program may use at most 128 MiB of HBM per device.

v0:
```python
import math

import jax
import jax.numpy as jnp
from jax import lax
from jax.sharding import PartitionSpec as P

STEPS = 4
SUBITERS = 3


EPS = 1e-06
EXACT = lax.Precision.HIGHEST


def extended(block, sides, width):
    for axis, dim in sides:
        count = lax.axis_size(axis)
        forward = [(i, i + 1) for i in range(count - 1)]
        backward = [(target, source) for source, target in forward]
        low = lax.ppermute(
            lax.slice_in_dim(block, block.shape[dim] - width, None, axis=dim), axis, forward
        )
        high = lax.ppermute(lax.slice_in_dim(block, 0, width, axis=dim), axis, backward)
        block = jnp.concatenate([low, block, high], axis=dim)
    return block


def swapped(block, axis, distance):
    count = lax.axis_size(axis)
    route = []
    for low in range(count):
        high = low | 1 << distance
        if high != low and high < count:
            route += [(low, high), (high, low)]
    return lax.ppermute(block, axis, route)


def neighbour(padded, direction, offset):
    window = [slice(1, -1), slice(1, -1), slice(1, -1)]
    window[direction] = slice(1 + offset, padded.shape[direction] - 1 + offset)
    return padded[tuple(window)]


def advance(ext_field, ext_visc, diffuse_rate, velocity_now):
    padded_state = jnp.pad(ext_field, ((0, 0), (1, 1), (1, 1)))
    padded_visc = jnp.pad(ext_visc, ((0, 0), (1, 1), (1, 1)))
    centre = padded_state[1:-1, 1:-1, 1:-1]
    visc_mid = padded_visc[1:-1, 1:-1, 1:-1]
    updated = centre
    for direction in range(3):
        ahead_cell = neighbour(padded_state, direction, 1)
        behind_cell = neighbour(padded_state, direction, -1)
        face_ahead = 0.5 * diffuse_rate * (visc_mid + neighbour(padded_visc, direction, 1))
        face_behind = 0.5 * diffuse_rate * (visc_mid + neighbour(padded_visc, direction, -1))
        speed_now = velocity_now[direction]
        updated = (
            updated + face_ahead * (ahead_cell - centre) - face_behind * (centre - behind_cell)
        )
        updated = (
            updated
            - jnp.maximum(speed_now, 0.0) * (centre - behind_cell)
            - jnp.minimum(speed_now, 0.0) * (ahead_cell - centre)
        )
    return updated


def leading(gram_matrix, kept_rank, snap_width):
    full_size = 2 * snap_width
    row_ids = jnp.arange(full_size, dtype=jnp.float32)[:, None]
    col_ids = jnp.arange(snap_width, dtype=jnp.float32)[None, :]
    start_basis = jnp.cos(math.pi * (row_ids + 0.5) * (col_ids + 0.5) / full_size) * math.sqrt(
        1.0 / snap_width
    )
    live_cols = (jnp.arange(snap_width, dtype=jnp.int32) < kept_rank).astype(jnp.float32)
    current = start_basis * live_cols[None, :]
    for sweep_index in range(SUBITERS):
        image_cols = jnp.dot(gram_matrix, current, precision=EXACT) * live_cols[None, :]
        inner_gram = jnp.dot(image_cols.T, image_cols, precision=EXACT) + jnp.diag(1.0 - live_cols)
        factor_low = jnp.linalg.cholesky(inner_gram)
        current = jax.scipy.linalg.solve_triangular(factor_low, image_cols.T, lower=True).T
    return current


def pick(lookup_table, position):
    places = jnp.arange(lookup_table.shape[0], dtype=jnp.int32) == position
    selector = places.reshape((-1,) + (1,) * (lookup_table.ndim - 1))
    return jnp.sum(jnp.where(selector, lookup_table, jnp.zeros_like(lookup_table)), axis=0)


def order_matrix(row_perm):
    full_size = row_perm.shape[-1]
    targets = jnp.arange(full_size, dtype=jnp.int32)
    return (row_perm[..., :, None] == targets).astype(jnp.float32)


def own_block(full_rows, run_index, run_count, snap_width, planes, row_count, columns):
    shaped = full_rows.reshape(snap_width, planes, row_count, columns)
    block_rows = row_count // run_count
    return lax.dynamic_slice_in_dim(shaped, run_index * block_rows, block_rows, 2)


def local(start_field, viscosity, diffusivity, velocity, assignment, child_order, keep_ranks):
    run_count = lax.axis_size("run")
    space_count = lax.axis_size("space")
    run_index = lax.axis_index("run")
    chosen = pick(assignment, run_index)
    diffuse_rate = pick(diffusivity, chosen)
    velocity_now = pick(velocity, chosen)
    current = start_field[0]
    planes, row_count, columns = current.shape
    cell_count = planes * row_count * columns * space_count
    snap_width = STEPS
    snapshots = []
    visc_ext = viscosity
    for step_index in range(STEPS):
        if step_index == 0:
            both_ext = extended(jnp.stack([current, viscosity]), (("space", 1),), 1)
            state_ext = both_ext[0]
            visc_ext = both_ext[1]
        else:
            state_ext = extended(current, (("space", 0),), 1)
        current = advance(state_ext, visc_ext, diffuse_rate, velocity_now)
        snapshots.append(current)
    leaf_rows = jnp.stack(snapshots).reshape(snap_width, -1)
    squares = lax.psum(jnp.sum(leaf_rows * leaf_rows, axis=1), "space")
    leaf_rows = leaf_rows / jnp.sqrt(squares / cell_count + EPS)[:, None]
    levels_total = run_count.bit_length() - 1
    factor_rows = leaf_rows
    for tree_level in range(levels_total):
        partner = swapped(factor_rows, "run", tree_level)
        upper_bit = run_index >> tree_level & 1
        lower_side = jnp.where(upper_bit == 1, partner, factor_rows)
        upper_side = jnp.where(upper_bit == 1, factor_rows, partner)
        stacked = jnp.concatenate([lower_side, upper_side], axis=0)
        gram_matrix = lax.psum(jnp.dot(stacked, stacked.T, precision=EXACT), "space")
        node_id = run_count - (run_count >> tree_level) + (run_index >> tree_level + 1)
        reorder = order_matrix(pick(child_order, node_id))
        kept_rank = pick(keep_ranks, node_id)
        column_scale = jnp.ones((2 * snap_width,), jnp.float32)
        gram_matrix = gram_matrix * column_scale[:, None] * column_scale[None, :] / cell_count
        gram_matrix = jnp.dot(
            jnp.dot(reorder, gram_matrix, precision=EXACT), reorder.T, precision=EXACT
        )
        basis_now = leading(gram_matrix, kept_rank, snap_width)
        basis_now = jnp.dot(reorder.T, basis_now, precision=EXACT)
        factor_rows = jnp.dot((basis_now * column_scale[:, None]).T, stacked, precision=EXACT)
    result = own_block(factor_rows, run_index, run_count, snap_width, planes, row_count, columns)
    return result


def solution(mesh):
    in_specs = (P("run", "space", None, None), P("space", None, None), P(), P(), P(), P(), P())
    out_specs = P(None, "space", "run", None)
    return jax.shard_map(local, mesh=mesh, in_specs=in_specs, out_specs=out_specs, check_vma=False)
```

profile of v0, /device:TPU:1, one launch (start us, length us, event | category | flops | bytes accessed | tf_op | source)
XLA Modules:
  0.0 906.3 jit_solution(2372585501499943864)
XLA Ops:
  2.4 8.8 collective-permute-start
  20.7 4.4 collective-permute-done.1
  31.5 4.4 collective-permute-start.3
  35.9 4.9 collective-permute-done.2
  45.4 4.4 collective-permute-start.5
  49.8 4.9 collective-permute-done.4
  59.3 4.4 collective-permute-start.7
  74.1 122.5 %psum.28 = f32[4]{0:T(128)S(1)} all-reduce(f32[4]{0:T(128)S(1)} %multiply_reduce_fusion), channel_id=1, replica_groups=mesh['run'=8,'space'=64] {'space'}, use_global_device_ids=true, to_apply=%region_7.8 | all-reduce | flops 4 | bytes 32 | tf_op jit(solution)/shard_map/psum | solution.py:126
  199.6 4.0 collective-permute-start.8
  206.4 42.4 %collective-permute-done.8 = f32[4,131072]{1,0:T(4,128)} collective-permute-done((f32[4,131072]{1,0:T(4,128)}, f32[4,131072]{1,0:T(4,128)}, u32[]{:S(2)}, u32[]{:S(2)}) %collective-permute-start.8) | collective-permute-done | bytes 2097184 | tf_op jit(solution)/shard_map/ppermute | solution.py:36
  248.8 3.7 broadcast_select_fusion.1
  253.9 9.3 %fusion.5 = f32[8,8]{1,0:T(8,128)S(1)} fusion(f32[4,131072]{1,0:T(4,128)S(1)} %get-tuple-element.25, f32[4,131072]{1,0:T(4,128)S(1)} %get-tuple-element.24), kind=kOutput, calls=%fused_computation.8 | convolution fusion | flops 101711872 | bytes 4194560 | tf_op jit(solution)/shard_map/dot_general | solution.py:136
  263.2 125.1 %psum.29 = f32[8,8]{1,0:T(8,128)S(1)} all-reduce(f32[8,8]{1,0:T(8,128)S(1)} %fusion.5), channel_id=1, replica_groups=mesh['run'=8,'space'=64] {'space'}, use_global_device_ids=true, to_apply=%region_8.9 | all-reduce | flops 64 | bytes 512 | tf_op jit(solution)/shard_map/psum | solution.py:136
  397.0 6.2 fusion.4
  403.2 6.0 collective-permute-start.9
  411.8 87.9 %collective-permute-done.9 = f32[4,131072]{1,0:T(4,128)} collective-permute-done((f32[4,131072]{1,0:T(4,128)}, f32[4,131072]{1,0:T(4,128)}, u32[]{:S(2)}, u32[]{:S(2)}) %collective-permute-start.9) | collective-permute-done | bytes 2097184 | tf_op jit(solution)/shard_map/ppermute | solution.py:36
  503.9 9.3 %fusion.3 = f32[8,8]{1,0:T(8,128)S(1)} fusion(f32[4,131072]{1,0:T(4,128)S(1)} %get-tuple-element.23, f32[4,131072]{1,0:T(4,128)S(1)} %get-tuple-element.22), kind=kOutput, calls=%fused_computation.6 | convolution fusion | flops 101711872 | bytes 4194560 | tf_op jit(solution)/shard_map/dot_general | solution.py:136
  513.2 124.6 %psum.30 = f32[8,8]{1,0:T(8,128)S(1)} all-reduce(f32[8,8]{1,0:T(8,128)S(1)} %fusion.3), channel_id=1, replica_groups=mesh['run'=8,'space'=64] {'space'}, use_global_device_ids=true, to_apply=%region_12.15 | all-reduce | flops 64 | bytes 512 | tf_op jit(solution)/shard_map/psum | solution.py:136
  646.5 6.2 fusion.2
  652.7 8.7 collective-permute-start.10
  662.7 89.6 %collective-permute-done.10 = f32[4,131072]{1,0:T(4,128)} collective-permute-done((f32[4,131072]{1,0:T(4,128)}, f32[4,131072]{1,0:T(4,128)}, u32[]{:S(2)}, u32[]{:S(2)}) %collective-permute-start.10) | collective-permute-done | bytes 2097184 | tf_op jit(solution)/shard_map/ppermute | solution.py:36
  756.7 9.3 %fusion.1 = f32[8,8]{1,0:T(8,128)S(1)} fusion(f32[4,131072]{1,0:T(4,128)S(1)} %get-tuple-element.21, f32[4,131072]{1,0:T(4,128)S(1)} %get-tuple-element.20), kind=kOutput, calls=%fused_computation.4 | convolution fusion | flops 101711872 | bytes 4194560 | tf_op jit(solution)/shard_map/dot_general | solution.py:136
  766.0 124.7 %psum.31 = f32[8,8]{1,0:T(8,128)S(1)} all-reduce(f32[8,8]{1,0:T(8,128)S(1)} %fusion.1), channel_id=1, replica_groups=mesh['run'=8,'space'=64] {'space'}, use_global_device_ids=true, to_apply=%region_14.17 | all-reduce | flops 64 | bytes 512 | tf_op jit(solution)/shard_map/psum | solution.py:136
  899.3 5.3 fusion
  (173 shorter events, 80.2 us)
Async XLA Ops:
  0.0 25.1 %copy-start.6 = (f32[1,256,512]{2,1,0:T(8,128)S(1)}, f32[1,256,512]{2,1,0:T(8,128)}, u32[]{:S(2)}) copy-start(f32[1,256,512]{2,1,0:T(8,128)} %param.11) | copy-start | bytes 1572868
  0.0 25.1 %copy-start.5 = (f32[1,1,256,512]{3,2,1,0:T(8,128)S(1)}, f32[1,1,256,512]{3,2,1,0:T(8,128)}, u32[]{:S(2)}) copy-start(f32[1,1,256,512]{3,2,1,0:T(8,128)} %param.10) | copy-start | bytes 1572868
  0.0 13.1 %copy-start.11 = (s32[8]{0:T(128)S(1)}, s32[8]{0:T(128)}, u32[]{:S(2)}) copy-start(s32[8]{0:T(128)} %param.14) | copy-start | bytes 100
  0.0 14.4 %copy-start.9 = (f32[8,3]{0,1:T(4,128)S(1)}, f32[8,3]{0,1:T(4,128)}, u32[]{:S(2)}) copy-start(f32[8,3]{0,1:T(4,128)} %param.13) | copy-start | bytes 292
  0.0 18.8 %copy-start.12 = (f32[8]{0:T(128)S(1)}, f32[8]{0:T(128)}, u32[]{:S(2)}) copy-start(f32[8]{0:T(128)} %param.12) | copy-start | bytes 100
  2.4 18.3 %collective-permute-start = (f32[2,1,256,512]{3,2,1,0:T(8,128)}, f32[2,1,256,512]{3,2,1,0:T(8,128)S(1)}, u32[]{:S(2)}, u32[]{:S(2)}) collective-permute-start(f32[2,1,256,512]{3,2,1,0:T(8,128)} %pad_maximum_fusion.11), channel_id=1, source_target_pairs={{1,0},{2,1},{3,2},{4,3},{5,4},{6,5},{7,6},{8,7},{9,8},{10,9},{11,1... | collective-permute-start | bytes 3145736 | tf_op jit(solution)/shard_map/ppermute | solution.py:24
  11.1 14.0 %collective-permute-start.1 = (f32[2,1,256,512]{3,2,1,0:T(8,128)}, f32[2,1,256,512]{3,2,1,0:T(8,128)}, u32[]{:S(2)}, u32[]{:S(2)}) collective-permute-start(f32[2,1,256,512]{3,2,1,0:T(8,128)} %pad_maximum_fusion.11), channel_id=1, source_target_pairs={{0,1},{1,2},{2,3},{3,4},{4,5},{5,6},{6,7},{7,8},{8,9},{9,10},{10,1... | collective-permute-start | bytes 3145736 | tf_op jit(solution)/shard_map/ppermute | solution.py:21
  20.7 5.9 copy-start.7
  29.5 11.2 %collective-permute-start.2 = (f32[1,256,512]{2,1,0:T(8,128)S(1)}, f32[1,256,512]{2,1,0:T(8,128)S(1)}, u32[]{:S(2)}, u32[]{:S(2)}) collective-permute-start(f32[1,256,512]{2,1,0:T(8,128)S(1)} %get-tuple-element.13), channel_id=1, source_target_pairs={{1,0},{2,1},{3,2},{4,3},{5,4},{6,5},{7,6},{8,7},{9,8},{10,9},{11,1... | collective-permute-start | bytes 1572872 | tf_op jit(solution)/shard_map/ppermute | solution.py:24
  31.5 10.5 %collective-permute-start.3 = (f32[1,256,512]{2,1,0:T(8,128)S(1)}, f32[1,256,512]{2,1,0:T(8,128)S(1)}, u32[]{:S(2)}, u32[]{:S(2)}) collective-permute-start(f32[1,256,512]{2,1,0:T(8,128)S(1)} %get-tuple-element.13), channel_id=1, source_target_pairs={{0,1},{1,2},{2,3},{3,4},{4,5},{5,6},{6,7},{7,8},{8,9},{9,10},{10,1... | collective-permute-start | bytes 1572872 | tf_op jit(solution)/shard_map/ppermute | solution.py:21
  43.4 11.2 %collective-permute-start.4 = (f32[1,256,512]{2,1,0:T(8,128)S(1)}, f32[1,256,512]{2,1,0:T(8,128)S(1)}, u32[]{:S(2)}, u32[]{:S(2)}) collective-permute-start(f32[1,256,512]{2,1,0:T(8,128)S(1)} %multiply_subtract_fusion.1), channel_id=1, source_target_pairs={{1,0},{2,1},{3,2},{4,3},{5,4},{6,5},{7,6},{8,7},{9,8},{10,9},{11,1... | collective-permute-start | bytes 1572872 | tf_op jit(solution)/shard_map/ppermute | solution.py:24
  45.4 10.5 %collective-permute-start.5 = (f32[1,256,512]{2,1,0:T(8,128)S(1)}, f32[1,256,512]{2,1,0:T(8,128)S(1)}, u32[]{:S(2)}, u32[]{:S(2)}) collective-permute-start(f32[1,256,512]{2,1,0:T(8,128)S(1)} %multiply_subtract_fusion.1), channel_id=1, source_target_pairs={{0,1},{1,2},{2,3},{3,4},{4,5},{5,6},{6,7},{7,8},{8,9},{9,10},{10,1... | collective-permute-start | bytes 1572872 | tf_op jit(solution)/shard_map/ppermute | solution.py:21
  57.4 11.2 %collective-permute-start.6 = (f32[1,256,512]{2,1,0:T(8,128)S(1)}, f32[1,256,512]{2,1,0:T(8,128)S(1)}, u32[]{:S(2)}, u32[]{:S(2)}) collective-permute-start(f32[1,256,512]{2,1,0:T(8,128)S(1)} %multiply_subtract_fusion), channel_id=1, source_target_pairs={{1,0},{2,1},{3,2},{4,3},{5,4},{6,5},{7,6},{8,7},{9,8},{10,9},{11,1... | collective-permute-start | bytes 1572872 | tf_op jit(solution)/shard_map/ppermute | solution.py:24
  59.3 10.5 %collective-permute-start.7 = (f32[1,256,512]{2,1,0:T(8,128)S(1)}, f32[1,256,512]{2,1,0:T(8,128)S(1)}, u32[]{:S(2)}, u32[]{:S(2)}) collective-permute-start(f32[1,256,512]{2,1,0:T(8,128)S(1)} %multiply_subtract_fusion), channel_id=1, source_target_pairs={{0,1},{1,2},{2,3},{3,4},{4,5},{5,6},{6,7},{7,8},{8,9},{9,10},{10,1... | collective-permute-start | bytes 1572872 | tf_op jit(solution)/shard_map/ppermute | solution.py:21
  65.3 131.3 %copy-start.3 = (f32[1,1,256,512]{3,1,2,0:T(1,128)}, f32[1,1,256,512]{3,1,2,0:T(1,128)S(1)}, u32[]{:S(2)}) copy-start(f32[1,1,256,512]{3,1,2,0:T(1,128)S(1)} %copy.47) | copy-start | bytes 1572868
  71.8 127.8 %copy-start.4 = (f32[1,1,256,512]{3,1,2,0:T(1,128)}, f32[1,1,256,512]{3,1,2,0:T(1,128)S(1)}, u32[]{:S(2)}) copy-start(f32[1,1,256,512]{3,1,2,0:T(1,128)S(1)} %copy.48) | copy-start | bytes 1572868
  196.6 7.0 copy-start.10
  196.6 9.7 %copy-start.8 = (s32[7,8]{1,0:T(8,128)S(1)}, s32[7,8]{1,0:T(8,128)}, u32[]{:S(2)}) copy-start(s32[7,8]{1,0:T(8,128)} %param.15) | copy-start | bytes 676
  199.6 49.2 %collective-permute-start.8 = (f32[4,131072]{1,0:T(4,128)}, f32[4,131072]{1,0:T(4,128)}, u32[]{:S(2)}, u32[]{:S(2)}) collective-permute-start(f32[4,131072]{1,0:T(4,128)} %broadcast_divide_fusion), channel_id=1, source_target_pairs={{0,64},{64,0},{128,192},{192,128},{256,320},{320,256},{384,448},{4... | collective-permute-start | bytes 6291464 | tf_op jit(solution)/shard_map/ppermute | solution.py:36
  252.5 1.4 copy-start
  403.2 96.4 %collective-permute-start.9 = (f32[4,131072]{1,0:T(4,128)}, f32[4,131072]{1,0:T(4,128)}, u32[]{:S(2)}, u32[]{:S(2)}) collective-permute-start(f32[4,131072]{1,0:T(4,128)} %fusion.4), channel_id=1, source_target_pairs={{0,128},{128,0},{64,192},{192,64},{256,384},{384,256},{320,448},{4... | collective-permute-start | bytes 6291464 | tf_op jit(solution)/shard_map/ppermute | solution.py:36
  502.6 1.4 copy-start.2
  652.7 99.6 %collective-permute-start.10 = (f32[4,131072]{1,0:T(4,128)}, f32[4,131072]{1,0:T(4,128)}, u32[]{:S(2)}, u32[]{:S(2)}) collective-permute-start(f32[4,131072]{1,0:T(4,128)} %fusion.2), channel_id=1, source_target_pairs={{0,256},{256,0},{64,320},{320,64},{128,384},{384,128},{192,448},{4... | collective-permute-start | bytes 6291464 | tf_op jit(solution)/shard_map/ppermute | solution.py:36
  755.3 1.4 copy-start.1
where the time goes:
time: 915 us; the launch traced here: 906 us
  blocking collectives  497 us (54%)
  waiting for transfers between devices  241 us (26%)
  other arithmetic  53.3 us (6%)
  matrix products  52.4 us (6%)
  starting transfers between devices  48.2 us (5%)
  local copies, waits for them, and re-layouts  9.43 us (1%)
    psum x3, blocking collectives, local(): lax.psum(jnp.dot(stacked, stacked.T, precision=EXACT), 'space')  374 us
    ppermute x3, waiting for transfers between devices, swapped(): return lax.ppermute(block, axis, route)  220 us
    psum x1, blocking collectives, local(): squares = lax.psum(jnp.sum(leaf_rows * leaf_rows, axis=1), 'space')  122 us
    dot_general x3, matrix products, local(): jnp.dot(stacked, stacked.T, precision=EXACT)  27.9 us
    ppermute x3, starting transfers between devices, swapped(): return lax.ppermute(block, axis, route)  18.6 us
  transfers between devices with their start and end apart: 11, of which 10 were waited for; matrix products, arithmetic and copies ran while one was open for 1% of the time, Pallas kernels for 0%

commit v1 on v0

v1 whole, which is shorter than its diff:
```python
import math

import jax
import jax.numpy as jnp
from jax import lax
from jax.experimental import pallas as pl
from jax.experimental.pallas import tpu as pltpu
from jax.sharding import Mesh, PartitionSpec as P

STEPS = 4
SUBITERS = 3
EPS = 1e-06
RUNS = 8
NY = 256
NZ = 512
NX = 64
BLOCK = NY // RUNS
HALO = STEPS
EXT = BLOCK + 2 * HALO
CELLS = NX * NY * NZ
EXACT = lax.Precision.HIGHEST
SPACE = ("x", "y", "core")
VMEM = pl.BlockSpec(memory_space=pltpu.VMEM)
SMEM = pl.BlockSpec(memory_space=pltpu.SMEM)


def sub_iota(shape):
    return lax.broadcasted_iota(jnp.int32, shape, 0)


def lane_iota(shape):
    return lax.broadcasted_iota(jnp.int32, shape, 1)


def params(limit=40 << 20):
    return pltpu.CompilerParams(vmem_limit_bytes=limit)


def blocks_kernel(field_ref, visc_ref, out_ref, visc_out):
    run = lax.axis_index("run")
    low = sub_iota((8, NZ)) < 4
    zero = jnp.zeros((8, NZ), jnp.float32)
    tiles = NY // 8

    def shifted(before, after):
        return pltpu.roll(jnp.where(low, after, before), 4, 0)

    before = zero
    for m in range(tiles + 1):
        after = field_ref[0, 0, 8 * m : 8 * m + 8, :] if m < tiles else zero
        tile = shifted(before, after)
        before = after
        for q in range(RUNS):
            j = m - 4 * q
            if 0 <= j <= 4:
                out_ref[q, 8 * j : 8 * j + 8, :] = tile
    for j in range(5):
        m = 4 * run + j
        prev_at = pl.multiple_of(8 * jnp.maximum(m - 1, 0), 8)
        next_at = pl.multiple_of(8 * jnp.minimum(m, tiles - 1), 8)
        prev = jnp.where(m > 0, visc_ref[0, pl.ds(prev_at, 8), :], 0.0)
        nxt = jnp.where(m < tiles, visc_ref[0, pl.ds(next_at, 8), :], 0.0)
        visc_out[0, 8 * j : 8 * j + 8, :] = shifted(prev, nxt)


def row_blocks(field, visc):
    return pl.pallas_call(
        blocks_kernel,
        out_shape=(
            jax.ShapeDtypeStruct((RUNS, EXT, NZ), jnp.float32),
            jax.ShapeDtypeStruct((1, EXT, NZ), jnp.float32),
        ),
        in_specs=[VMEM, VMEM],
        out_specs=(VMEM, VMEM),
        compiler_params=params(),
        cost_estimate=pl.CostEstimate(flops=200000, bytes_accessed=2000000, transcendentals=0),
        name="row_blocks",
    )(field, visc)


def step_kernel(last, diff_ref, vel_ref, assign_ref, u_ref, sib_ref, cross_ref, v_ref, vs_ref, vc_ref, *outs):
    run = lax.axis_index("run")
    even = lax.axis_index("core") == 0
    shape = (EXT, NZ)
    row = sub_iota(shape) + (BLOCK * run - HALO)
    inside = (row >= 0) & (row < NY)
    col = lane_iota(shape)
    first_col = col == 0
    last_col = col == NZ - 1
    v = v_ref[0]
    vs = vs_ref[0]
    vc = vc_ref[0]

    def ahead_row(a):
        return pltpu.roll(a, EXT - 1, 0)

    def behind_row(a):
        return pltpu.roll(a, 1, 0)

    def ahead_col(a):
        return jnp.where(last_col, 0.0, pltpu.roll(a, NZ - 1, 1))

    def behind_col(a):
        return jnp.where(first_col, 0.0, pltpu.roll(a, 1, 1))

    c_sib = 0.5 * (v + vs)
    c_cross = 0.5 * (v + vc)
    c_yp = 0.5 * (v + ahead_row(v))
    c_ym = 0.5 * (v + behind_row(v))
    c_zp = 0.5 * (v + ahead_col(v))
    c_zm = 0.5 * (v + behind_col(v))
    for q in range(RUNS):
        s = assign_ref[q]
        kappa = diff_ref[s]
        ups = [-jnp.minimum(vel_ref[s, d], 0.0) for d in range(3)]
        downs = [jnp.maximum(vel_ref[s, d], 0.0) for d in range(3)]
        u = u_ref[q]
        w_sib = jnp.where(even, ups[0], downs[0])
        w_cross = jnp.where(even, downs[0], ups[0])
        new = u + (kappa * c_sib + w_sib) * (sib_ref[q] - u)
        new = new + (kappa * c_cross + w_cross) * (cross_ref[q] - u)
        new = new + (kappa * c_yp + ups[1]) * (ahead_row(u) - u)
        new = new + (kappa * c_ym + downs[1]) * (behind_row(u) - u)
        new = new + (kappa * c_zp + ups[2]) * (ahead_col(u) - u)
        new = new + (kappa * c_zm + downs[2]) * (behind_col(u) - u)
        new = jnp.where(inside, new, 0.0)
        if not last:
            outs[0][q] = new
        outs[-1][q] = pltpu.roll(new, EXT - HALO, 0)[:BLOCK]


def advance(last, coefs, state, sib, cross, visc, visc_sib, visc_cross):
    core = jax.ShapeDtypeStruct((RUNS, BLOCK, NZ), jnp.float32)
    full = jax.ShapeDtypeStruct((RUNS, EXT, NZ), jnp.float32)
    out = (core,) if last else (full, core)

    def body(*refs):
        step_kernel(last, *refs)

    return pl.pallas_call(
        body,
        out_shape=out,
        in_specs=[SMEM, SMEM, SMEM] + [VMEM] * 6,
        out_specs=tuple(VMEM for _ in out),
        compiler_params=params(),
        cost_estimate=pl.CostEstimate(flops=6000000, bytes_accessed=4000000, transcendentals=0),
        name="step_last" if last else "step",
    )(*coefs, state, sib, cross, visc, visc_sib, visc_cross)


def merge(x, y, width):
    sub = sub_iota((8, 128))
    pick = (sub & width) == 0
    keep = jnp.where(pick, x, y)
    give = jnp.where(pick, y, x)
    if width == 4:
        moved = pltpu.roll(give, 4, 0)
    else:
        moved = jnp.where(pick, pltpu.roll(give, 8 - width, 0), pltpu.roll(give, width, 0))
    return keep + moved


def gram_kernel(group, last, *refs):
    cores = refs[: group + 1]
    prev_ref = refs[group + 1] if group else None
    out_ref = refs[-1]
    mine = cores[group]
    lane = lane_iota((8, 128))
    packed = prev_ref[...] if group else jnp.zeros((8, 128), jnp.float32)
    for other in range(group + 1):
        theirs = cores[other]
        for half in range(2):
            accs = tuple(jnp.zeros((8, 128), jnp.float32) for _ in range(32))

            def body(i, accs, theirs=theirs, half=half):
                rows = pl.ds(pl.multiple_of(8 * i, 8), 8)
                accs = list(accs)
                for l in range(NZ // 128):
                    cols = slice(128 * l, 128 * l + 128)
                    a = [mine[4 * half + k, rows, cols] for k in range(4)]
                    for b in range(8):
                        t = theirs[b, rows, cols]
                        for k in range(4):
                            accs[8 * k + b] = accs[8 * k + b] + a[k] * t
                return tuple(accs)

            accs = lax.fori_loop(0, BLOCK // 8, body, accs)
            for k in range(4):
                level = list(accs[8 * k : 8 * k + 8])
                for width in (4, 2, 1):
                    count = len(level) // 2
                    level = [merge(level[i], level[i + count], width) for i in range(count)]
                total = jnp.sum(level[0], axis=1, keepdims=True)
                at = 32 * other + 8 * group + 4 * half + k
                packed = jnp.where(lane == at, total, packed)
    if last:
        for i in range(RUNS):
            out_ref[i] = packed
    else:
        out_ref[...] = packed


def gram(cores, prev, last):
    group = len(cores) - 1
    shape = (RUNS, 8, 128) if last else (8, 128)
    args = list(cores) + ([prev] if group else [])

    def body(*refs):
        gram_kernel(group, last, *refs)

    return pl.pallas_call(
        body,
        out_shape=jax.ShapeDtypeStruct(shape, jnp.float32),
        in_specs=[VMEM] * len(args),
        out_specs=VMEM,
        compiler_params=params(),
        cost_estimate=pl.CostEstimate(flops=2200000 * (group + 1), bytes_accessed=600000 * (group + 1), transcendentals=0),
        name=f"gram{group}",
    )(*args)


def spread_kernel(in_ref, out_ref):
    total = in_ref[0]
    for i in range(1, RUNS):
        total = total + in_ref[i]
    for i in range(RUNS):
        out_ref[i] = total


def spread(parts):
    return pl.pallas_call(
        spread_kernel,
        out_shape=jax.ShapeDtypeStruct(parts.shape, jnp.float32),
        in_specs=[VMEM],
        out_specs=VMEM,
        name="spread",
    )(parts)


def dot(a, b):
    return jnp.dot(a, b, precision=EXACT, preferred_element_type=jnp.float32)


def dct():
    size = 2 * STEPS
    return [
        [math.sqrt(1.0 / STEPS) * math.cos(math.pi * (i + 0.5) * (j + 0.5) / size) for j in range(STEPS)]
        for i in range(size)
    ]


def sublane_sum(a):
    for width in (4, 2, 1):
        a = a + pltpu.roll(a, width, 0)
    return a


def level_basis(gram_now, nodes, first_node, order_ref, keep_ref):
    shape = (8, 128)
    sub = sub_iota(shape)
    lane = lane_iota(shape) & (nodes - 1)
    table = dct()
    basis = [jnp.zeros(shape, jnp.float32) for _ in range(STEPS)]
    live = [jnp.zeros(shape, jnp.float32) for _ in range(STEPS)]
    for k in range(nodes):
        node = first_node + k
        here = lane == k
        for c in range(STEPS):
            flag = jnp.where(keep_ref[node] > c, 1.0, 0.0)
            live[c] = jnp.where(here, flag, live[c])
        for i in range(2 * STEPS):
            spot = here & (sub == order_ref[node, i])
            for c in range(STEPS):
                basis[c] = jnp.where(spot, table[i][c], basis[c])
    basis = [z * m for z, m in zip(basis, live)]
    cols = []
    for j in range(8):
        col = jnp.zeros(shape, jnp.float32)
        for k in range(nodes):
            piece = gram_now[8 * k : 8 * k + 8, 8 * k + j : 8 * k + j + 1]
            col = jnp.where(lane == k, piece, col)
        cols.append(col)
    for _ in range(SUBITERS):
        image = []
        for c in range(STEPS):
            total = cols[0] * basis[c][0:1, :]
            for j in range(1, 8):
                total = total + cols[j] * basis[c][j : j + 1, :]
            image.append(total * live[c])
        inner = {}
        for a in range(STEPS):
            for b in range(a + 1):
                inner[a, b] = sublane_sum(image[a] * image[b])
            inner[a, a] = inner[a, a] + (1.0 - live[a])
        low = {}
        inv = []
        for b in range(STEPS):
            pivot = inner[b, b]
            for k in range(b):
                pivot = pivot - low[b, k] * low[b, k]
            root = 1.0 / jnp.sqrt(pivot)
            inv.append(root)
            for a in range(b + 1, STEPS):
                entry = inner[a, b]
                for k in range(b):
                    entry = entry - low[a, k] * low[b, k]
                low[a, b] = entry * root
        fresh = []
        for a in range(STEPS):
            value = image[a]
            for k in range(a):
                value = value - low[a, k] * fresh[k]
            fresh.append(value * inv[a])
        basis = fresh
    return basis


def weights(basis, nodes):
    lane = lane_iota((8, 128))
    rows = []
    for k in range(nodes):
        block = jnp.zeros((8, 128), jnp.float32)
        for c in range(STEPS):
            block = jnp.where(lane == STEPS * k + c, basis[c][:, k : k + 1], block)
        rows.append(block)
    return jnp.concatenate(rows, axis=0) if nodes > 1 else rows[0]


def finish_kernel(order_ref, keep_ref, part_ref, c0, c1, c2, c3, out_ref, w_ref):
    packed = part_ref[0]
    for i in range(1, RUNS):
        packed = packed + part_ref[i]
    size = RUNS * STEPS
    raw = jnp.concatenate(
        [packed if j == 0 else pltpu.roll(packed, 128 - size * j, 1) for j in range(STEPS)], axis=0
    )
    sub = sub_iota((size, 128))
    lane = lane_iota((size, 128))
    raw = jnp.where(lane < size, raw, 0.0)
    square = jnp.concatenate([raw, jnp.zeros((128 - size, 128), jnp.float32)], axis=0)
    mirror = square.T[:size, :]
    raw = jnp.where((sub >> 3) <= (lane >> 3), raw, mirror)
    source = 8 * (sub & 3) + (sub >> 2)
    perm = jnp.where(lane == source, 1.0, 0.0)
    rows = dot(perm[:, :size], raw)
    target = 8 * (lane & 3) + (lane >> 2)
    perm_t = jnp.where((sub == target) & (lane < size), 1.0, 0.0)
    full = dot(rows[:, :size], perm_t)
    diag = jnp.where(sub == lane, full, 0.0)
    mu_col = jnp.sum(diag, axis=1, keepdims=True) / CELLS
    mu_row = jnp.sum(diag, axis=0, keepdims=True) / CELLS
    scale_col = 1.0 / jnp.sqrt(mu_col + EPS)
    scale_row = 1.0 / jnp.sqrt(mu_row + EPS)
    gram_now = full * scale_col * scale_row / CELLS
    nodes = RUNS // 2
    first_node = 0
    total = None
    while nodes:
        basis = level_basis(gram_now, nodes, first_node, order_ref, keep_ref)
        w = weights(basis, nodes)
        rows_now = 8 * nodes
        total = w if total is None else dot(total[:, :rows_now], w)
        if nodes > 1:
            half = dot(gram_now[:, :rows_now], w)
            w_t = jnp.concatenate([w, jnp.zeros((128 - rows_now, 128), jnp.float32)], axis=0).T
            gram_now = dot(w_t[: STEPS * nodes, :rows_now], half)
        first_node += nodes
        nodes //= 2
    total = total * scale_col
    for c in range(STEPS):
        w_ref[c] = jnp.broadcast_to(total[:, c : c + 1], (size, 128))
    cores = (c0, c1, c2, c3)
    for l in range(NZ // 128):
        cols = slice(128 * l, 128 * l + 128)
        for i in range(BLOCK // 8):
            rws = slice(8 * i, 8 * i + 8)
            accs = [None] * STEPS
            for q in range(RUNS):
                for t in range(STEPS):
                    x = cores[t][q, rws, cols]
                    k = STEPS * q + t
                    for c in range(STEPS):
                        term = w_ref[c, k : k + 1, :] * x
                        accs[c] = term if accs[c] is None else accs[c] + term
            for c in range(STEPS):
                out_ref[c, 0, rws, cols] = accs[c]


def finish(order, keep, parts, cores):
    return pl.pallas_call(
        finish_kernel,
        out_shape=jax.ShapeDtypeStruct((STEPS, 1, BLOCK, NZ), jnp.float32),
        in_specs=[SMEM, SMEM] + [VMEM] * 5,
        out_specs=VMEM,
        scratch_shapes=[pltpu.VMEM((STEPS, RUNS * STEPS, 128), jnp.float32)],
        compiler_params=params(),
        cost_estimate=pl.CostEstimate(flops=5000000, bytes_accessed=2400000, transcendentals=0),
        name="finish",
    )(order, keep, parts, *cores)


def local(start_field, viscosity, diffusivity, velocity, assignment, child_order, keep_ranks):
    coefs = (diffusivity, velocity, assignment)
    sibling = [(i, i ^ 1) for i in range(NX)]
    crossing = [(i, i + 1) for i in range(1, NX - 1, 2)] + [(i + 1, i) for i in range(1, NX - 1, 2)]
    blocks, visc = row_blocks(start_field, viscosity)
    state = lax.all_to_all(blocks, "run", 0, 0)
    send = jnp.concatenate([state, visc], axis=0)
    cores = []
    packed = None
    for step in range(STEPS):
        cross = lax.ppermute(send, SPACE, crossing)
        sib = lax.ppermute(send, SPACE, sibling)
        if cores:
            packed = gram(cores, packed, False)
        if step == 0:
            visc_sib, visc_cross = sib[RUNS:], cross[RUNS:]
        last = step == STEPS - 1
        result = advance(last, coefs, state, sib, cross, visc, visc_sib, visc_cross)
        cores.append(result[-1])
        state = send = result[0]
    parts = gram(cores, packed, True)
    parts = spread(lax.all_to_all(parts, ("x", "core"), 0, 0))
    parts = spread(lax.all_to_all(parts, "y", 0, 0))
    parts = lax.all_to_all(parts, "run", 0, 0)
    return finish(child_order, keep_ranks, parts, cores)


def solution(mesh):
    fine = Mesh(mesh.devices.reshape(8, 4, 8, 2), ("run", "x", "y", "core"))
    in_specs = (P("run", SPACE, None, None), P(SPACE, None, None), P(), P(), P(), P(), P())
    out_specs = P(None, SPACE, "run", None)
    return jax.shard_map(local, mesh=fine, in_specs=in_specs, out_specs=out_specs, check_vma=False)
```

time: 915 us -> 149 us (0.16)
  blocking collectives: 497 us -> 67.9 us
  waiting for transfers between devices: 241 us -> 31.4 us
  other arithmetic: 53.3 us -> 0 us
  matrix products: 52.4 us -> 0 us
  starting transfers between devices: 48.2 us -> 24.8 us
  Pallas kernels: 0 us -> 19.5 us
    psum x4 -> x0, blocking collectives: 497 us -> none  [the longest x3 374 us: local(): lax.psum(jnp.dot(stacked, stacked.T, precision=EXACT), 'space')]
    ppermute x11 -> x8, waiting for transfers between devices: 241 us -> 31.4 us  [the longest x4 31.4 us: local(): cross = lax.ppermute(send, SPACE, crossing)]
    all_to_all x0 -> x4, blocking collectives: none -> 67.9 us  [the longest x1 29.8 us: local(): state = lax.all_to_all(blocks, 'run', 0, 0)]
    dot_general x33 -> x0, matrix products: 50.6 us -> none  [the longest x3 27.9 us: local(): jnp.dot(stacked, stacked.T, precision=EXACT)]
    ppermute x11 -> x8, starting transfers between devices: 48.2 us -> 24.8 us  [the longest x4 15 us: local(): cross = lax.ppermute(send, SPACE, crossing)]
    another operation x46 -> x0, other arithmetic: 20.6 us -> none  [the longest x27 9.49 us: leading(): factor_low = jnp.linalg.cholesky(inner_gram)]
    pallas_call x0 -> x12, Pallas kernels: none -> 19.5 us  [the longest x4 7.02 us: advance(): pl.pallas_call(body, out_shape=out, in_specs=[SMEM, SMEM, SMEM] + [VMEM]...]
    select_n x3 -> x0, other arithmetic: 9.6 us -> none  [local(): lower_side = jnp.where(upper_bit == 1, partner, factor_rows)]
  transfers between devices with their start and end apart: 11 -> 8, of which waited for: 10 -> 4; matrix products, arithmetic and copies ran while one was open for 1% -> 0% of each run, Pallas kernels for 0% -> 2%
where the time goes in v1:
time: 149 us; the launch traced here: 147 us
  blocking collectives  67.9 us (46%)
  waiting for transfers between devices  31.4 us (21%)
  starting transfers between devices  24.8 us (17%)
  Pallas kernels  19.5 us (13%)
  local copies, waits for them, and re-layouts  3.74 us (3%)
    ppermute x4, waiting for transfers between devices, local(): cross = lax.ppermute(send, SPACE, crossing)  31.4 us
    all_to_all x1, blocking collectives, local(): state = lax.all_to_all(blocks, 'run', 0, 0)  29.8 us
    all_to_all x1, blocking collectives, local(): parts = spread(lax.all_to_all(parts, ('x', 'core'), 0, 0))  16.3 us
    ppermute x4, starting transfers between devices, local(): cross = lax.ppermute(send, SPACE, crossing)  15 us
    all_to_all x1, blocking collectives, local(): parts = spread(lax.all_to_all(parts, 'y', 0, 0))  11.5 us
    all_to_all x1, blocking collectives, local(): parts = lax.all_to_all(parts, 'run', 0, 0)  10.2 us
    ppermute x4, starting transfers between devices, local(): sib = lax.ppermute(send, SPACE, sibling)  9.76 us
    pallas_call x4, Pallas kernels, advance(): pl.pallas_call(body, out_shape=out, in_specs=[SMEM, SMEM, SMEM] + [VMEM]...  7.02 us
  transfers between devices with their start and end apart: 8, of which 4 were waited for; matrix products, arithmetic and copies ran while one was open for 0% of the time, Pallas kernels for 2%

profile of v1, /device:TPU:1, one launch (start us, length us, event | category | flops | bytes accessed | tf_op | source)
XLA Modules:
  0.0 147.5 jit_solution(5415514925851128967)
XLA Ops:
  2.2 29.8 %all_to_all.20.refs_3_ = f32[8,40,512]{2,1,0:T(8,128)S(1)} all-to-all(f32[8,40,512]{2,1,0:T(8,128)S(1)} %get-tuple-element.13), channel_id=1, replica_groups=mesh['run'=8,'x'=4,'y'=8,'core'=2] {'run'}, dimensions={0} | all-to-all | bytes 1310720 | tf_op jit(solution)/shard_map/all_to_all | solution.py:407
  33.5 4.0 %collective-permute-start = (f32[9,40,512]{2,1,0:T(8,128)}, f32[9,40,512]{2,1,0:T(8,128)S(1)}, u32[]{:S(2)}, u32[]{:S(2)}) collective-permute-start(f32[9,40,512]{2,1,0:T(8,128)} %constant_dynamic-update-slice_fusion), channel_id=1, source_target_pairs={{0,1},{1,0},{2,3},{3,2},{4,5},{5,4},{6,7},{7,6},{8,9},{9,8},{10,11... | collective-permute-start | bytes 2211848 | tf_op jit(solution)/shard_map/ppermute | solution.py:413
  37.5 3.1 %collective-permute-start.1 = (f32[9,40,512]{2,1,0:T(8,128)}, f32[9,40,512]{2,1,0:T(8,128)S(1)}, u32[]{:S(2)}, u32[]{:S(2)}) collective-permute-start(f32[9,40,512]{2,1,0:T(8,128)} %constant_dynamic-update-slice_fusion), channel_id=1, source_target_pairs={{1,2},{3,4},{5,6},{7,8},{9,10},{11,12},{13,14},{15,16},{17,18},{19... | collective-permute-start | bytes 2211848 | tf_op jit(solution)/shard_map/ppermute | solution.py:412
  40.8 9.8 %collective-permute-done.1.refs_5_ = f32[9,40,512]{2,1,0:T(8,128)S(1)} collective-permute-done((f32[9,40,512]{2,1,0:T(8,128)}, f32[9,40,512]{2,1,0:T(8,128)S(1)}, u32[]{:S(2)}, u32[]{:S(2)}) %collective-permute-start.1) | collective-permute-done | bytes 737312 | tf_op jit(solution)/shard_map/ppermute | solution.py:412
  50.5 1.8 %step.3 = (f32[8,40,512]{2,1,0:T(8,128)S(1)}, f32[8,32,512]{2,1,0:T(8,128)S(1)}) custom-call(f32[8]{0:T(128)S(1)} %copy-done.2, f32[8,3]{1,0:T(8,128)S(1)} %copy.8.refs_1_, s32[8]{0:T(128)S(1)} %copy-done.3, f32[8,40,512]{2,1,0:T(8,128)S(1)} %all_to_all.20.refs_3_, f32[9,40,512]{2,1,0:T(8,128)S(1)} %collective-permute-done.refs_4_, ...), custom_call_target="tpu_custom_call" | custom-call | flops 6000000 | bytes 4000000 | tf_op jit(solution)/shard_map/step/pallas_call | solution.py:140
  52.3 1.9 %collective-permute-start.2 = (f32[8,40,512]{2,1,0:T(8,128)S(1)}, f32[8,40,512]{2,1,0:T(8,128)S(1)}, u32[]{:S(2)}, u32[]{:S(2)}) collective-permute-start(f32[8,40,512]{2,1,0:T(8,128)S(1)} %get-tuple-element.16.refs_3_), channel_id=1, source_target_pairs={{0,1},{1,0},{2,3},{3,2},{4,5},{5,4},{6,7},{7,6},{8,9},{9,8},{10,11... | collective-permute-start | bytes 1966088 | tf_op jit(solution)/shard_map/ppermute | solution.py:413
  54.2 3.6 %collective-permute-start.3 = (f32[8,40,512]{2,1,0:T(8,128)S(1)}, f32[8,40,512]{2,1,0:T(8,128)S(1)}, u32[]{:S(2)}, u32[]{:S(2)}) collective-permute-start(f32[8,40,512]{2,1,0:T(8,128)S(1)} %get-tuple-element.16.refs_3_), channel_id=1, source_target_pairs={{1,2},{3,4},{5,6},{7,8},{9,10},{11,12},{13,14},{15,16},{17,18},{19... | collective-permute-start | bytes 1966088 | tf_op jit(solution)/shard_map/ppermute | solution.py:412
  57.8 8.3 %collective-permute-done.3.refs_5_ = f32[8,40,512]{2,1,0:T(8,128)S(1)} collective-permute-done((f32[8,40,512]{2,1,0:T(8,128)S(1)}, f32[8,40,512]{2,1,0:T(8,128)S(1)}, u32[]{:S(2)}, u32[]{:S(2)}) %collective-permute-start.3) | collective-permute-done | bytes 655392 | tf_op jit(solution)/shard_map/ppermute | solution.py:412
  66.1 1.8 %step.4 = (f32[8,40,512]{2,1,0:T(8,128)S(1)}, f32[8,32,512]{2,1,0:T(8,128)S(1)}) custom-call(f32[8]{0:T(128)S(1)} %copy-done.2, f32[8,3]{1,0:T(8,128)S(1)} %copy.8.refs_1_, s32[8]{0:T(128)S(1)} %copy-done.3, f32[8,40,512]{2,1,0:T(8,128)S(1)} %get-tuple-element.16.refs_3_, f32[8,40,512]{2,1,0:T(8,128)S(1)} %collective-permute-done.2.refs_4_, ...), custom_call_target="tpu_custom_call" | custom-call | flops 6000000 | bytes 4000000 | tf_op jit(solution)/shard_map/step/pallas_call | solution.py:140
  67.9 1.9 %collective-permute-start.4 = (f32[8,40,512]{2,1,0:T(8,128)S(1)}, f32[8,40,512]{2,1,0:T(8,128)S(1)}, u32[]{:S(2)}, u32[]{:S(2)}) collective-permute-start(f32[8,40,512]{2,1,0:T(8,128)S(1)} %get-tuple-element.18.refs_3_), channel_id=1, source_target_pairs={{0,1},{1,0},{2,3},{3,2},{4,5},{5,4},{6,7},{7,6},{8,9},{9,8},{10,11... | collective-permute-start | bytes 1966088 | tf_op jit(solution)/shard_map/ppermute | solution.py:413
  69.8 3.7 %collective-permute-start.5 = (f32[8,40,512]{2,1,0:T(8,128)S(1)}, f32[8,40,512]{2,1,0:T(8,128)S(1)}, u32[]{:S(2)}, u32[]{:S(2)}) collective-permute-start(f32[8,40,512]{2,1,0:T(8,128)S(1)} %get-tuple-element.18.refs_3_), channel_id=1, source_target_pairs={{1,2},{3,4},{5,6},{7,8},{9,10},{11,12},{13,14},{15,16},{17,18},{19... | collective-permute-start | bytes 1966088 | tf_op jit(solution)/shard_map/ppermute | solution.py:412
  73.5 8.2 %collective-permute-done.5.refs_5_ = f32[8,40,512]{2,1,0:T(8,128)S(1)} collective-permute-done((f32[8,40,512]{2,1,0:T(8,128)S(1)}, f32[8,40,512]{2,1,0:T(8,128)S(1)}, u32[]{:S(2)}, u32[]{:S(2)}) %collective-permute-start.5) | collective-permute-done | bytes 655392 | tf_op jit(solution)/shard_map/ppermute | solution.py:412
  81.8 1.8 %step.5 = (f32[8,40,512]{2,1,0:T(8,128)S(1)}, f32[8,32,512]{2,1,0:T(8,128)S(1)}) custom-call(f32[8]{0:T(128)S(1)} %copy-done.2, f32[8,3]{1,0:T(8,128)S(1)} %copy.8.refs_1_, s32[8]{0:T(128)S(1)} %copy-done.3, f32[8,40,512]{2,1,0:T(8,128)S(1)} %get-tuple-element.18.refs_3_, f32[8,40,512]{2,1,0:T(8,128)S(1)} %collective-permute-done.4.refs_4_, ...), custom_call_target="tpu_custom_call" | custom-call | flops 6000000 | bytes 4000000 | tf_op jit(solution)/shard_map/step/pallas_call | solution.py:140
  83.5 1.9 %collective-permute-start.6 = (f32[8,40,512]{2,1,0:T(8,128)S(1)}, f32[8,40,512]{2,1,0:T(8,128)S(1)}, u32[]{:S(2)}, u32[]{:S(2)}) collective-permute-start(f32[8,40,512]{2,1,0:T(8,128)S(1)} %get-tuple-element.20.refs_3_), channel_id=1, source_target_pairs={{0,1},{1,0},{2,3},{3,2},{4,5},{5,4},{6,7},{7,6},{8,9},{9,8},{10,11... | collective-permute-start | bytes 1966088 | tf_op jit(solution)/shard_map/ppermute | solution.py:413
  85.5 4.6 %collective-permute-start.7 = (f32[8,40,512]{2,1,0:T(8,128)S(1)}, f32[8,40,512]{2,1,0:T(8,128)S(1)}, u32[]{:S(2)}, u32[]{:S(2)}) collective-permute-start(f32[8,40,512]{2,1,0:T(8,128)S(1)} %get-tuple-element.20.refs_3_), channel_id=1, source_target_pairs={{1,2},{3,4},{5,6},{7,8},{9,10},{11,12},{13,14},{15,16},{17,18},{19... | collective-permute-start | bytes 1966088 | tf_op jit(solution)/shard_map/ppermute | solution.py:412
  91.7 1.6 %gram2.1.refs_4_ = f32[8,128]{1,0:T(8,128)S(1)} custom-call(f32[8,32,512]{2,1,0:T(8,128)S(1)} %get-tuple-element.15.refs_0_.c0, f32[8,32,512]{2,1,0:T(8,128)S(1)} %get-tuple-element.17.refs_1_.c1, f32[8,32,512]{2,1,0:T(8,128)S(1)} %get-tuple-element.19.refs_2_.c2, f32[8,128]{1,0:T(8,128)S(1)} %gram1.1.refs_3_), custom_call_target="tpu_custom_call" | custom-call | flops 6600000 | bytes 1800000 | tf_op jit(solution)/shard_map/gram2/pallas_call | solution.py:211
  93.3 5.1 %collective-permute-done.7.refs_5_ = f32[8,40,512]{2,1,0:T(8,128)S(1)} collective-permute-done((f32[8,40,512]{2,1,0:T(8,128)S(1)}, f32[8,40,512]{2,1,0:T(8,128)S(1)}, u32[]{:S(2)}, u32[]{:S(2)}) %collective-permute-start.7) | collective-permute-done | bytes 655392 | tf_op jit(solution)/shard_map/ppermute | solution.py:412
  98.4 1.8 %step_last.1.refs_3_.c3 = f32[8,32,512]{2,1,0:T(8,128)S(1)} custom-call(f32[8]{0:T(128)S(1)} %copy-done.2, f32[8,3]{1,0:T(8,128)S(1)} %copy.8.refs_1_, s32[8]{0:T(128)S(1)} %copy-done.3, f32[8,40,512]{2,1,0:T(8,128)S(1)} %get-tuple-element.20.refs_3_, f32[8,40,512]{2,1,0:T(8,128)S(1)} %collective-permute-done.6.refs_4_, ...), custom_call_target="tpu_custom_call" | custom-call | flops 6000000 | bytes 4000000 | tf_op jit(solution)/shard_map/step_last/pallas_call | solution.py:140
  100.1 2.2 %gram3.1 = f32[8,8,128]{2,1,0:T(8,128)S(1)} custom-call(f32[8,32,512]{2,1,0:T(8,128)S(1)} %get-tuple-element.15.refs_0_.c0, f32[8,32,512]{2,1,0:T(8,128)S(1)} %get-tuple-element.17.refs_1_.c1, f32[8,32,512]{2,1,0:T(8,128)S(1)} %get-tuple-element.19.refs_2_.c2, f32[8,32,512]{2,1,0:T(8,128)S(1)} %step_last.1.refs_3_.c3, f32[8,128]{1,0:T(8,128)S(1)} %gram2.1.refs_4_), custom_call_target="tpu_custom_call" | custom-call | flops 8800000 | bytes 2400000 | tf_op jit(solution)/shard_map/gram3/pallas_call | solution.py:211
  102.3 16.3 %all_to_all.21.in_ref = f32[8,8,128]{2,1,0:T(8,128)} all-to-all(f32[8,8,128]{2,1,0:T(8,128)S(1)} %gram3.1), channel_id=1, replica_groups=mesh['run'=8,'x'=4,'y'=8,'core'=2] {'x','core'}, dimensions={0} | all-to-all | bytes 65536 | tf_op jit(solution)/shard_map/all_to_all | solution.py:423
  118.6 1.4 spread.2
  120.0 11.5 %all_to_all.22.in_ref = f32[8,8,128]{2,1,0:T(8,128)} all-to-all(f32[8,8,128]{2,1,0:T(8,128)} %spread.2), channel_id=1, replica_groups=mesh['run'=8,'x'=4,'y'=8,'core'=2] {'y'}, dimensions={0} | all-to-all | bytes 65536 | tf_op jit(solution)/shard_map/all_to_all | solution.py:424
  133.0 10.2 %all_to_all.23.part_ref = f32[8,8,128]{2,1,0:T(8,128)S(1)} all-to-all(f32[8,8,128]{2,1,0:T(8,128)} %spread.3), channel_id=1, replica_groups=mesh['run'=8,'x'=4,'y'=8,'core'=2] {'run'}, dimensions={0} | all-to-all | bytes 65536 | tf_op jit(solution)/shard_map/all_to_all | solution.py:425
  143.2 4.3 %finish.1 = f32[4,1,32,512]{3,2,1,0:T(8,128)} custom-call(s32[7,8]{1,0:T(8,128)S(1)} %copy-done.4, s32[7]{0:T(128)S(1)} %copy-done.5, f32[8,8,128]{2,1,0:T(8,128)S(1)} %all_to_all.23.part_ref, f32[8,32,512]{2,1,0:T(8,128)S(1)} %get-tuple-element.15.refs_0_.c0, f32[8,32,512]{2,1,0:T(8,128)S(1)} %get-tuple-element.17.refs_1_.c1, ...), custom_call_target="tpu_custom_call" | custom-call | flops 5000000 | bytes 2400000 | tf_op jit(solution)/shard_map/finish/pallas_call | solution.py:390
  (27 shorter events, 6.8 us)
Async XLA Ops:
  0.0 1.0 copy-start
  1.0 1.0 copy-start.1
  32.9 7.8 %copy-start.6 = (f32[8,3]{0,1:T(4,128)S(1)}, f32[8,3]{0,1:T(4,128)}, u32[]{:S(2)}) copy-start(f32[8,3]{0,1:T(4,128)} %param.10) | copy-start | bytes 292
  33.5 7.2 %collective-permute-start = (f32[9,40,512]{2,1,0:T(8,128)}, f32[9,40,512]{2,1,0:T(8,128)S(1)}, u32[]{:S(2)}, u32[]{:S(2)}) collective-permute-start(f32[9,40,512]{2,1,0:T(8,128)} %constant_dynamic-update-slice_fusion), channel_id=1, source_target_pairs={{0,1},{1,0},{2,3},{3,2},{4,5},{5,4},{6,7},{7,6},{8,9},{9,8},{10,11... | collective-permute-start | bytes 2211848 | tf_op jit(solution)/shard_map/ppermute | solution.py:413
  37.5 13.0 %collective-permute-start.1 = (f32[9,40,512]{2,1,0:T(8,128)}, f32[9,40,512]{2,1,0:T(8,128)S(1)}, u32[]{:S(2)}, u32[]{:S(2)}) collective-permute-start(f32[9,40,512]{2,1,0:T(8,128)} %constant_dynamic-update-slice_fusion), channel_id=1, source_target_pairs={{1,2},{3,4},{5,6},{7,8},{9,10},{11,12},{13,14},{15,16},{17,18},{19... | collective-permute-start | bytes 2211848 | tf_op jit(solution)/shard_map/ppermute | solution.py:412
  40.7 9.8 %copy-start.2 = (f32[8]{0:T(128)S(1)}, f32[8]{0:T(128)}, u32[]{:S(2)}) copy-start(f32[8]{0:T(128)} %refs_0_.7) | copy-start | bytes 100
  40.7 9.8 %copy-start.3 = (s32[8]{0:T(128)S(1)}, s32[8]{0:T(128)}, u32[]{:S(2)}) copy-start(s32[8]{0:T(128)} %refs_2_.7) | copy-start | bytes 100
  52.3 5.5 %collective-permute-start.2 = (f32[8,40,512]{2,1,0:T(8,128)S(1)}, f32[8,40,512]{2,1,0:T(8,128)S(1)}, u32[]{:S(2)}, u32[]{:S(2)}) collective-permute-start(f32[8,40,512]{2,1,0:T(8,128)S(1)} %get-tuple-element.16.refs_3_), channel_id=1, source_target_pairs={{0,1},{1,0},{2,3},{3,2},{4,5},{5,4},{6,7},{7,6},{8,9},{9,8},{10,11... | collective-permute-start | bytes 1966088 | tf_op jit(solution)/shard_map/ppermute | solution.py:413
  54.2 11.9 %collective-permute-start.3 = (f32[8,40,512]{2,1,0:T(8,128)S(1)}, f32[8,40,512]{2,1,0:T(8,128)S(1)}, u32[]{:S(2)}, u32[]{:S(2)}) collective-permute-start(f32[8,40,512]{2,1,0:T(8,128)S(1)} %get-tuple-element.16.refs_3_), channel_id=1, source_target_pairs={{1,2},{3,4},{5,6},{7,8},{9,10},{11,12},{13,14},{15,16},{17,18},{19... | collective-permute-start | bytes 1966088 | tf_op jit(solution)/shard_map/ppermute | solution.py:412
  67.9 5.6 %collective-permute-start.4 = (f32[8,40,512]{2,1,0:T(8,128)S(1)}, f32[8,40,512]{2,1,0:T(8,128)S(1)}, u32[]{:S(2)}, u32[]{:S(2)}) collective-permute-start(f32[8,40,512]{2,1,0:T(8,128)S(1)} %get-tuple-element.18.refs_3_), channel_id=1, source_target_pairs={{0,1},{1,0},{2,3},{3,2},{4,5},{5,4},{6,7},{7,6},{8,9},{9,8},{10,11... | collective-permute-start | bytes 1966088 | tf_op jit(solution)/shard_map/ppermute | solution.py:413
  69.8 12.0 %collective-permute-start.5 = (f32[8,40,512]{2,1,0:T(8,128)S(1)}, f32[8,40,512]{2,1,0:T(8,128)S(1)}, u32[]{:S(2)}, u32[]{:S(2)}) collective-permute-start(f32[8,40,512]{2,1,0:T(8,128)S(1)} %get-tuple-element.18.refs_3_), channel_id=1, source_target_pairs={{1,2},{3,4},{5,6},{7,8},{9,10},{11,12},{13,14},{15,16},{17,18},{19... | collective-permute-start | bytes 1966088 | tf_op jit(solution)/shard_map/ppermute | solution.py:412
  83.5 9.8 %collective-permute-start.6 = (f32[8,40,512]{2,1,0:T(8,128)S(1)}, f32[8,40,512]{2,1,0:T(8,128)S(1)}, u32[]{:S(2)}, u32[]{:S(2)}) collective-permute-start(f32[8,40,512]{2,1,0:T(8,128)S(1)} %get-tuple-element.20.refs_3_), channel_id=1, source_target_pairs={{0,1},{1,0},{2,3},{3,2},{4,5},{5,4},{6,7},{7,6},{8,9},{9,8},{10,11... | collective-permute-start | bytes 1966088 | tf_op jit(solution)/shard_map/ppermute | solution.py:413
  85.5 12.9 %collective-permute-start.7 = (f32[8,40,512]{2,1,0:T(8,128)S(1)}, f32[8,40,512]{2,1,0:T(8,128)S(1)}, u32[]{:S(2)}, u32[]{:S(2)}) collective-permute-start(f32[8,40,512]{2,1,0:T(8,128)S(1)} %get-tuple-element.20.refs_3_), channel_id=1, source_target_pairs={{1,2},{3,4},{5,6},{7,8},{9,10},{11,12},{13,14},{15,16},{17,18},{19... | collective-permute-start | bytes 1966088 | tf_op jit(solution)/shard_map/ppermute | solution.py:412
  132.9 10.3 %copy-start.4 = (s32[7,8]{1,0:T(8,128)S(1)}, s32[7,8]{1,0:T(8,128)}, u32[]{:S(2)}) copy-start(s32[7,8]{1,0:T(8,128)} %order_ref.1) | copy-start | bytes 676
  132.9 10.3 %copy-start.5 = (s32[7]{0:T(128)S(1)}, s32[7]{0:T(128)}, u32[]{:S(2)}) copy-start(s32[7]{0:T(128)} %keep_ref.1) | copy-start | bytes 88

commit v2 on v1

--- a/solution.py
+++ b/solution.py
@@ -20,6 +20,9 @@
 CELLS = NX * NY * NZ
 EXACT = lax.Precision.HIGHEST
 SPACE = ("x", "y", "core")
+GROUPS = ((0, 4), (4, 8))
+FIRST = 16
+SECOND = 32
 VMEM = pl.BlockSpec(memory_space=pltpu.VMEM)
 SMEM = pl.BlockSpec(memory_space=pltpu.SMEM)
 
@@ -78,7 +81,28 @@
     )(field, visc)
 
 
-def step_kernel(last, diff_ref, vel_ref, assign_ref, u_ref, sib_ref, cross_ref, v_ref, vs_ref, vc_ref, *outs):
+def assemble_kernel(state_ref, visc_ref, *outs):
+    for g, (start, stop) in enumerate(GROUPS):
+        for q in range(start, stop):
+            outs[g][q - start] = state_ref[q]
+    outs[0][GROUPS[0][1]] = visc_ref[0]
+
+
+def assemble(state, visc):
+    shapes = [stop - start for start, stop in GROUPS]
+    shapes[0] += 1
+    return pl.pallas_call(
+        assemble_kernel,
+        out_shape=tuple(jax.ShapeDtypeStruct((n, EXT, NZ), jnp.float32) for n in shapes),
+        in_specs=[VMEM, VMEM],
+        out_specs=tuple(VMEM for _ in shapes),
+        compiler_params=params(),
+        cost_estimate=pl.CostEstimate(flops=0, bytes_accessed=1400000, transcendentals=0),
+        name="assemble",
+    )(state, visc)
+
+
+def step_kernel(last, start, stop, diff_ref, vel_ref, assign_ref, u_ref, sib_ref, cross_ref, v_ref, vs_ref, vc_ref, *outs):
     run = lax.axis_index("run")
     even = lax.axis_index("core") == 0
     shape = (EXT, NZ)
@@ -88,8 +112,8 @@
     first_col = col == 0
     last_col = col == NZ - 1
     v = v_ref[0]
-    vs = vs_ref[0]
-    vc = vc_ref[0]
+    vs = vs_ref[GROUPS[0][1]]
+    vc = vc_ref[GROUPS[0][1]]
 
     def ahead_row(a):
         return pltpu.roll(a, EXT - 1, 0)
@@ -109,8 +133,8 @@
     c_ym = 0.5 * (v + behind_row(v))
     c_zp = 0.5 * (v + ahead_col(v))
     c_zm = 0.5 * (v + behind_col(v))
-    for q in range(RUNS):
-        s = assign_ref[q]
+    for q in range(stop - start):
+        s = assign_ref[start + q]
         kappa = diff_ref[s]
         ups = [-jnp.minimum(vel_ref[s, d], 0.0) for d in range(3)]
         downs = [jnp.maximum(vel_ref[s, d], 0.0) for d in range(3)]
@@ -129,13 +153,14 @@
         outs[-1][q] = pltpu.roll(new, EXT - HALO, 0)[:BLOCK]
 
 
-def advance(last, coefs, state, sib, cross, visc, visc_sib, visc_cross):
-    core = jax.ShapeDtypeStruct((RUNS, BLOCK, NZ), jnp.float32)
-    full = jax.ShapeDtypeStruct((RUNS, EXT, NZ), jnp.float32)
+def advance(last, group, coefs, state, sib, cross, visc, visc_sib, visc_cross):
+    start, stop = group
+    core = jax.ShapeDtypeStruct((stop - start, BLOCK, NZ), jnp.float32)
+    full = jax.ShapeDtypeStruct((stop - start, EXT, NZ), jnp.float32)
     out = (core,) if last else (full, core)
 
     def body(*refs):
-        step_kernel(last, *refs)
+        step_kernel(last, start, stop, *refs)
 
     return pl.pallas_call(
         body,
@@ -143,7 +168,9 @@
         in_specs=[SMEM, SMEM, SMEM] + [VMEM] * 6,
         out_specs=tuple(VMEM for _ in out),
         compiler_params=params(),
-        cost_estimate=pl.CostEstimate(flops=6000000, bytes_accessed=4000000, transcendentals=0),
+        cost_estimate=pl.CostEstimate(
+            flops=750000 * (stop - start), bytes_accessed=500000 * (stop - start), transcendentals=0
+        ),
         name="step_last" if last else "step",
     )(*coefs, state, sib, cross, visc, visc_sib, visc_cross)
 
@@ -160,9 +187,14 @@
     return keep + moved
 
 
+def by_run(refs):
+    return [refs[g].at[q - start] for g, (start, stop) in enumerate(GROUPS) for q in range(start, stop)]
+
+
 def gram_kernel(group, last, *refs):
-    cores = refs[: group + 1]
-    prev_ref = refs[group + 1] if group else None
+    pieces = len(GROUPS)
+    cores = [by_run(refs[pieces * t : pieces * t + pieces]) for t in range(group + 1)]
+    prev_ref = refs[pieces * (group + 1)] if group else None
     out_ref = refs[-1]
     mine = cores[group]
     lane = lane_iota((8, 128))
@@ -177,9 +209,9 @@
                 accs = list(accs)
                 for l in range(NZ // 128):
                     cols = slice(128 * l, 128 * l + 128)
-                    a = [mine[4 * half + k, rows, cols] for k in range(4)]
+                    a = [mine[4 * half + k][rows, cols] for k in range(4)]
                     for b in range(8):
-                        t = theirs[b, rows, cols]
+                        t = theirs[b][rows, cols]
                         for k in range(4):
                             accs[8 * k + b] = accs[8 * k + b] + a[k] * t
                 return tuple(accs)
@@ -194,7 +226,7 @@
                 at = 32 * other + 8 * group + 4 * half + k
                 packed = jnp.where(lane == at, total, packed)
     if last:
-        for i in range(RUNS):
+        for i in range(FIRST):
             out_ref[i] = packed
     else:
         out_ref[...] = packed
@@ -202,8 +234,8 @@
 
 def gram(cores, prev, last):
     group = len(cores) - 1
-    shape = (RUNS, 8, 128) if last else (8, 128)
-    args = list(cores) + ([prev] if group else [])
+    shape = (FIRST, 8, 128) if last else (8, 128)
+    args = [piece for core in cores for piece in core] + ([prev] if group else [])
 
     def body(*refs):
         gram_kernel(group, last, *refs)
@@ -221,18 +253,19 @@
 
 def spread_kernel(in_ref, out_ref):
     total = in_ref[0]
-    for i in range(1, RUNS):
+    for i in range(1, FIRST):
         total = total + in_ref[i]
-    for i in range(RUNS):
+    for i in range(SECOND):
         out_ref[i] = total
 
 
 def spread(parts):
     return pl.pallas_call(
         spread_kernel,
-        out_shape=jax.ShapeDtypeStruct(parts.shape, jnp.float32),
+        out_shape=jax.ShapeDtypeStruct((SECOND, 8, 128), jnp.float32),
         in_specs=[VMEM],
         out_specs=VMEM,
+        compiler_params=params(),
         name="spread",
     )(parts)
 
@@ -326,9 +359,12 @@
     return jnp.concatenate(rows, axis=0) if nodes > 1 else rows[0]
 
 
-def finish_kernel(order_ref, keep_ref, part_ref, c0, c1, c2, c3, out_ref, w_ref):
+def finish_kernel(order_ref, keep_ref, part_ref, *refs):
+    out_ref, w_ref = refs[-2:]
+    pieces = len(GROUPS)
+    cores = [by_run(refs[pieces * t : pieces * t + pieces]) for t in range(STEPS)]
     packed = part_ref[0]
-    for i in range(1, RUNS):
+    for i in range(1, part_ref.shape[0]):
         packed = packed + part_ref[i]
     size = RUNS * STEPS
     raw = jnp.concatenate(
@@ -369,7 +405,6 @@
     total = total * scale_col
     for c in range(STEPS):
         w_ref[c] = jnp.broadcast_to(total[:, c : c + 1], (size, 128))
-    cores = (c0, c1, c2, c3)
     for l in range(NZ // 128):
         cols = slice(128 * l, 128 * l + 128)
         for i in range(BLOCK // 8):
@@ -377,7 +412,7 @@
             accs = [None] * STEPS
             for q in range(RUNS):
                 for t in range(STEPS):
-                    x = cores[t][q, rws, cols]
+                    x = cores[t][q][rws, cols]
                     k = STEPS * q + t
                     for c in range(STEPS):
                         term = w_ref[c, k : k + 1, :] * x
@@ -390,13 +425,13 @@
     return pl.pallas_call(
         finish_kernel,
         out_shape=jax.ShapeDtypeStruct((STEPS, 1, BLOCK, NZ), jnp.float32),
-        in_specs=[SMEM, SMEM] + [VMEM] * 5,
+        in_specs=[SMEM, SMEM, VMEM] + [VMEM] * (STEPS * len(GROUPS)),
         out_specs=VMEM,
         scratch_shapes=[pltpu.VMEM((STEPS, RUNS * STEPS, 128), jnp.float32)],
         compiler_params=params(),
         cost_estimate=pl.CostEstimate(flops=5000000, bytes_accessed=2400000, transcendentals=0),
         name="finish",
-    )(order, keep, parts, *cores)
+    )(order, keep, parts, *[piece for core in cores for piece in core])
 
 
 def local(start_field, viscosity, diffusivity, velocity, assignment, child_order, keep_ranks):
@@ -404,25 +439,29 @@
     sibling = [(i, i ^ 1) for i in range(NX)]
     crossing = [(i, i + 1) for i in range(1, NX - 1, 2)] + [(i + 1, i) for i in range(1, NX - 1, 2)]
     blocks, visc = row_blocks(start_field, viscosity)
-    state = lax.all_to_all(blocks, "run", 0, 0)
-    send = jnp.concatenate([state, visc], axis=0)
+    states = list(assemble(lax.all_to_all(blocks, "run", 0, 0), visc))
     cores = []
     packed = None
     for step in range(STEPS):
-        cross = lax.ppermute(send, SPACE, crossing)
-        sib = lax.ppermute(send, SPACE, sibling)
+        last = step == STEPS - 1
+        halos = []
+        for state in states:
+            sib = lax.ppermute(state, SPACE, sibling)
+            cross = lax.ppermute(state, SPACE, crossing)
+            halos.append((sib, cross))
+        if step == 0:
+            around = halos[0]
         if cores:
             packed = gram(cores, packed, False)
-        if step == 0:
-            visc_sib, visc_cross = sib[RUNS:], cross[RUNS:]
-        last = step == STEPS - 1
-        result = advance(last, coefs, state, sib, cross, visc, visc_sib, visc_cross)
-        cores.append(result[-1])
-        state = send = result[0]
+        results = [
+            advance(last, group, coefs, state, *halo, visc, *around)
+            for group, state, halo in zip(GROUPS, states, halos)
+        ]
+        cores.append([result[-1] for result in results])
+        states = [result[0] for result in results]
     parts = gram(cores, packed, True)
-    parts = spread(lax.all_to_all(parts, ("x", "core"), 0, 0))
-    parts = spread(lax.all_to_all(parts, "y", 0, 0))
-    parts = lax.all_to_all(parts, "run", 0, 0)
+    parts = spread(lax.all_to_all(parts, ("y", "core"), 0, 0))
+    parts = lax.all_to_all(parts, ("run", "x"), 0, 0)
     return finish(child_order, keep_ranks, parts, cores)
 
 

time: 149 us -> 127 us (0.85)
  waiting for transfers between devices: 31.4 us -> 0.04 us
  starting transfers between devices: 24.8 us -> 46.1 us
  blocking collectives: 67.9 us -> 57.8 us
  local copies, waits for them, and re-layouts: 3.74 us -> 2.2 us
    ppermute x8 -> x16, waiting for transfers between devices: 31.4 us -> 0.04 us  [the longest x8 0.02 us: local(): cross = lax.ppermute(state, SPACE, crossing)]
    ppermute x8 -> x16, starting transfers between devices: 24.8 us -> 46.1 us  [the longest x8 30.7 us: local(): cross = lax.ppermute(state, SPACE, crossing)]
    all_to_all x4 -> x3, blocking collectives: 67.9 us -> 57.8 us  [the longest x1 29.8 us: local(): states = list(assemble(lax.all_to_all(blocks, 'run', 0, 0), visc))]
    pallas_call x4 -> x8, Pallas kernels: 7.02 us -> 9.75 us  [advance(): pl.pallas_call(body, out_shape=out, in_specs=[SMEM, SMEM, SMEM] + [VMEM]...]
    pallas_call x2, Pallas kernels: 2.76 us -> 0.07 us  [the longest x1 0.05 us: assemble(): pl.pallas_call(assemble_kernel, out_shape=tuple((jax.ShapeDtypeStruct((n,...]
    unnamed x16 -> x15, local copies, waits for them, and re-layouts: 3.07 us -> 2.2 us
  transfers between devices with their start and end apart: 8 -> 16, of which waited for: 4 -> 0; matrix products, arithmetic and copies ran while one was open for 0% -> 0% of each run, Pallas kernels for 2% -> 9%
where the time goes in v2:
time: 127 us; the launch traced here: 126 us
  blocking collectives  57.8 us (46%)
  starting transfers between devices  46.1 us (36%)
  Pallas kernels  19.6 us (15%)
  local copies, waits for them, and re-layouts  2.2 us (2%)
    ppermute x8, starting transfers between devices, local(): cross = lax.ppermute(state, SPACE, crossing)  30.7 us
    all_to_all x1, blocking collectives, local(): states = list(assemble(lax.all_to_all(blocks, 'run', 0, 0), visc))  29.8 us
    ppermute x8, starting transfers between devices, local(): sib = lax.ppermute(state, SPACE, sibling)  15.4 us
    all_to_all x1, blocking collectives, local(): parts = lax.all_to_all(parts, ('run', 'x'), 0, 0)  14.5 us
    all_to_all x1, blocking collectives, local(): parts = spread(lax.all_to_all(parts, ('y', 'core'), 0, 0))  13.4 us
    pallas_call x8, Pallas kernels, advance(): pl.pallas_call(body, out_shape=out, in_specs=[SMEM, SMEM, SMEM] + [VMEM]...  9.75 us
    pallas_call x4, Pallas kernels, gram(): pl.pallas_call(body, out_shape=jax.ShapeDtypeStruct(shape, jnp.float32),...  5.35 us
    pallas_call x1, Pallas kernels, finish(): pl.pallas_call(finish_kernel, out_shape=jax.ShapeDtypeStruct((STEPS, 1, B...  4.33 us
  transfers between devices with their start and end apart: 16, of which 0 were waited for; matrix products, arithmetic and copies ran while one was open for 0% of the time, Pallas kernels for 9%

profile of v2, /device:TPU:1, one launch (start us, length us, event | category | flops | bytes accessed | tf_op | source)
XLA Modules:
  0.0 126.0 jit_solution(14869263637237058624)
XLA Ops:
  2.2 29.8 %all_to_all.15.state_ref = f32[8,40,512]{2,1,0:T(8,128)S(1)} all-to-all(f32[8,40,512]{2,1,0:T(8,128)S(1)} %get-tuple-element.21), channel_id=1, replica_groups=mesh['run'=8,'x'=4,'y'=8,'core'=2] {'run'}, dimensions={0} | all-to-all | bytes 1310720 | tf_op jit(solution)/shard_map/all_to_all | solution.py:442
  32.0 5.2 %collective-permute-start.1 = (f32[5,40,512]{2,1,0:T(8,128)S(1)}, f32[5,40,512]{2,1,0:T(8,128)S(1)}, u32[]{:S(2)}, u32[]{:S(2)}) collective-permute-start(f32[5,40,512]{2,1,0:T(8,128)S(1)} %get-tuple-element.23.refs_3_), channel_id=1, source_target_pairs={{1,2},{3,4},{5,6},{7,8},{9,10},{11,12},{13,14},{15,16},{17,18},{19... | collective-permute-start | bytes 1228808 | tf_op jit(solution)/shard_map/ppermute | solution.py:450
  37.2 1.9 %collective-permute-start = (f32[5,40,512]{2,1,0:T(8,128)S(1)}, f32[5,40,512]{2,1,0:T(8,128)S(1)}, u32[]{:S(2)}, u32[]{:S(2)}) collective-permute-start(f32[5,40,512]{2,1,0:T(8,128)S(1)} %get-tuple-element.23.refs_3_), channel_id=1, source_target_pairs={{0,1},{1,0},{2,3},{3,2},{4,5},{5,4},{6,7},{7,6},{8,9},{9,8},{10,11... | collective-permute-start | bytes 1228808 | tf_op jit(solution)/shard_map/ppermute | solution.py:449
  39.2 3.6 %collective-permute-start.3 = (f32[4,40,512]{2,1,0:T(8,128)S(1)}, f32[4,40,512]{2,1,0:T(8,128)S(1)}, u32[]{:S(2)}, u32[]{:S(2)}) collective-permute-start(f32[4,40,512]{2,1,0:T(8,128)S(1)} %get-tuple-element.25.refs_3_), channel_id=1, source_target_pairs={{1,2},{3,4},{5,6},{7,8},{9,10},{11,12},{13,14},{15,16},{17,18},{19... | collective-permute-start | bytes 983048 | tf_op jit(solution)/shard_map/ppermute | solution.py:450
  42.8 1.9 %collective-permute-start.2 = (f32[4,40,512]{2,1,0:T(8,128)S(1)}, f32[4,40,512]{2,1,0:T(8,128)S(1)}, u32[]{:S(2)}, u32[]{:S(2)}) collective-permute-start(f32[4,40,512]{2,1,0:T(8,128)S(1)} %get-tuple-element.25.refs_3_), channel_id=1, source_target_pairs={{0,1},{1,0},{2,3},{3,2},{4,5},{5,4},{6,7},{7,6},{8,9},{9,8},{10,11... | collective-permute-start | bytes 983048 | tf_op jit(solution)/shard_map/ppermute | solution.py:449
  46.0 3.6 %collective-permute-start.5 = (f32[4,40,512]{2,1,0:T(8,128)S(1)}, f32[4,40,512]{2,1,0:T(8,128)S(1)}, u32[]{:S(2)}, u32[]{:S(2)}) collective-permute-start(f32[4,40,512]{2,1,0:T(8,128)S(1)} %get-tuple-element.27.refs_3_), channel_id=1, source_target_pairs={{1,2},{3,4},{5,6},{7,8},{9,10},{11,12},{13,14},{15,16},{17,18},{19... | collective-permute-start | bytes 983048 | tf_op jit(solution)/shard_map/ppermute | solution.py:450
  49.6 1.9 %collective-permute-start.4 = (f32[4,40,512]{2,1,0:T(8,128)S(1)}, f32[4,40,512]{2,1,0:T(8,128)S(1)}, u32[]{:S(2)}, u32[]{:S(2)}) collective-permute-start(f32[4,40,512]{2,1,0:T(8,128)S(1)} %get-tuple-element.27.refs_3_), channel_id=1, source_target_pairs={{0,1},{1,0},{2,3},{3,2},{4,5},{5,4},{6,7},{7,6},{8,9},{9,8},{10,11... | collective-permute-start | bytes 983048 | tf_op jit(solution)/shard_map/ppermute | solution.py:449
  51.6 1.2 step.7
  52.8 4.8 %collective-permute-start.7 = (f32[4,40,512]{2,1,0:T(8,128)S(1)}, f32[4,40,512]{2,1,0:T(8,128)S(1)}, u32[]{:S(2)}, u32[]{:S(2)}) collective-permute-start(f32[4,40,512]{2,1,0:T(8,128)S(1)} %get-tuple-element.29.refs_3_), channel_id=1, source_target_pairs={{1,2},{3,4},{5,6},{7,8},{9,10},{11,12},{13,14},{15,16},{17,18},{19... | collective-permute-start | bytes 983048 | tf_op jit(solution)/shard_map/ppermute | solution.py:450
  57.6 1.9 %collective-permute-start.6 = (f32[4,40,512]{2,1,0:T(8,128)S(1)}, f32[4,40,512]{2,1,0:T(8,128)S(1)}, u32[]{:S(2)}, u32[]{:S(2)}) collective-permute-start(f32[4,40,512]{2,1,0:T(8,128)S(1)} %get-tuple-element.29.refs_3_), channel_id=1, source_target_pairs={{0,1},{1,0},{2,3},{3,2},{4,5},{5,4},{6,7},{7,6},{8,9},{9,8},{10,11... | collective-permute-start | bytes 983048 | tf_op jit(solution)/shard_map/ppermute | solution.py:449
  60.8 2.7 %collective-permute-start.9 = (f32[4,40,512]{2,1,0:T(8,128)S(1)}, f32[4,40,512]{2,1,0:T(8,128)S(1)}, u32[]{:S(2)}, u32[]{:S(2)}) collective-permute-start(f32[4,40,512]{2,1,0:T(8,128)S(1)} %get-tuple-element.31.refs_3_), channel_id=1, source_target_pairs={{1,2},{3,4},{5,6},{7,8},{9,10},{11,12},{13,14},{15,16},{17,18},{19... | collective-permute-start | bytes 983048 | tf_op jit(solution)/shard_map/ppermute | solution.py:450
  63.5 1.9 %collective-permute-start.8 = (f32[4,40,512]{2,1,0:T(8,128)S(1)}, f32[4,40,512]{2,1,0:T(8,128)S(1)}, u32[]{:S(2)}, u32[]{:S(2)}) collective-permute-start(f32[4,40,512]{2,1,0:T(8,128)S(1)} %get-tuple-element.31.refs_3_), channel_id=1, source_target_pairs={{0,1},{1,0},{2,3},{3,2},{4,5},{5,4},{6,7},{7,6},{8,9},{9,8},{10,11... | collective-permute-start | bytes 983048 | tf_op jit(solution)/shard_map/ppermute | solution.py:449
  66.7 4.1 %collective-permute-start.11 = (f32[4,40,512]{2,1,0:T(8,128)S(1)}, f32[4,40,512]{2,1,0:T(8,128)S(1)}, u32[]{:S(2)}, u32[]{:S(2)}) collective-permute-start(f32[4,40,512]{2,1,0:T(8,128)S(1)} %get-tuple-element.33.refs_3_), channel_id=1, source_target_pairs={{1,2},{3,4},{5,6},{7,8},{9,10},{11,12},{13,14},{15,16},{17,18},{19... | collective-permute-start | bytes 983048 | tf_op jit(solution)/shard_map/ppermute | solution.py:450
  70.8 1.9 %collective-permute-start.10 = (f32[4,40,512]{2,1,0:T(8,128)S(1)}, f32[4,40,512]{2,1,0:T(8,128)S(1)}, u32[]{:S(2)}, u32[]{:S(2)}) collective-permute-start(f32[4,40,512]{2,1,0:T(8,128)S(1)} %get-tuple-element.33.refs_3_), channel_id=1, source_target_pairs={{0,1},{1,0},{2,3},{3,2},{4,5},{5,4},{6,7},{7,6},{8,9},{9,8},{10,11... | collective-permute-start | bytes 983048 | tf_op jit(solution)/shard_map/ppermute | solution.py:449
  72.7 1.2 step.10
  73.9 2.7 %collective-permute-start.13 = (f32[4,40,512]{2,1,0:T(8,128)S(1)}, f32[4,40,512]{2,1,0:T(8,128)S(1)}, u32[]{:S(2)}, u32[]{:S(2)}) collective-permute-start(f32[4,40,512]{2,1,0:T(8,128)S(1)} %get-tuple-element.35.refs_3_), channel_id=1, source_target_pairs={{1,2},{3,4},{5,6},{7,8},{9,10},{11,12},{13,14},{15,16},{17,18},{19... | collective-permute-start | bytes 983048 | tf_op jit(solution)/shard_map/ppermute | solution.py:450
  76.6 1.9 %collective-permute-start.12 = (f32[4,40,512]{2,1,0:T(8,128)S(1)}, f32[4,40,512]{2,1,0:T(8,128)S(1)}, u32[]{:S(2)}, u32[]{:S(2)}) collective-permute-start(f32[4,40,512]{2,1,0:T(8,128)S(1)} %get-tuple-element.35.refs_3_), channel_id=1, source_target_pairs={{0,1},{1,0},{2,3},{3,2},{4,5},{5,4},{6,7},{7,6},{8,9},{9,8},{10,11... | collective-permute-start | bytes 983048 | tf_op jit(solution)/shard_map/ppermute | solution.py:449
  79.8 4.1 %collective-permute-start.15 = (f32[4,40,512]{2,1,0:T(8,128)S(1)}, f32[4,40,512]{2,1,0:T(8,128)S(1)}, u32[]{:S(2)}, u32[]{:S(2)}) collective-permute-start(f32[4,40,512]{2,1,0:T(8,128)S(1)} %get-tuple-element.36.refs_3_), channel_id=1, source_target_pairs={{1,2},{3,4},{5,6},{7,8},{9,10},{11,12},{13,14},{15,16},{17,18},{19... | collective-permute-start | bytes 983048 | tf_op jit(solution)/shard_map/ppermute | solution.py:450
  83.9 1.9 %collective-permute-start.14 = (f32[4,40,512]{2,1,0:T(8,128)S(1)}, f32[4,40,512]{2,1,0:T(8,128)S(1)}, u32[]{:S(2)}, u32[]{:S(2)}) collective-permute-start(f32[4,40,512]{2,1,0:T(8,128)S(1)} %get-tuple-element.36.refs_3_), channel_id=1, source_target_pairs={{0,1},{1,0},{2,3},{3,2},{4,5},{5,4},{6,7},{7,6},{8,9},{9,8},{10,11... | collective-permute-start | bytes 983048 | tf_op jit(solution)/shard_map/ppermute | solution.py:449
  87.4 1.6 %gram2.1.refs_8_ = f32[8,128]{1,0:T(8,128)S(1)} custom-call(f32[4,32,512]{2,1,0:T(8,128)S(1)} %get-tuple-element.24.refs_0_, f32[4,32,512]{2,1,0:T(8,128)S(1)} %get-tuple-element.26.refs_1_, f32[4,32,512]{2,1,0:T(8,128)S(1)} %get-tuple-element.28.refs_2_, f32[4,32,512]{2,1,0:T(8,128)S(1)} %get-tuple-element.30.refs_3_, ...), custom_call_target="tpu_custom_call" | custom-call | flops 6600000 | bytes 1800000 | tf_op jit(solution)/shard_map/gram2/pallas_call | solution.py:243
  91.5 2.2 %gram3.1 = f32[16,8,128]{2,1,0:T(8,128)S(1)} custom-call(f32[4,32,512]{2,1,0:T(8,128)S(1)} %get-tuple-element.24.refs_0_, f32[4,32,512]{2,1,0:T(8,128)S(1)} %get-tuple-element.26.refs_1_, f32[4,32,512]{2,1,0:T(8,128)S(1)} %get-tuple-element.28.refs_2_, f32[4,32,512]{2,1,0:T(8,128)S(1)} %get-tuple-element.30.refs_3_, ...), custom_call_target="tpu_custom_call" | custom-call | flops 8800000 | bytes 2400000 | tf_op jit(solution)/shard_map/gram3/pallas_call | solution.py:243
  93.7 13.4 %all_to_all.16.in_ref = f32[16,8,128]{2,1,0:T(8,128)S(1)} all-to-all(f32[16,8,128]{2,1,0:T(8,128)S(1)} %gram3.1), channel_id=1, replica_groups=mesh['run'=8,'x'=4,'y'=8,'core'=2] {'y','core'}, dimensions={0} | all-to-all | bytes 131072 | tf_op jit(solution)/shard_map/all_to_all | solution.py:463
  107.2 14.5 %all_to_all.17.part_ref = f32[32,8,128]{2,1,0:T(8,128)S(1)} all-to-all(f32[32,8,128]{2,1,0:T(8,128)S(1)} %spread.1), channel_id=1, replica_groups=mesh['run'=8,'x'=4,'y'=8,'core'=2] {'run','x'}, dimensions={0} | all-to-all | bytes 262144 | tf_op jit(solution)/shard_map/all_to_all | solution.py:464
  121.7 4.3 %finish.1 = f32[4,1,32,512]{3,2,1,0:T(8,128)} custom-call(s32[7,8]{1,0:T(8,128)S(1)} %copy-done.4, s32[7]{0:T(128)S(1)} %copy-done.5, f32[32,8,128]{2,1,0:T(8,128)S(1)} %all_to_all.17.part_ref, f32[4,32,512]{2,1,0:T(8,128)S(1)} %get-tuple-element.24.refs_0_, f32[4,32,512]{2,1,0:T(8,128)S(1)} %get-tuple-element.26.refs_1_, ...), custom_call_target="tpu_custom_call" | custom-call | flops 5000000 | bytes 2400000 | tf_op jit(solution)/shard_map/finish/pallas_call | solution.py:425
  (42 shorter events, 11.2 us)
Async XLA Ops:
  0.0 1.0 copy-start
  1.0 1.0 copy-start.1
  32.0 12.7 %copy-start.6 = (f32[8,3]{0,1:T(4,128)S(1)}, f32[8,3]{0,1:T(4,128)}, u32[]{:S(2)}) copy-start(f32[8,3]{0,1:T(4,128)} %param.10) | copy-start | bytes 292
  32.0 12.8 %collective-permute-start.1 = (f32[5,40,512]{2,1,0:T(8,128)S(1)}, f32[5,40,512]{2,1,0:T(8,128)S(1)}, u32[]{:S(2)}, u32[]{:S(2)}) collective-permute-start(f32[5,40,512]{2,1,0:T(8,128)S(1)} %get-tuple-element.23.refs_3_), channel_id=1, source_target_pairs={{1,2},{3,4},{5,6},{7,8},{9,10},{11,12},{13,14},{15,16},{17,18},{19... | collective-permute-start | bytes 1228808 | tf_op jit(solution)/shard_map/ppermute | solution.py:450
  37.2 7.6 %collective-permute-start = (f32[5,40,512]{2,1,0:T(8,128)S(1)}, f32[5,40,512]{2,1,0:T(8,128)S(1)}, u32[]{:S(2)}, u32[]{:S(2)}) collective-permute-start(f32[5,40,512]{2,1,0:T(8,128)S(1)} %get-tuple-element.23.refs_3_), channel_id=1, source_target_pairs={{0,1},{1,0},{2,3},{3,2},{4,5},{5,4},{6,7},{7,6},{8,9},{9,8},{10,11... | collective-permute-start | bytes 1228808 | tf_op jit(solution)/shard_map/ppermute | solution.py:449
  39.2 5.6 %copy-start.2 = (f32[8]{0:T(128)S(1)}, f32[8]{0:T(128)}, u32[]{:S(2)}) copy-start(f32[8]{0:T(128)} %refs_0_.15) | copy-start | bytes 100
  39.2 5.6 %copy-start.3 = (s32[8]{0:T(128)S(1)}, s32[8]{0:T(128)}, u32[]{:S(2)}) copy-start(s32[8]{0:T(128)} %refs_2_.15) | copy-start | bytes 100
  39.2 12.4 %collective-permute-start.3 = (f32[4,40,512]{2,1,0:T(8,128)S(1)}, f32[4,40,512]{2,1,0:T(8,128)S(1)}, u32[]{:S(2)}, u32[]{:S(2)}) collective-permute-start(f32[4,40,512]{2,1,0:T(8,128)S(1)} %get-tuple-element.25.refs_3_), channel_id=1, source_target_pairs={{1,2},{3,4},{5,6},{7,8},{9,10},{11,12},{13,14},{15,16},{17,18},{19... | collective-permute-start | bytes 983048 | tf_op jit(solution)/shard_map/ppermute | solution.py:450
  42.8 8.8 %collective-permute-start.2 = (f32[4,40,512]{2,1,0:T(8,128)S(1)}, f32[4,40,512]{2,1,0:T(8,128)S(1)}, u32[]{:S(2)}, u32[]{:S(2)}) collective-permute-start(f32[4,40,512]{2,1,0:T(8,128)S(1)} %get-tuple-element.25.refs_3_), channel_id=1, source_target_pairs={{0,1},{1,0},{2,3},{3,2},{4,5},{5,4},{6,7},{7,6},{8,9},{9,8},{10,11... | collective-permute-start | bytes 983048 | tf_op jit(solution)/shard_map/ppermute | solution.py:449
  46.0 13.5 %collective-permute-start.5 = (f32[4,40,512]{2,1,0:T(8,128)S(1)}, f32[4,40,512]{2,1,0:T(8,128)S(1)}, u32[]{:S(2)}, u32[]{:S(2)}) collective-permute-start(f32[4,40,512]{2,1,0:T(8,128)S(1)} %get-tuple-element.27.refs_3_), channel_id=1, source_target_pairs={{1,2},{3,4},{5,6},{7,8},{9,10},{11,12},{13,14},{15,16},{17,18},{19... | collective-permute-start | bytes 983048 | tf_op jit(solution)/shard_map/ppermute | solution.py:450
  49.6 9.9 %collective-permute-start.4 = (f32[4,40,512]{2,1,0:T(8,128)S(1)}, f32[4,40,512]{2,1,0:T(8,128)S(1)}, u32[]{:S(2)}, u32[]{:S(2)}) collective-permute-start(f32[4,40,512]{2,1,0:T(8,128)S(1)} %get-tuple-element.27.refs_3_), channel_id=1, source_target_pairs={{0,1},{1,0},{2,3},{3,2},{4,5},{5,4},{6,7},{7,6},{8,9},{9,8},{10,11... | collective-permute-start | bytes 983048 | tf_op jit(solution)/shard_map/ppermute | solution.py:449
  52.8 12.6 %collective-permute-start.7 = (f32[4,40,512]{2,1,0:T(8,128)S(1)}, f32[4,40,512]{2,1,0:T(8,128)S(1)}, u32[]{:S(2)}, u32[]{:S(2)}) collective-permute-start(f32[4,40,512]{2,1,0:T(8,128)S(1)} %get-tuple-element.29.refs_3_), channel_id=1, source_target_pairs={{1,2},{3,4},{5,6},{7,8},{9,10},{11,12},{13,14},{15,16},{17,18},{19... | collective-permute-start | bytes 983048 | tf_op jit(solution)/shard_map/ppermute | solution.py:450
  57.6 7.8 %collective-permute-start.6 = (f32[4,40,512]{2,1,0:T(8,128)S(1)}, f32[4,40,512]{2,1,0:T(8,128)S(1)}, u32[]{:S(2)}, u32[]{:S(2)}) collective-permute-start(f32[4,40,512]{2,1,0:T(8,128)S(1)} %get-tuple-element.29.refs_3_), channel_id=1, source_target_pairs={{0,1},{1,0},{2,3},{3,2},{4,5},{5,4},{6,7},{7,6},{8,9},{9,8},{10,11... | collective-permute-start | bytes 983048 | tf_op jit(solution)/shard_map/ppermute | solution.py:449
  60.8 11.9 %collective-permute-start.9 = (f32[4,40,512]{2,1,0:T(8,128)S(1)}, f32[4,40,512]{2,1,0:T(8,128)S(1)}, u32[]{:S(2)}, u32[]{:S(2)}) collective-permute-start(f32[4,40,512]{2,1,0:T(8,128)S(1)} %get-tuple-element.31.refs_3_), channel_id=1, source_target_pairs={{1,2},{3,4},{5,6},{7,8},{9,10},{11,12},{13,14},{15,16},{17,18},{19... | collective-permute-start | bytes 983048 | tf_op jit(solution)/shard_map/ppermute | solution.py:450
  63.5 9.2 %collective-permute-start.8 = (f32[4,40,512]{2,1,0:T(8,128)S(1)}, f32[4,40,512]{2,1,0:T(8,128)S(1)}, u32[]{:S(2)}, u32[]{:S(2)}) collective-permute-start(f32[4,40,512]{2,1,0:T(8,128)S(1)} %get-tuple-element.31.refs_3_), channel_id=1, source_target_pairs={{0,1},{1,0},{2,3},{3,2},{4,5},{5,4},{6,7},{7,6},{8,9},{9,8},{10,11... | collective-permute-start | bytes 983048 | tf_op jit(solution)/shard_map/ppermute | solution.py:449
  66.7 11.9 %collective-permute-start.11 = (f32[4,40,512]{2,1,0:T(8,128)S(1)}, f32[4,40,512]{2,1,0:T(8,128)S(1)}, u32[]{:S(2)}, u32[]{:S(2)}) collective-permute-start(f32[4,40,512]{2,1,0:T(8,128)S(1)} %get-tuple-element.33.refs_3_), channel_id=1, source_target_pairs={{1,2},{3,4},{5,6},{7,8},{9,10},{11,12},{13,14},{15,16},{17,18},{19... | collective-permute-start | bytes 983048 | tf_op jit(solution)/shard_map/ppermute | solution.py:450
  70.8 7.8 %collective-permute-start.10 = (f32[4,40,512]{2,1,0:T(8,128)S(1)}, f32[4,40,512]{2,1,0:T(8,128)S(1)}, u32[]{:S(2)}, u32[]{:S(2)}) collective-permute-start(f32[4,40,512]{2,1,0:T(8,128)S(1)} %get-tuple-element.33.refs_3_), channel_id=1, source_target_pairs={{0,1},{1,0},{2,3},{3,2},{4,5},{5,4},{6,7},{7,6},{8,9},{9,8},{10,11... | collective-permute-start | bytes 983048 | tf_op jit(solution)/shard_map/ppermute | solution.py:449
  73.9 15.1 %collective-permute-start.13 = (f32[4,40,512]{2,1,0:T(8,128)S(1)}, f32[4,40,512]{2,1,0:T(8,128)S(1)}, u32[]{:S(2)}, u32[]{:S(2)}) collective-permute-start(f32[4,40,512]{2,1,0:T(8,128)S(1)} %get-tuple-element.35.refs_3_), channel_id=1, source_target_pairs={{1,2},{3,4},{5,6},{7,8},{9,10},{11,12},{13,14},{15,16},{17,18},{19... | collective-permute-start | bytes 983048 | tf_op jit(solution)/shard_map/ppermute | solution.py:450
  76.6 12.4 %collective-permute-start.12 = (f32[4,40,512]{2,1,0:T(8,128)S(1)}, f32[4,40,512]{2,1,0:T(8,128)S(1)}, u32[]{:S(2)}, u32[]{:S(2)}) collective-permute-start(f32[4,40,512]{2,1,0:T(8,128)S(1)} %get-tuple-element.35.refs_3_), channel_id=1, source_target_pairs={{0,1},{1,0},{2,3},{3,2},{4,5},{5,4},{6,7},{7,6},{8,9},{9,8},{10,11... | collective-permute-start | bytes 983048 | tf_op jit(solution)/shard_map/ppermute | solution.py:449
  79.8 10.4 %collective-permute-start.15 = (f32[4,40,512]{2,1,0:T(8,128)S(1)}, f32[4,40,512]{2,1,0:T(8,128)S(1)}, u32[]{:S(2)}, u32[]{:S(2)}) collective-permute-start(f32[4,40,512]{2,1,0:T(8,128)S(1)} %get-tuple-element.36.refs_3_), channel_id=1, source_target_pairs={{1,2},{3,4},{5,6},{7,8},{9,10},{11,12},{13,14},{15,16},{17,18},{19... | collective-permute-start | bytes 983048 | tf_op jit(solution)/shard_map/ppermute | solution.py:450
  83.9 6.3 %collective-permute-start.14 = (f32[4,40,512]{2,1,0:T(8,128)S(1)}, f32[4,40,512]{2,1,0:T(8,128)S(1)}, u32[]{:S(2)}, u32[]{:S(2)}) collective-permute-start(f32[4,40,512]{2,1,0:T(8,128)S(1)} %get-tuple-element.36.refs_3_), channel_id=1, source_target_pairs={{0,1},{1,0},{2,3},{3,2},{4,5},{5,4},{6,7},{7,6},{8,9},{9,8},{10,11... | collective-permute-start | bytes 983048 | tf_op jit(solution)/shard_map/ppermute | solution.py:449
  107.1 14.6 %copy-start.4 = (s32[7,8]{1,0:T(8,128)S(1)}, s32[7,8]{1,0:T(8,128)}, u32[]{:S(2)}) copy-start(s32[7,8]{1,0:T(8,128)} %order_ref.1) | copy-start | bytes 676
  107.1 14.5 %copy-start.5 = (s32[7]{0:T(128)S(1)}, s32[7]{0:T(128)}, u32[]{:S(2)}) copy-start(s32[7]{0:T(128)} %keep_ref.1) | copy-start | bytes 88

commit v3 on v1

--- a/solution.py
+++ b/solution.py
@@ -20,6 +20,8 @@
 CELLS = NX * NY * NZ
 EXACT = lax.Precision.HIGHEST
 SPACE = ("x", "y", "core")
+FIRST = 16
+SECOND = 32
 VMEM = pl.BlockSpec(memory_space=pltpu.VMEM)
 SMEM = pl.BlockSpec(memory_space=pltpu.SMEM)
 
@@ -36,60 +38,95 @@
     return pltpu.CompilerParams(vmem_limit_bytes=limit)
 
 
-def blocks_kernel(field_ref, visc_ref, out_ref, visc_out):
-    run = lax.axis_index("run")
+ROWS = 8
+TILES = NY // 8
+
+
+def shifted(before, after):
     low = sub_iota((8, NZ)) < 4
+    return pltpu.roll(jnp.where(low, after, before), 4, 0)
+
+
+def blocks_kernel(field_ref, out_ref):
     zero = jnp.zeros((8, NZ), jnp.float32)
-    tiles = NY // 8
-
-    def shifted(before, after):
-        return pltpu.roll(jnp.where(low, after, before), 4, 0)
-
     before = zero
-    for m in range(tiles + 1):
-        after = field_ref[0, 0, 8 * m : 8 * m + 8, :] if m < tiles else zero
+    for m in range(TILES + 1):
+        after = field_ref[0, 0, 8 * m : 8 * m + 8, :] if m < TILES else zero
         tile = shifted(before, after)
         before = after
         for q in range(RUNS):
             j = m - 4 * q
             if 0 <= j <= 4:
                 out_ref[q, 8 * j : 8 * j + 8, :] = tile
+
+
+def row_blocks(field):
+    return pl.pallas_call(
+        blocks_kernel,
+        out_shape=jax.ShapeDtypeStruct((RUNS, EXT, NZ), jnp.float32),
+        in_specs=[VMEM],
+        out_specs=VMEM,
+        compiler_params=params(),
+        cost_estimate=pl.CostEstimate(flops=200000, bytes_accessed=1200000, transcendentals=0),
+        name="row_blocks",
+    )(field)
+
+
+def rates_kernel(diff_ref, vel_ref, assign_ref, table_ref):
+    even = lax.axis_index("core") == 0
+    for q in range(RUNS):
+        s = assign_ref[q]
+        ups = [-jnp.minimum(vel_ref[d, s], 0.0) for d in range(3)]
+        downs = [jnp.maximum(vel_ref[d, s], 0.0) for d in range(3)]
+        w_sib = jnp.where(even, ups[0], downs[0])
+        w_cross = jnp.where(even, downs[0], ups[0])
+        values = (0.5 * diff_ref[s], w_sib, w_cross, ups[1], downs[1], ups[2], downs[2])
+        for k, value in enumerate(values):
+            table_ref[ROWS * q + k : ROWS * q + k + 1, :] = jnp.full((1, NZ), value, jnp.float32)
+
+
+def run_rates(diffusivity, velocity, assignment):
+    return pl.pallas_call(
+        rates_kernel,
+        out_shape=jax.ShapeDtypeStruct((ROWS * RUNS, NZ), jnp.float32),
+        in_specs=[SMEM, SMEM, SMEM],
+        out_specs=VMEM,
+        compiler_params=params(),
+        cost_estimate=pl.CostEstimate(flops=0, bytes_accessed=140000, transcendentals=0),
+        name="rates",
+    )(diffusivity, velocity.T, assignment)
+
+
+def assemble_kernel(state_ref, visc_ref, out_ref):
+    run = lax.axis_index("run")
+    for q in range(RUNS):
+        out_ref[q] = state_ref[q]
     for j in range(5):
         m = 4 * run + j
         prev_at = pl.multiple_of(8 * jnp.maximum(m - 1, 0), 8)
-        next_at = pl.multiple_of(8 * jnp.minimum(m, tiles - 1), 8)
+        next_at = pl.multiple_of(8 * jnp.minimum(m, TILES - 1), 8)
         prev = jnp.where(m > 0, visc_ref[0, pl.ds(prev_at, 8), :], 0.0)
-        nxt = jnp.where(m < tiles, visc_ref[0, pl.ds(next_at, 8), :], 0.0)
-        visc_out[0, 8 * j : 8 * j + 8, :] = shifted(prev, nxt)
-
-
-def row_blocks(field, visc):
-    return pl.pallas_call(
-        blocks_kernel,
-        out_shape=(
-            jax.ShapeDtypeStruct((RUNS, EXT, NZ), jnp.float32),
-            jax.ShapeDtypeStruct((1, EXT, NZ), jnp.float32),
-        ),
+        nxt = jnp.where(m < TILES, visc_ref[0, pl.ds(next_at, 8), :], 0.0)
+        out_ref[RUNS, 8 * j : 8 * j + 8, :] = shifted(prev, nxt)
+
+
+def assemble(state, visc):
+    return pl.pallas_call(
+        assemble_kernel,
+        out_shape=jax.ShapeDtypeStruct((RUNS + 1, EXT, NZ), jnp.float32),
         in_specs=[VMEM, VMEM],
-        out_specs=(VMEM, VMEM),
-        compiler_params=params(),
-        cost_estimate=pl.CostEstimate(flops=200000, bytes_accessed=2000000, transcendentals=0),
-        name="row_blocks",
-    )(field, visc)
-
-
-def step_kernel(last, diff_ref, vel_ref, assign_ref, u_ref, sib_ref, cross_ref, v_ref, vs_ref, vc_ref, *outs):
-    run = lax.axis_index("run")
-    even = lax.axis_index("core") == 0
-    shape = (EXT, NZ)
-    row = sub_iota(shape) + (BLOCK * run - HALO)
-    inside = (row >= 0) & (row < NY)
-    col = lane_iota(shape)
+        out_specs=VMEM,
+        compiler_params=params(),
+        cost_estimate=pl.CostEstimate(flops=0, bytes_accessed=1400000, transcendentals=0),
+        name="assemble",
+    )(state, visc)
+
+
+def interior_kernel(u_ref, v_ref, table_ref, out_ref):
+    col = lane_iota((EXT, NZ))
     first_col = col == 0
     last_col = col == NZ - 1
-    v = v_ref[0]
-    vs = vs_ref[0]
-    vc = vc_ref[0]
+    v = v_ref[RUNS]
 
     def ahead_row(a):
         return pltpu.roll(a, EXT - 1, 0)
@@ -103,49 +140,67 @@
     def behind_col(a):
         return jnp.where(first_col, 0.0, pltpu.roll(a, 1, 1))
 
-    c_sib = 0.5 * (v + vs)
-    c_cross = 0.5 * (v + vc)
-    c_yp = 0.5 * (v + ahead_row(v))
-    c_ym = 0.5 * (v + behind_row(v))
-    c_zp = 0.5 * (v + ahead_col(v))
-    c_zm = 0.5 * (v + behind_col(v))
+    moves = (ahead_row, behind_row, ahead_col, behind_col)
+    coefs = [v + move(v) for move in moves]
     for q in range(RUNS):
-        s = assign_ref[q]
-        kappa = diff_ref[s]
-        ups = [-jnp.minimum(vel_ref[s, d], 0.0) for d in range(3)]
-        downs = [jnp.maximum(vel_ref[s, d], 0.0) for d in range(3)]
         u = u_ref[q]
-        w_sib = jnp.where(even, ups[0], downs[0])
-        w_cross = jnp.where(even, downs[0], ups[0])
-        new = u + (kappa * c_sib + w_sib) * (sib_ref[q] - u)
-        new = new + (kappa * c_cross + w_cross) * (cross_ref[q] - u)
-        new = new + (kappa * c_yp + ups[1]) * (ahead_row(u) - u)
-        new = new + (kappa * c_ym + downs[1]) * (behind_row(u) - u)
-        new = new + (kappa * c_zp + ups[2]) * (ahead_col(u) - u)
-        new = new + (kappa * c_zm + downs[2]) * (behind_col(u) - u)
+        rates = [table_ref[ROWS * q + k : ROWS * q + k + 1, :] for k in range(7)]
+        new = u
+        for k, move in enumerate(moves):
+            new = new + (rates[0] * coefs[k] + rates[3 + k]) * (move(u) - u)
+        out_ref[q] = new
+
+
+def interior(state, visc, table):
+    return pl.pallas_call(
+        interior_kernel,
+        out_shape=jax.ShapeDtypeStruct((RUNS, EXT, NZ), jnp.float32),
+        in_specs=[VMEM] * 3,
+        out_specs=VMEM,
+        compiler_params=params(),
+        cost_estimate=pl.CostEstimate(flops=4000000, bytes_accessed=1400000, transcendentals=0),
+        name="interior",
+    )(state, visc, table)
+
+
+def close_kernel(edge, want, acc_ref, u_ref, sib_ref, cross_ref, v_ref, vs_ref, vc_ref, table_ref, *outs):
+    run = lax.axis_index("run")
+    row = sub_iota((EXT, NZ)) + (BLOCK * run - HALO)
+    inside = (row >= 0) & (row < NY)
+    if edge:
+        place = (lax.axis_index("x") * 8 + lax.axis_index("y")) * 2 + lax.axis_index("core")
+        inside = inside & (place > 0) & (place < NX - 1)
+    v = v_ref[RUNS]
+    c_sib = v + vs_ref[RUNS]
+    c_cross = v + vc_ref[RUNS]
+    for q in range(RUNS):
+        rates = [table_ref[ROWS * q + k : ROWS * q + k + 1, :] for k in range(3)]
+        u = u_ref[q]
+        new = acc_ref[q] + (rates[0] * c_sib + rates[1]) * (sib_ref[q] - u)
+        new = new + (rates[0] * c_cross + rates[2]) * (cross_ref[q] - u)
         new = jnp.where(inside, new, 0.0)
-        if not last:
+        if "full" in want:
             outs[0][q] = new
-        outs[-1][q] = pltpu.roll(new, EXT - HALO, 0)[:BLOCK]
-
-
-def advance(last, coefs, state, sib, cross, visc, visc_sib, visc_cross):
-    core = jax.ShapeDtypeStruct((RUNS, BLOCK, NZ), jnp.float32)
-    full = jax.ShapeDtypeStruct((RUNS, EXT, NZ), jnp.float32)
-    out = (core,) if last else (full, core)
+        if "core" in want:
+            outs[-1][q] = pltpu.roll(new, EXT - HALO, 0)[:BLOCK]
+
+
+def close(want, acc, u, sib, cross, v, v_sib, v_cross, table, edge=False):
+    sizes = [EXT] * ("full" in want) + [BLOCK] * ("core" in want)
+    args = [acc, u, sib, cross, v, v_sib, v_cross, table]
 
     def body(*refs):
-        step_kernel(last, *refs)
+        close_kernel(edge, want, *refs)
 
     return pl.pallas_call(
         body,
-        out_shape=out,
-        in_specs=[SMEM, SMEM, SMEM] + [VMEM] * 6,
-        out_specs=tuple(VMEM for _ in out),
-        compiler_params=params(),
-        cost_estimate=pl.CostEstimate(flops=6000000, bytes_accessed=4000000, transcendentals=0),
-        name="step_last" if last else "step",
-    )(*coefs, state, sib, cross, visc, visc_sib, visc_cross)
+        out_shape=tuple(jax.ShapeDtypeStruct((RUNS, rows, NZ), jnp.float32) for rows in sizes),
+        in_specs=[VMEM] * len(args),
+        out_specs=tuple(VMEM for _ in sizes),
+        compiler_params=params(),
+        cost_estimate=pl.CostEstimate(flops=1200000, bytes_accessed=1600000, transcendentals=0),
+        name="close_" + "_".join(want),
+    )(*args)
 
 
 def merge(x, y, width):
@@ -170,31 +225,33 @@
     for other in range(group + 1):
         theirs = cores[other]
         for half in range(2):
-            accs = tuple(jnp.zeros((8, 128), jnp.float32) for _ in range(32))
-
-            def body(i, accs, theirs=theirs, half=half):
+            first = 4 if other == group and half else 0
+            wide = 8 - first
+            accs = tuple(jnp.zeros((8, 128), jnp.float32) for _ in range(4 * wide))
+
+            def body(i, accs, theirs=theirs, half=half, first=first, wide=wide):
                 rows = pl.ds(pl.multiple_of(8 * i, 8), 8)
                 accs = list(accs)
                 for l in range(NZ // 128):
                     cols = slice(128 * l, 128 * l + 128)
                     a = [mine[4 * half + k, rows, cols] for k in range(4)]
-                    for b in range(8):
-                        t = theirs[b, rows, cols]
+                    for b in range(wide):
+                        t = theirs[first + b, rows, cols]
                         for k in range(4):
-                            accs[8 * k + b] = accs[8 * k + b] + a[k] * t
+                            accs[wide * k + b] = accs[wide * k + b] + a[k] * t
                 return tuple(accs)
 
             accs = lax.fori_loop(0, BLOCK // 8, body, accs)
             for k in range(4):
-                level = list(accs[8 * k : 8 * k + 8])
+                level = [jnp.zeros((8, 128), jnp.float32)] * first + list(accs[wide * k : wide * k + wide])
                 for width in (4, 2, 1):
                     count = len(level) // 2
                     level = [merge(level[i], level[i + count], width) for i in range(count)]
                 total = jnp.sum(level[0], axis=1, keepdims=True)
-                at = 32 * other + 8 * group + 4 * half + k
+                at = 32 * other + STEPS * (4 * half + k) + group
                 packed = jnp.where(lane == at, total, packed)
     if last:
-        for i in range(RUNS):
+        for i in range(FIRST):
             out_ref[i] = packed
     else:
         out_ref[...] = packed
@@ -202,7 +259,7 @@
 
 def gram(cores, prev, last):
     group = len(cores) - 1
-    shape = (RUNS, 8, 128) if last else (8, 128)
+    shape = (FIRST, 8, 128) if last else (8, 128)
     args = list(cores) + ([prev] if group else [])
 
     def body(*refs):
@@ -221,18 +278,19 @@
 
 def spread_kernel(in_ref, out_ref):
     total = in_ref[0]
-    for i in range(1, RUNS):
+    for i in range(1, FIRST):
         total = total + in_ref[i]
-    for i in range(RUNS):
+    for i in range(SECOND):
         out_ref[i] = total
 
 
 def spread(parts):
     return pl.pallas_call(
         spread_kernel,
-        out_shape=jax.ShapeDtypeStruct(parts.shape, jnp.float32),
+        out_shape=jax.ShapeDtypeStruct((SECOND, 8, 128), jnp.float32),
         in_specs=[VMEM],
         out_specs=VMEM,
+        compiler_params=params(),
         name="spread",
     )(parts)
 
@@ -326,9 +384,11 @@
     return jnp.concatenate(rows, axis=0) if nodes > 1 else rows[0]
 
 
-def finish_kernel(order_ref, keep_ref, part_ref, c0, c1, c2, c3, out_ref, w_ref):
+def finish_kernel(order_ref, keep_ref, part_ref, *refs):
+    out_ref, w_ref = refs[-2:]
+    cores = refs[:STEPS]
     packed = part_ref[0]
-    for i in range(1, RUNS):
+    for i in range(1, part_ref.shape[0]):
         packed = packed + part_ref[i]
     size = RUNS * STEPS
     raw = jnp.concatenate(
@@ -337,15 +397,12 @@
     sub = sub_iota((size, 128))
     lane = lane_iota((size, 128))
     raw = jnp.where(lane < size, raw, 0.0)
-    square = jnp.concatenate([raw, jnp.zeros((128 - size, 128), jnp.float32)], axis=0)
+    perm = jnp.where(lane == 8 * (sub & 3) + (sub >> 2), 1.0, 0.0)
+    full = dot(perm[:, :size], raw)
+    square = jnp.concatenate([full, jnp.zeros((128 - size, 128), jnp.float32)], axis=0)
     mirror = square.T[:size, :]
-    raw = jnp.where((sub >> 3) <= (lane >> 3), raw, mirror)
-    source = 8 * (sub & 3) + (sub >> 2)
-    perm = jnp.where(lane == source, 1.0, 0.0)
-    rows = dot(perm[:, :size], raw)
-    target = 8 * (lane & 3) + (lane >> 2)
-    perm_t = jnp.where((sub == target) & (lane < size), 1.0, 0.0)
-    full = dot(rows[:, :size], perm_t)
+    same = ((sub & 3) == (lane & 3)) & (((lane & 16) == 0) | ((sub & 16) != 0))
+    full = jnp.where(((sub & 3) < (lane & 3)) | same, full, mirror)
     diag = jnp.where(sub == lane, full, 0.0)
     mu_col = jnp.sum(diag, axis=1, keepdims=True) / CELLS
     mu_row = jnp.sum(diag, axis=0, keepdims=True) / CELLS
@@ -369,7 +426,6 @@
     total = total * scale_col
     for c in range(STEPS):
         w_ref[c] = jnp.broadcast_to(total[:, c : c + 1], (size, 128))
-    cores = (c0, c1, c2, c3)
     for l in range(NZ // 128):
         cols = slice(128 * l, 128 * l + 128)
         for i in range(BLOCK // 8):
@@ -390,7 +446,7 @@
     return pl.pallas_call(
         finish_kernel,
         out_shape=jax.ShapeDtypeStruct((STEPS, 1, BLOCK, NZ), jnp.float32),
-        in_specs=[SMEM, SMEM] + [VMEM] * 5,
+        in_specs=[SMEM, SMEM, VMEM] + [VMEM] * STEPS,
         out_specs=VMEM,
         scratch_shapes=[pltpu.VMEM((STEPS, RUNS * STEPS, 128), jnp.float32)],
         compiler_params=params(),
@@ -400,29 +456,49 @@
 
 
 def local(start_field, viscosity, diffusivity, velocity, assignment, child_order, keep_ranks):
-    coefs = (diffusivity, velocity, assignment)
     sibling = [(i, i ^ 1) for i in range(NX)]
     crossing = [(i, i + 1) for i in range(1, NX - 1, 2)] + [(i + 1, i) for i in range(1, NX - 1, 2)]
-    blocks, visc = row_blocks(start_field, viscosity)
-    state = lax.all_to_all(blocks, "run", 0, 0)
-    send = jnp.concatenate([state, visc], axis=0)
+    blocks = lax.all_to_all(row_blocks(start_field), "run", 0, 0)
+    own = assemble(blocks, viscosity)
+    table = run_rates(diffusivity, velocity, assignment)
+    planes = None
     cores = []
     packed = None
-    for step in range(STEPS):
-        cross = lax.ppermute(send, SPACE, crossing)
-        sib = lax.ppermute(send, SPACE, sibling)
-        if cores:
+
+    def swap_cross(a):
+        return lax.ppermute(a, SPACE, crossing)
+
+    def swap_sib(a):
+        return lax.ppermute(a, SPACE, sibling)
+
+    for turn in range(STEPS // 2):
+        sib1 = swap_sib(own)
+        cross1 = swap_cross(own)
+        if planes is None:
+            v, vs1, vc1 = own, sib1, cross1
+        acc_own = interior(own, v, table)
+        acc_sib = interior(sib1, vs1, table)
+        last = turn == STEPS // 2 - 1
+        cross2 = swap_cross(sib1)
+        sib2 = swap_sib(cross1)
+        if planes is None:
+            planes = vs2, vc2 = sib2, cross2
+        acc_cross = interior(cross1, vc1, table)
+        fresh, core = close(("full", "core"), acc_own, own, sib1, cross1, v, vs1, vc1, table)
+        cores.append(core)
+        packed = gram(cores, packed, False)
+        (near_sib,) = close(("full",), acc_sib, sib1, sib2, own, vs1, vs2, v, table)
+        acc_own = interior(fresh, v, table)
+        (near_cross,) = close(("full",), acc_cross, cross1, own, cross2, vc1, v, vc2, table, edge=True)
+        want = ("core",) if last else ("full", "core")
+        result = close(want, acc_own, fresh, near_sib, near_cross, v, vs1, vc1, table)
+        cores.append(result[-1])
+        own = result[0]
+        if not last:
             packed = gram(cores, packed, False)
-        if step == 0:
-            visc_sib, visc_cross = sib[RUNS:], cross[RUNS:]
-        last = step == STEPS - 1
-        result = advance(last, coefs, state, sib, cross, visc, visc_sib, visc_cross)
-        cores.append(result[-1])
-        state = send = result[0]
     parts = gram(cores, packed, True)
-    parts = spread(lax.all_to_all(parts, ("x", "core"), 0, 0))
-    parts = spread(lax.all_to_all(parts, "y", 0, 0))
-    parts = lax.all_to_all(parts, "run", 0, 0)
+    parts = spread(lax.all_to_all(parts, ("y", "core"), 0, 0))
+    parts = lax.all_to_all(parts, ("run", "x"), 0, 0)
     return finish(child_order, keep_ranks, parts, cores)
 
 

time: 149 us -> 117 us (0.79)
  waiting for transfers between devices: 31.4 us -> 15.8 us
  blocking collectives: 67.9 us -> 61.2 us
  starting transfers between devices: 24.8 us -> 20.9 us
  local copies, waits for them, and re-layouts: 3.74 us -> 1.08 us
  Pallas kernels: 19.5 us -> 17.5 us
    ppermute x8, waiting for transfers between devices: 31.4 us -> 15.8 us  [the longest x4 15.8 us: swap_cross(): return lax.ppermute(a, SPACE, crossing)]
    all_to_all x4 -> x3, blocking collectives: 67.9 us -> 61.2 us  [the longest x1 29.9 us: local(): blocks = lax.all_to_all(row_blocks(start_field), 'run', 0, 0)]
    ppermute x8, starting transfers between devices: 24.8 us -> 20.9 us  [the longest x4 11.1 us: swap_cross(): return lax.ppermute(a, SPACE, crossing)]
    unnamed x16 -> x14, local copies, waits for them, and re-layouts: 3.07 us -> 1.08 us
    pallas_call x7 -> x20, Pallas kernels: 9.85 us -> 8.38 us  [the longest x8 5.43 us: interior(): pl.pallas_call(interior_kernel, out_shape=jax.ShapeDtypeStruct((RUNS, EXT...]
  transfers between devices with their start and end apart: 8 -> 8, of which waited for: 4 -> 3; matrix products, arithmetic and copies ran while one was open for 0% -> 0% of each run, Pallas kernels for 2% -> 9%
where the time goes in v3:
time: 117 us
  blocking collectives  61.2 us (52%)
  starting transfers between devices  20.9 us (18%)
  Pallas kernels  17.5 us (15%)
  waiting for transfers between devices  15.8 us (14%)
    all_to_all x1, blocking collectives, local(): blocks = lax.all_to_all(row_blocks(start_field), 'run', 0, 0)  29.9 us
    all_to_all x1, blocking collectives, local(): parts = spread(lax.all_to_all(parts, ('y', 'core'), 0, 0))  17.2 us
    ppermute x4, waiting for transfers between devices, swap_cross(): return lax.ppermute(a, SPACE, crossing)  15.8 us
    all_to_all x1, blocking collectives, local(): parts = lax.all_to_all(parts, ('run', 'x'), 0, 0)  14 us
    ppermute x4, starting transfers between devices, swap_cross(): return lax.ppermute(a, SPACE, crossing)  11.1 us
    ppermute x4, starting transfers between devices, swap_sib(): return lax.ppermute(a, SPACE, sibling)  9.75 us
    pallas_call x8, Pallas kernels, interior(): pl.pallas_call(interior_kernel, out_shape=jax.ShapeDtypeStruct((RUNS, EXT...  5.43 us
    pallas_call x4, Pallas kernels, gram(): pl.pallas_call(body, out_shape=jax.ShapeDtypeStruct(shape, jnp.float32),...  4.96 us
  transfers between devices with their start and end apart: 8, of which 3 were waited for; matrix products, arithmetic and copies ran while one was open for 0% of the time, Pallas kernels for 9%

profile of v3, /device:TPU:1, one launch (start us, length us, event | category | flops | bytes accessed | tf_op | source)
XLA Modules:
  0.0 116.7 jit_solution(9066494004770186512)
XLA Ops:
  0.0 1.0 copy-done
  1.1 29.9 %all_to_all.15.state_ref = f32[8,40,512]{2,1,0:T(8,128)S(1)} all-to-all(f32[8,40,512]{2,1,0:T(8,128)S(1)} %row_blocks.1), channel_id=1, replica_groups=mesh['run'=8,'x'=4,'y'=8,'core'=2] {'run'}, dimensions={0} | all-to-all | bytes 1310720 | tf_op jit(solution)/shard_map/all_to_all | solution.py:461
  31.1 4.0 %collective-permute-start = (f32[9,40,512]{2,1,0:T(8,128)S(1)}, f32[9,40,512]{2,1,0:T(8,128)S(1)}, u32[]{:S(2)}, u32[]{:S(2)}) collective-permute-start(f32[9,40,512]{2,1,0:T(8,128)S(1)} %assemble.1.u_ref.v_ref.refs_1_.refs_4_.refs_3_.refs_6_.refs_2_.refs_5_), channel_id=1, source_target_pairs={{0,1},{1,0},{2,3},{3,2},{4,5},{5,4},{6,7},{7,6},{8,9},{9,8},{10,11... | collective-permute-start | bytes 2211848 | tf_op jit(solution)/shard_map/ppermute | solution.py:472
  35.2 3.1 %collective-permute-start.1 = (f32[9,40,512]{2,1,0:T(8,128)S(1)}, f32[9,40,512]{2,1,0:T(8,128)S(1)}, u32[]{:S(2)}, u32[]{:S(2)}) collective-permute-start(f32[9,40,512]{2,1,0:T(8,128)S(1)} %assemble.1.u_ref.v_ref.refs_1_.refs_4_.refs_3_.refs_6_.refs_2_.refs_5_), channel_id=1, source_target_pairs={{1,2},{3,4},{5,6},{7,8},{9,10},{11,12},{13,14},{15,16},{17,18},{19... | collective-permute-start | bytes 2211848 | tf_op jit(solution)/shard_map/ppermute | solution.py:469
  38.3 2.5 %collective-permute-start.3 = (f32[9,40,512]{2,1,0:T(8,128)S(1)}, f32[9,40,512]{2,1,0:T(8,128)S(1)}, u32[]{:S(2)}, u32[]{:S(2)}) collective-permute-start(f32[9,40,512]{2,1,0:T(8,128)S(1)} %collective-permute-done.refs_2_.refs_5_.u_ref.v_ref.refs_1_.refs_4_), channel_id=1, source_target_pairs={{1,2},{3,4},{5,6},{7,8},{9,10},{11,12},{13,14},{15,16},{17,18},{19... | collective-permute-start | bytes 2211848 | tf_op jit(solution)/shard_map/ppermute | solution.py:469
  40.8 7.2 %collective-permute-done.1.refs_3_.refs_6_.u_ref.v_ref.refs_1_.refs_4_ = f32[9,40,512]{2,1,0:T(8,128)S(1)} collective-permute-done((f32[9,40,512]{2,1,0:T(8,128)S(1)}, f32[9,40,512]{2,1,0:T(8,128)S(1)}, u32[]{:S(2)}, u32[]{:S(2)}) %collective-permute-start.1) | collective-permute-done | bytes 737312 | tf_op jit(solution)/shard_map/ppermute | solution.py:469
  48.0 1.9 %collective-permute-start.2 = (f32[9,40,512]{2,1,0:T(8,128)S(1)}, f32[9,40,512]{2,1,0:T(8,128)S(1)}, u32[]{:S(2)}, u32[]{:S(2)}) collective-permute-start(f32[9,40,512]{2,1,0:T(8,128)S(1)} %collective-permute-done.1.refs_3_.refs_6_.u_ref.v_ref.refs_1_.refs_4_), channel_id=1, source_target_pairs={{0,1},{1,0},{2,3},{3,2},{4,5},{5,4},{6,7},{7,6},{8,9},{9,8},{10,11... | collective-permute-start | bytes 2211848 | tf_op jit(solution)/shard_map/ppermute | solution.py:472
  50.5 0.7 interior.8.refs_0_
  51.5 0.7 interior.9.refs_0_
  52.2 0.7 interior.11.refs_0_
  52.9 0.7 interior.10.refs_0_
  53.6 2.3 %collective-permute-done.3.refs_3_.refs_6_ = f32[9,40,512]{2,1,0:T(8,128)S(1)} collective-permute-done((f32[9,40,512]{2,1,0:T(8,128)S(1)}, f32[9,40,512]{2,1,0:T(8,128)S(1)}, u32[]{:S(2)}, u32[]{:S(2)}) %collective-permute-start.3) | collective-permute-done | bytes 737312 | tf_op jit(solution)/shard_map/ppermute | solution.py:469
  56.7 1.9 %collective-permute-start.4 = (f32[8,40,512]{2,1,0:T(8,128)S(1)}, f32[8,40,512]{2,1,0:T(8,128)S(1)}, u32[]{:S(2)}, u32[]{:S(2)}) collective-permute-start(f32[8,40,512]{2,1,0:T(8,128)S(1)} %get-tuple-element.14.u_ref.refs_1_.refs_3_.refs_2_), channel_id=1, source_target_pairs={{0,1},{1,0},{2,3},{3,2},{4,5},{5,4},{6,7},{7,6},{8,9},{9,8},{10,11... | collective-permute-start | bytes 1966088 | tf_op jit(solution)/shard_map/ppermute | solution.py:472
  58.6 3.6 %collective-permute-start.5 = (f32[8,40,512]{2,1,0:T(8,128)S(1)}, f32[8,40,512]{2,1,0:T(8,128)S(1)}, u32[]{:S(2)}, u32[]{:S(2)}) collective-permute-start(f32[8,40,512]{2,1,0:T(8,128)S(1)} %get-tuple-element.14.u_ref.refs_1_.refs_3_.refs_2_), channel_id=1, source_target_pairs={{1,2},{3,4},{5,6},{7,8},{9,10},{11,12},{13,14},{15,16},{17,18},{19... | collective-permute-start | bytes 1966088 | tf_op jit(solution)/shard_map/ppermute | solution.py:469
  62.2 2.0 %collective-permute-start.7 = (f32[8,40,512]{2,1,0:T(8,128)S(1)}, f32[8,40,512]{2,1,0:T(8,128)S(1)}, u32[]{:S(2)}, u32[]{:S(2)}) collective-permute-start(f32[8,40,512]{2,1,0:T(8,128)S(1)} %collective-permute-done.4.refs_2_.u_ref.refs_1_), channel_id=1, source_target_pairs={{1,2},{3,4},{5,6},{7,8},{9,10},{11,12},{13,14},{15,16},{17,18},{19... | collective-permute-start | bytes 1966088 | tf_op jit(solution)/shard_map/ppermute | solution.py:469
  64.2 6.3 %collective-permute-done.5.refs_3_.u_ref.refs_1_ = f32[8,40,512]{2,1,0:T(8,128)S(1)} collective-permute-done((f32[8,40,512]{2,1,0:T(8,128)S(1)}, f32[8,40,512]{2,1,0:T(8,128)S(1)}, u32[]{:S(2)}, u32[]{:S(2)}) %collective-permute-start.5) | collective-permute-done | bytes 655392 | tf_op jit(solution)/shard_map/ppermute | solution.py:469
  70.5 1.9 %collective-permute-start.6 = (f32[8,40,512]{2,1,0:T(8,128)S(1)}, f32[8,40,512]{2,1,0:T(8,128)S(1)}, u32[]{:S(2)}, u32[]{:S(2)}) collective-permute-start(f32[8,40,512]{2,1,0:T(8,128)S(1)} %collective-permute-done.5.refs_3_.u_ref.refs_1_), channel_id=1, source_target_pairs={{0,1},{1,0},{2,3},{3,2},{4,5},{5,4},{6,7},{7,6},{8,9},{9,8},{10,11... | collective-permute-start | bytes 1966088 | tf_op jit(solution)/shard_map/ppermute | solution.py:472
  72.8 0.7 interior.12.refs_0_
  73.5 1.0 gram1.1.refs_3_
  76.8 1.5 %gram2.1.refs_4_ = f32[8,128]{1,0:T(8,128)S(1)} custom-call(f32[8,32,512]{2,1,0:T(8,128)S(1)} %get-tuple-element.11.refs_0_, f32[8,32,512]{2,1,0:T(8,128)S(1)} %get-tuple-element.13.refs_1_, f32[8,32,512]{2,1,0:T(8,128)S(1)} %get-tuple-element.15.refs_2_, f32[8,128]{1,0:T(8,128)S(1)} %gram1.1.refs_3_), custom_call_target="tpu_custom_call" | custom-call | flops 6600000 | bytes 1800000 | tf_op jit(solution)/shard_map/gram2/pallas_call | solution.py:268
  79.2 2.1 %gram3.1 = f32[16,8,128]{2,1,0:T(8,128)S(1)} custom-call(f32[8,32,512]{2,1,0:T(8,128)S(1)} %get-tuple-element.11.refs_0_, f32[8,32,512]{2,1,0:T(8,128)S(1)} %get-tuple-element.13.refs_1_, f32[8,32,512]{2,1,0:T(8,128)S(1)} %get-tuple-element.15.refs_2_, f32[8,32,512]{2,1,0:T(8,128)S(1)} %close_core.1.refs_3_, f32[8,128]{1,0:T(8,128)S(1)} %gram2.1.refs_4_), custom_call_target="tpu_custom_call" | custom-call | flops 8800000 | bytes 2400000 | tf_op jit(solution)/shard_map/gram3/pallas_call | solution.py:268
  81.3 17.2 %all_to_all.16.in_ref = f32[16,8,128]{2,1,0:T(8,128)S(1)} all-to-all(f32[16,8,128]{2,1,0:T(8,128)S(1)} %gram3.1), channel_id=1, replica_groups=mesh['run'=8,'x'=4,'y'=8,'core'=2] {'y','core'}, dimensions={0} | all-to-all | bytes 131072 | tf_op jit(solution)/shard_map/all_to_all | solution.py:500
  98.5 14.0 %all_to_all.17.part_ref = f32[32,8,128]{2,1,0:T(8,128)S(1)} all-to-all(f32[32,8,128]{2,1,0:T(8,128)S(1)} %spread.1), channel_id=1, replica_groups=mesh['run'=8,'x'=4,'y'=8,'core'=2] {'run','x'}, dimensions={0} | all-to-all | bytes 262144 | tf_op jit(solution)/shard_map/all_to_all | solution.py:501
  112.6 4.1 %finish.1 = f32[4,1,32,512]{3,2,1,0:T(8,128)} custom-call(s32[7,8]{1,0:T(8,128)S(1)} %copy-done.2, s32[7]{0:T(128)S(1)} %copy-done.6, f32[32,8,128]{2,1,0:T(8,128)S(1)} %all_to_all.17.part_ref, f32[8,32,512]{2,1,0:T(8,128)S(1)} %get-tuple-element.11.refs_0_, f32[8,32,512]{2,1,0:T(8,128)S(1)} %get-tuple-element.13.refs_1_, ...), custom_call_target="tpu_custom_call" | custom-call | flops 5000000 | bytes 2400000 | tf_op jit(solution)/shard_map/finish/pallas_call | solution.py:446
  (34 shorter events, 5.4 us)
Async XLA Ops:
  0.0 1.0 copy-start
  1.1 30.0 %copy-start.1 = (f32[1,256,512]{2,1,0:T(8,128)S(1)}, f32[1,256,512]{2,1,0:T(8,128)}, u32[]{:S(2)}) copy-start(f32[1,256,512]{2,1,0:T(8,128)} %visc_ref.1) | copy-start | bytes 1572868
  31.1 18.8 %copy-start.3 = (f32[8,3]{0,1:T(4,128)S(1)}, f32[8,3]{0,1:T(4,128)}, u32[]{:S(2)}) copy-start(f32[8,3]{0,1:T(4,128)} %param.10) | copy-start | bytes 292
  31.1 18.8 %copy-start.4 = (f32[8]{0:T(128)S(1)}, f32[8]{0:T(128)}, u32[]{:S(2)}) copy-start(f32[8]{0:T(128)} %diff_ref.1) | copy-start | bytes 100
  31.1 18.8 %copy-start.5 = (s32[8]{0:T(128)S(1)}, s32[8]{0:T(128)}, u32[]{:S(2)}) copy-start(s32[8]{0:T(128)} %assign_ref.1) | copy-start | bytes 100
  31.1 7.1 %collective-permute-start = (f32[9,40,512]{2,1,0:T(8,128)S(1)}, f32[9,40,512]{2,1,0:T(8,128)S(1)}, u32[]{:S(2)}, u32[]{:S(2)}) collective-permute-start(f32[9,40,512]{2,1,0:T(8,128)S(1)} %assemble.1.u_ref.v_ref.refs_1_.refs_4_.refs_3_.refs_6_.refs_2_.refs_5_), channel_id=1, source_target_pairs={{0,1},{1,0},{2,3},{3,2},{4,5},{5,4},{6,7},{7,6},{8,9},{9,8},{10,11... | collective-permute-start | bytes 2211848 | tf_op jit(solution)/shard_map/ppermute | solution.py:472
  35.2 12.8 %collective-permute-start.1 = (f32[9,40,512]{2,1,0:T(8,128)S(1)}, f32[9,40,512]{2,1,0:T(8,128)S(1)}, u32[]{:S(2)}, u32[]{:S(2)}) collective-permute-start(f32[9,40,512]{2,1,0:T(8,128)S(1)} %assemble.1.u_ref.v_ref.refs_1_.refs_4_.refs_3_.refs_6_.refs_2_.refs_5_), channel_id=1, source_target_pairs={{1,2},{3,4},{5,6},{7,8},{9,10},{11,12},{13,14},{15,16},{17,18},{19... | collective-permute-start | bytes 2211848 | tf_op jit(solution)/shard_map/ppermute | solution.py:469
  38.3 17.6 %collective-permute-start.3 = (f32[9,40,512]{2,1,0:T(8,128)S(1)}, f32[9,40,512]{2,1,0:T(8,128)S(1)}, u32[]{:S(2)}, u32[]{:S(2)}) collective-permute-start(f32[9,40,512]{2,1,0:T(8,128)S(1)} %collective-permute-done.refs_2_.refs_5_.u_ref.v_ref.refs_1_.refs_4_), channel_id=1, source_target_pairs={{1,2},{3,4},{5,6},{7,8},{9,10},{11,12},{13,14},{15,16},{17,18},{19... | collective-permute-start | bytes 2211848 | tf_op jit(solution)/shard_map/ppermute | solution.py:469
  48.0 8.2 %collective-permute-start.2 = (f32[9,40,512]{2,1,0:T(8,128)S(1)}, f32[9,40,512]{2,1,0:T(8,128)S(1)}, u32[]{:S(2)}, u32[]{:S(2)}) collective-permute-start(f32[9,40,512]{2,1,0:T(8,128)S(1)} %collective-permute-done.1.refs_3_.refs_6_.u_ref.v_ref.refs_1_.refs_4_), channel_id=1, source_target_pairs={{0,1},{1,0},{2,3},{3,2},{4,5},{5,4},{6,7},{7,6},{8,9},{9,8},{10,11... | collective-permute-start | bytes 2211848 | tf_op jit(solution)/shard_map/ppermute | solution.py:472
  56.7 5.5 %collective-permute-start.4 = (f32[8,40,512]{2,1,0:T(8,128)S(1)}, f32[8,40,512]{2,1,0:T(8,128)S(1)}, u32[]{:S(2)}, u32[]{:S(2)}) collective-permute-start(f32[8,40,512]{2,1,0:T(8,128)S(1)} %get-tuple-element.14.u_ref.refs_1_.refs_3_.refs_2_), channel_id=1, source_target_pairs={{0,1},{1,0},{2,3},{3,2},{4,5},{5,4},{6,7},{7,6},{8,9},{9,8},{10,11... | collective-permute-start | bytes 1966088 | tf_op jit(solution)/shard_map/ppermute | solution.py:472
  58.6 11.9 %collective-permute-start.5 = (f32[8,40,512]{2,1,0:T(8,128)S(1)}, f32[8,40,512]{2,1,0:T(8,128)S(1)}, u32[]{:S(2)}, u32[]{:S(2)}) collective-permute-start(f32[8,40,512]{2,1,0:T(8,128)S(1)} %get-tuple-element.14.u_ref.refs_1_.refs_3_.refs_2_), channel_id=1, source_target_pairs={{1,2},{3,4},{5,6},{7,8},{9,10},{11,12},{13,14},{15,16},{17,18},{19... | collective-permute-start | bytes 1966088 | tf_op jit(solution)/shard_map/ppermute | solution.py:469
  62.2 16.1 %collective-permute-start.7 = (f32[8,40,512]{2,1,0:T(8,128)S(1)}, f32[8,40,512]{2,1,0:T(8,128)S(1)}, u32[]{:S(2)}, u32[]{:S(2)}) collective-permute-start(f32[8,40,512]{2,1,0:T(8,128)S(1)} %collective-permute-done.4.refs_2_.u_ref.refs_1_), channel_id=1, source_target_pairs={{1,2},{3,4},{5,6},{7,8},{9,10},{11,12},{13,14},{15,16},{17,18},{19... | collective-permute-start | bytes 1966088 | tf_op jit(solution)/shard_map/ppermute | solution.py:469
  70.5 8.1 %collective-permute-start.6 = (f32[8,40,512]{2,1,0:T(8,128)S(1)}, f32[8,40,512]{2,1,0:T(8,128)S(1)}, u32[]{:S(2)}, u32[]{:S(2)}) collective-permute-start(f32[8,40,512]{2,1,0:T(8,128)S(1)} %collective-permute-done.5.refs_3_.u_ref.refs_1_), channel_id=1, source_target_pairs={{0,1},{1,0},{2,3},{3,2},{4,5},{5,4},{6,7},{7,6},{8,9},{9,8},{10,11... | collective-permute-start | bytes 1966088 | tf_op jit(solution)/shard_map/ppermute | solution.py:472
  98.5 14.1 %copy-start.2 = (s32[7,8]{1,0:T(8,128)S(1)}, s32[7,8]{1,0:T(8,128)}, u32[]{:S(2)}) copy-start(s32[7,8]{1,0:T(8,128)} %order_ref.1) | copy-start | bytes 676
  98.5 14.0 %copy-start.6 = (s32[7]{0:T(128)S(1)}, s32[7]{0:T(128)}, u32[]{:S(2)}) copy-start(s32[7]{0:T(128)} %keep_ref.1) | copy-start | bytes 88

commit v4 on v3

--- a/solution.py
+++ b/solution.py
@@ -122,6 +122,23 @@
     )(state, visc)
 
 
+def trim_kernel(in_ref, out_ref):
+    for q in range(RUNS):
+        out_ref[q] = pltpu.roll(in_ref[q], EXT - HALO, 0)[:BLOCK]
+
+
+def trim(plane):
+    return pl.pallas_call(
+        trim_kernel,
+        out_shape=jax.ShapeDtypeStruct((RUNS, BLOCK, NZ), jnp.float32),
+        in_specs=[VMEM],
+        out_specs=VMEM,
+        compiler_params=params(),
+        cost_estimate=pl.CostEstimate(flops=0, bytes_accessed=1200000, transcendentals=0),
+        name="trim",
+    )(plane)
+
+
 def interior_kernel(u_ref, v_ref, table_ref, out_ref):
     col = lane_iota((EXT, NZ))
     first_col = col == 0
@@ -161,6 +178,12 @@
         cost_estimate=pl.CostEstimate(flops=4000000, bytes_accessed=1400000, transcendentals=0),
         name="interior",
     )(state, visc, table)
+
+
+def padded(rows):
+    if rows.shape[0] == EXT:
+        return rows
+    return pltpu.roll(jnp.concatenate([rows, jnp.zeros((2 * HALO, NZ), jnp.float32)], axis=0), HALO, 0)
 
 
 def close_kernel(edge, want, acc_ref, u_ref, sib_ref, cross_ref, v_ref, vs_ref, vc_ref, table_ref, *outs):
@@ -176,8 +199,9 @@
     for q in range(RUNS):
         rates = [table_ref[ROWS * q + k : ROWS * q + k + 1, :] for k in range(3)]
         u = u_ref[q]
-        new = acc_ref[q] + (rates[0] * c_sib + rates[1]) * (sib_ref[q] - u)
-        new = new + (rates[0] * c_cross + rates[2]) * (cross_ref[q] - u)
+        new = acc_ref[q] + (rates[0] * c_sib + rates[1]) * (padded(sib_ref[q]) - u)
+        across = padded(cross_ref[q])
+        new = new + (rates[0] * c_cross + rates[2]) * (across - u)
         new = jnp.where(inside, new, 0.0)
         if "full" in want:
             outs[0][q] = new
@@ -230,7 +254,7 @@
             accs = tuple(jnp.zeros((8, 128), jnp.float32) for _ in range(4 * wide))
 
             def body(i, accs, theirs=theirs, half=half, first=first, wide=wide):
-                rows = pl.ds(pl.multiple_of(8 * i, 8), 8)
+                rows = slice(8 * i, 8 * i + 8)
                 accs = list(accs)
                 for l in range(NZ // 128):
                     cols = slice(128 * l, 128 * l + 128)
@@ -241,7 +265,8 @@
                             accs[wide * k + b] = accs[wide * k + b] + a[k] * t
                 return tuple(accs)
 
-            accs = lax.fori_loop(0, BLOCK // 8, body, accs)
+            for i in range(BLOCK // 8):
+                accs = body(i, accs)
             for k in range(4):
                 level = [jnp.zeros((8, 128), jnp.float32)] * first + list(accs[wide * k : wide * k + wide])
                 for width in (4, 2, 1):
@@ -313,24 +338,52 @@
     return a
 
 
-def level_basis(gram_now, nodes, first_node, order_ref, keep_ref):
+def starts_kernel(order_ref, keep_ref, out_ref):
     shape = (8, 128)
     sub = sub_iota(shape)
+    table = dct()
+    nodes = RUNS // 2
+    first_node = 0
+    level = 0
+    while nodes:
+        lane = lane_iota(shape) & (nodes - 1)
+        basis = [jnp.zeros(shape, jnp.float32) for _ in range(STEPS)]
+        live = [jnp.zeros(shape, jnp.float32) for _ in range(STEPS)]
+        for k in range(nodes):
+            node = first_node + k
+            here = lane == k
+            for c in range(STEPS):
+                flag = jnp.where(keep_ref[node] > c, 1.0, 0.0)
+                live[c] = jnp.where(here, flag, live[c])
+            for i in range(2 * STEPS):
+                spot = here & (sub == order_ref[node, i])
+                for c in range(STEPS):
+                    basis[c] = jnp.where(spot, table[i][c], basis[c])
+        for c in range(STEPS):
+            out_ref[2 * STEPS * level + c] = basis[c] * live[c]
+            out_ref[2 * STEPS * level + STEPS + c] = live[c]
+        first_node += nodes
+        nodes //= 2
+        level += 1
+
+
+def starts(order, keep):
+    return pl.pallas_call(
+        starts_kernel,
+        out_shape=jax.ShapeDtypeStruct((3 * 2 * STEPS, 8, 128), jnp.float32),
+        in_specs=[SMEM, SMEM],
+        out_specs=VMEM,
+        compiler_params=params(),
+        cost_estimate=pl.CostEstimate(flops=0, bytes_accessed=100000, transcendentals=0),
+        name="starts",
+    )(order, keep)
+
+
+def level_basis(gram_now, nodes, level, start_ref):
+    shape = (8, 128)
     lane = lane_iota(shape) & (nodes - 1)
-    table = dct()
-    basis = [jnp.zeros(shape, jnp.float32) for _ in range(STEPS)]
-    live = [jnp.zeros(shape, jnp.float32) for _ in range(STEPS)]
-    for k in range(nodes):
-        node = first_node + k
-        here = lane == k
-        for c in range(STEPS):
-            flag = jnp.where(keep_ref[node] > c, 1.0, 0.0)
-            live[c] = jnp.where(here, flag, live[c])
-        for i in range(2 * STEPS):
-            spot = here & (sub == order_ref[node, i])
-            for c in range(STEPS):
-                basis[c] = jnp.where(spot, table[i][c], basis[c])
-    basis = [z * m for z, m in zip(basis, live)]
+    basis = [start_ref[2 * STEPS * level + c] for c in range(STEPS)]
+    live = [start_ref[2 * STEPS * level + STEPS + c] for c in range(STEPS)]
     cols = []
     for j in range(8):
         col = jnp.zeros(shape, jnp.float32)
@@ -356,7 +409,8 @@
             pivot = inner[b, b]
             for k in range(b):
                 pivot = pivot - low[b, k] * low[b, k]
-            root = 1.0 / jnp.sqrt(pivot)
+            root = lax.rsqrt(pivot)
+            root = root * (1.5 - 0.5 * pivot * root * root)
             inv.append(root)
             for a in range(b + 1, STEPS):
                 entry = inner[a, b]
@@ -384,7 +438,7 @@
     return jnp.concatenate(rows, axis=0) if nodes > 1 else rows[0]
 
 
-def finish_kernel(order_ref, keep_ref, part_ref, *refs):
+def finish_kernel(start_ref, part_ref, *refs):
     out_ref, w_ref = refs[-2:]
     cores = refs[:STEPS]
     packed = part_ref[0]
@@ -410,10 +464,10 @@
     scale_row = 1.0 / jnp.sqrt(mu_row + EPS)
     gram_now = full * scale_col * scale_row / CELLS
     nodes = RUNS // 2
-    first_node = 0
+    level = 0
     total = None
     while nodes:
-        basis = level_basis(gram_now, nodes, first_node, order_ref, keep_ref)
+        basis = level_basis(gram_now, nodes, level, start_ref)
         w = weights(basis, nodes)
         rows_now = 8 * nodes
         total = w if total is None else dot(total[:, :rows_now], w)
@@ -421,38 +475,40 @@
             half = dot(gram_now[:, :rows_now], w)
             w_t = jnp.concatenate([w, jnp.zeros((128 - rows_now, 128), jnp.float32)], axis=0).T
             gram_now = dot(w_t[: STEPS * nodes, :rows_now], half)
-        first_node += nodes
+        level += 1
         nodes //= 2
     total = total * scale_col
     for c in range(STEPS):
         w_ref[c] = jnp.broadcast_to(total[:, c : c + 1], (size, 128))
+    tiles = [slice(8 * i, 8 * i + 8) for i in range(BLOCK // 8)]
     for l in range(NZ // 128):
         cols = slice(128 * l, 128 * l + 128)
-        for i in range(BLOCK // 8):
-            rws = slice(8 * i, 8 * i + 8)
-            accs = [None] * STEPS
-            for q in range(RUNS):
-                for t in range(STEPS):
-                    x = cores[t][q, rws, cols]
-                    k = STEPS * q + t
-                    for c in range(STEPS):
-                        term = w_ref[c, k : k + 1, :] * x
-                        accs[c] = term if accs[c] is None else accs[c] + term
-            for c in range(STEPS):
-                out_ref[c, 0, rws, cols] = accs[c]
-
-
-def finish(order, keep, parts, cores):
+        accs = [[None] * len(tiles) for _ in range(STEPS)]
+        for q in range(RUNS):
+            for t in range(STEPS):
+                k = STEPS * q + t
+                xs = [cores[t][q, rows, cols] for rows in tiles]
+                for c in range(STEPS):
+                    weight = jnp.broadcast_to(w_ref[c, k : k + 1, :], (8, 128))
+                    for i, x in enumerate(xs):
+                        term = weight * x
+                        accs[c][i] = term if accs[c][i] is None else accs[c][i] + term
+        for c in range(STEPS):
+            for i, rows in enumerate(tiles):
+                out_ref[c, 0, rows, cols] = accs[c][i]
+
+
+def finish(start, parts, cores):
     return pl.pallas_call(
         finish_kernel,
         out_shape=jax.ShapeDtypeStruct((STEPS, 1, BLOCK, NZ), jnp.float32),
-        in_specs=[SMEM, SMEM, VMEM] + [VMEM] * STEPS,
+        in_specs=[VMEM] * (2 + STEPS),
         out_specs=VMEM,
         scratch_shapes=[pltpu.VMEM((STEPS, RUNS * STEPS, 128), jnp.float32)],
         compiler_params=params(),
         cost_estimate=pl.CostEstimate(flops=5000000, bytes_accessed=2400000, transcendentals=0),
         name="finish",
-    )(order, keep, parts, *cores)
+    )(start, parts, *cores)
 
 
 def local(start_field, viscosity, diffusivity, velocity, assignment, child_order, keep_ranks):
@@ -461,6 +517,7 @@
     blocks = lax.all_to_all(row_blocks(start_field), "run", 0, 0)
     own = assemble(blocks, viscosity)
     table = run_rates(diffusivity, velocity, assignment)
+    start = starts(child_order, keep_ranks)
     planes = None
     cores = []
     packed = None
@@ -479,8 +536,14 @@
         acc_own = interior(own, v, table)
         acc_sib = interior(sib1, vs1, table)
         last = turn == STEPS // 2 - 1
-        cross2 = swap_cross(sib1)
-        sib2 = swap_sib(cross1)
+        cross2 = swap_cross(trim(sib1) if last else sib1)
+        if cores:
+            early = (cross1, packed, acc_own)
+            cross1, packed, acc_own = lax.optimization_barrier(early)
+        else:
+            early = (cross1, acc_own, start)
+            cross1, acc_own, start = lax.optimization_barrier(early)
+        sib2 = swap_sib(trim(cross1) if last else cross1)
         if planes is None:
             planes = vs2, vc2 = sib2, cross2
         acc_cross = interior(cross1, vc1, table)
@@ -499,7 +562,7 @@
     parts = gram(cores, packed, True)
     parts = spread(lax.all_to_all(parts, ("y", "core"), 0, 0))
     parts = lax.all_to_all(parts, ("run", "x"), 0, 0)
-    return finish(child_order, keep_ranks, parts, cores)
+    return finish(start, parts, cores)
 
 
 def solution(mesh):

time: 117 us -> 113 us (0.966)
  waiting for transfers between devices: 15.8 us -> 13 us
  Pallas kernels: 17.5 us -> 15.8 us
    ppermute x4, waiting for transfers between devices: 15.8 us -> 13 us  [swap_cross(): return lax.ppermute(a, SPACE, crossing)]
    pallas_call x4, Pallas kernels: 4.96 us -> 3.01 us  [gram(): pl.pallas_call(body, out_shape=jax.ShapeDtypeStruct(shape, jnp.float32),...]
  transfers between devices with their start and end apart: 8 -> 8, of which waited for: 3 -> 4; matrix products, arithmetic and copies ran while one was open for 0% -> 0% of each run, Pallas kernels for 9% -> 9%
where the time goes in v4:
time: 113 us
  blocking collectives  61.1 us (54%)
  starting transfers between devices  21.1 us (19%)
  Pallas kernels  15.8 us (14%)
  waiting for transfers between devices  13 us (12%)
  local copies, waits for them, and re-layouts  1.71 us (2%)
    all_to_all x1, blocking collectives, local(): blocks = lax.all_to_all(row_blocks(start_field), 'run', 0, 0)  29.9 us
    all_to_all x1, blocking collectives, local(): parts = spread(lax.all_to_all(parts, ('y', 'core'), 0, 0))  17.1 us
    all_to_all x1, blocking collectives, local(): parts = lax.all_to_all(parts, ('run', 'x'), 0, 0)  14 us
    ppermute x4, waiting for transfers between devices, swap_cross(): return lax.ppermute(a, SPACE, crossing)  13 us
    ppermute x4, starting transfers between devices, swap_cross(): return lax.ppermute(a, SPACE, crossing)  11.1 us
    ppermute x4, starting transfers between devices, swap_sib(): return lax.ppermute(a, SPACE, sibling)  9.95 us
    pallas_call x8, Pallas kernels, interior(): pl.pallas_call(interior_kernel, out_shape=jax.ShapeDtypeStruct((RUNS, EXT...  5.43 us
    pallas_call x1, Pallas kernels, finish(): pl.pallas_call(finish_kernel, out_shape=jax.ShapeDtypeStruct((STEPS, 1, B...  3.44 us
  transfers between devices with their start and end apart: 8, of which 4 were waited for; matrix products, arithmetic and copies ran while one was open for 0% of the time, Pallas kernels for 9%

profile of v4, /device:TPU:1, one launch (start us, length us, event | category | flops | bytes accessed | tf_op | source)
XLA Modules:
  0.0 113.0 jit_solution(2959493463990191814)
XLA Ops:
  0.0 1.0 copy-done
  1.1 29.9 %all_to_all.15.state_ref = f32[8,40,512]{2,1,0:T(8,128)S(1)} all-to-all(f32[8,40,512]{2,1,0:T(8,128)S(1)} %row_blocks.1), channel_id=1, replica_groups=mesh['run'=8,'x'=4,'y'=8,'core'=2] {'run'}, dimensions={0} | all-to-all | bytes 1310720 | tf_op jit(solution)/shard_map/all_to_all | solution.py:517
  31.1 4.0 %collective-permute-start.1 = (f32[9,40,512]{2,1,0:T(8,128)S(1)}, f32[9,40,512]{2,1,0:T(8,128)S(1)}, u32[]{:S(2)}, u32[]{:S(2)}) collective-permute-start(f32[9,40,512]{2,1,0:T(8,128)S(1)} %assemble.1.u_ref.v_ref.refs_1_.refs_4_.refs_3_.refs_6_.refs_2_.refs_5_), channel_id=1, source_target_pairs={{0,1},{1,0},{2,3},{3,2},{4,5},{5,4},{6,7},{7,6},{8,9},{9,8},{10,11... | collective-permute-start | bytes 2211848 | tf_op jit(solution)/shard_map/ppermute | solution.py:529
  35.1 3.1 %collective-permute-start = (f32[9,40,512]{2,1,0:T(8,128)S(1)}, f32[9,40,512]{2,1,0:T(8,128)S(1)}, u32[]{:S(2)}, u32[]{:S(2)}) collective-permute-start(f32[9,40,512]{2,1,0:T(8,128)S(1)} %assemble.1.u_ref.v_ref.refs_1_.refs_4_.refs_3_.refs_6_.refs_2_.refs_5_), channel_id=1, source_target_pairs={{1,2},{3,4},{5,6},{7,8},{9,10},{11,12},{13,14},{15,16},{17,18},{19... | collective-permute-start | bytes 2211848 | tf_op jit(solution)/shard_map/ppermute | solution.py:526
  38.3 0.7 starts.1.start_ref
  40.3 0.7 interior.8.refs_0_
  41.0 2.5 %collective-permute-start.3 = (f32[9,40,512]{2,1,0:T(8,128)S(1)}, f32[9,40,512]{2,1,0:T(8,128)S(1)}, u32[]{:S(2)}, u32[]{:S(2)}) collective-permute-start(f32[9,40,512]{2,1,0:T(8,128)S(1)} %collective-permute-done.1.refs_2_.refs_5_.u_ref.v_ref.refs_1_.refs_4_), channel_id=1, source_target_pairs={{1,2},{3,4},{5,6},{7,8},{9,10},{11,12},{13,14},{15,16},{17,18},{19... | collective-permute-start | bytes 2211848 | tf_op jit(solution)/shard_map/ppermute | solution.py:526
  43.5 4.5 %collective-permute-done.refs_3_.refs_6_.u_ref.v_ref.refs_1_.refs_4_ = f32[9,40,512]{2,1,0:T(8,128)S(1)} collective-permute-done((f32[9,40,512]{2,1,0:T(8,128)S(1)}, f32[9,40,512]{2,1,0:T(8,128)S(1)}, u32[]{:S(2)}, u32[]{:S(2)}) %collective-permute-start) | collective-permute-done | bytes 737312 | tf_op jit(solution)/shard_map/ppermute | solution.py:526
  47.9 1.9 %collective-permute-start.2 = (f32[9,40,512]{2,1,0:T(8,128)S(1)}, f32[9,40,512]{2,1,0:T(8,128)S(1)}, u32[]{:S(2)}, u32[]{:S(2)}) collective-permute-start(f32[9,40,512]{2,1,0:T(8,128)S(1)} %collective-permute-done.refs_3_.refs_6_.u_ref.v_ref.refs_1_.refs_4_), channel_id=1, source_target_pairs={{0,1},{1,0},{2,3},{3,2},{4,5},{5,4},{6,7},{7,6},{8,9},{9,8},{10,11... | collective-permute-start | bytes 2211848 | tf_op jit(solution)/shard_map/ppermute | solution.py:529
  50.2 0.7 interior.9.refs_0_
  50.8 0.7 interior.11.refs_0_
  51.5 0.7 interior.10.refs_0_
  52.2 3.6 %collective-permute-done.3.refs_3_.refs_6_ = f32[9,40,512]{2,1,0:T(8,128)S(1)} collective-permute-done((f32[9,40,512]{2,1,0:T(8,128)S(1)}, f32[9,40,512]{2,1,0:T(8,128)S(1)}, u32[]{:S(2)}, u32[]{:S(2)}) %collective-permute-start.3) | collective-permute-done | bytes 737312 | tf_op jit(solution)/shard_map/ppermute | solution.py:526
  56.7 1.9 %collective-permute-start.5 = (f32[8,40,512]{2,1,0:T(8,128)S(1)}, f32[8,40,512]{2,1,0:T(8,128)S(1)}, u32[]{:S(2)}, u32[]{:S(2)}) collective-permute-start(f32[8,40,512]{2,1,0:T(8,128)S(1)} %get-tuple-element.23.u_ref.refs_1_.refs_3_.refs_2_), channel_id=1, source_target_pairs={{0,1},{1,0},{2,3},{3,2},{4,5},{5,4},{6,7},{7,6},{8,9},{9,8},{10,11... | collective-permute-start | bytes 1966088 | tf_op jit(solution)/shard_map/ppermute | solution.py:529
  58.6 3.6 %collective-permute-start.4 = (f32[8,40,512]{2,1,0:T(8,128)S(1)}, f32[8,40,512]{2,1,0:T(8,128)S(1)}, u32[]{:S(2)}, u32[]{:S(2)}) collective-permute-start(f32[8,40,512]{2,1,0:T(8,128)S(1)} %get-tuple-element.23.u_ref.refs_1_.refs_3_.refs_2_), channel_id=1, source_target_pairs={{1,2},{3,4},{5,6},{7,8},{9,10},{11,12},{13,14},{15,16},{17,18},{19... | collective-permute-start | bytes 1966088 | tf_op jit(solution)/shard_map/ppermute | solution.py:526
  63.8 2.0 %collective-permute-start.7 = (f32[8,32,512]{2,1,0:T(8,128)S(1)}, f32[8,32,512]{2,1,0:T(8,128)S(1)}, u32[]{:S(2)}, u32[]{:S(2)}) collective-permute-start(f32[8,32,512]{2,1,0:T(8,128)S(1)} %trim.3), channel_id=1, source_target_pairs={{1,2},{3,4},{5,6},{7,8},{9,10},{11,12},{13,14},{15,16},{17,18},{19... | collective-permute-start | bytes 1572872 | tf_op jit(solution)/shard_map/ppermute | solution.py:526
  65.8 4.7 %collective-permute-done.4.refs_3_.in_ref.u_ref.refs_1_ = f32[8,40,512]{2,1,0:T(8,128)S(1)} collective-permute-done((f32[8,40,512]{2,1,0:T(8,128)S(1)}, f32[8,40,512]{2,1,0:T(8,128)S(1)}, u32[]{:S(2)}, u32[]{:S(2)}) %collective-permute-start.4) | collective-permute-done | bytes 655392 | tf_op jit(solution)/shard_map/ppermute | solution.py:526
  70.5 2.1 %collective-permute-start.6 = (f32[8,32,512]{2,1,0:T(8,128)S(1)}, f32[8,32,512]{2,1,0:T(8,128)S(1)}, u32[]{:S(2)}, u32[]{:S(2)}) collective-permute-start(f32[8,32,512]{2,1,0:T(8,128)S(1)} %trim.2), channel_id=1, source_target_pairs={{0,1},{1,0},{2,3},{3,2},{4,5},{5,4},{6,7},{7,6},{8,9},{9,8},{10,11... | collective-permute-start | bytes 1572872 | tf_op jit(solution)/shard_map/ppermute | solution.py:529
  72.9 0.7 interior.13.refs_0_
  75.0 0.9 gram2.1.refs_4_
  77.1 1.2 %gram3.1 = f32[16,8,128]{2,1,0:T(8,128)S(1)} custom-call(f32[8,32,512]{2,1,0:T(8,128)S(1)} %get-tuple-element.20.refs_0_, f32[8,32,512]{2,1,0:T(8,128)S(1)} %get-tuple-element.22.refs_1_, f32[8,32,512]{2,1,0:T(8,128)S(1)} %get-tuple-element.26.refs_2_, f32[8,32,512]{2,1,0:T(8,128)S(1)} %close_core.1.refs_3_, f32[8,128]{1,0:T(8,128)S(1)} %gram2.1.refs_4_), custom_call_target="tpu_custom_call" | custom-call | flops 8800000 | bytes 2400000 | tf_op jit(solution)/shard_map/gram3/pallas_call | solution.py:293
  78.3 17.1 %all_to_all.16.in_ref = f32[16,8,128]{2,1,0:T(8,128)S(1)} all-to-all(f32[16,8,128]{2,1,0:T(8,128)S(1)} %gram3.1), channel_id=1, replica_groups=mesh['run'=8,'x'=4,'y'=8,'core'=2] {'y','core'}, dimensions={0} | all-to-all | bytes 131072 | tf_op jit(solution)/shard_map/all_to_all | solution.py:563
  95.5 14.0 %all_to_all.17.part_ref = f32[32,8,128]{2,1,0:T(8,128)S(1)} all-to-all(f32[32,8,128]{2,1,0:T(8,128)S(1)} %spread.1), channel_id=1, replica_groups=mesh['run'=8,'x'=4,'y'=8,'core'=2] {'run','x'}, dimensions={0} | all-to-all | bytes 262144 | tf_op jit(solution)/shard_map/all_to_all | solution.py:564
  109.5 3.4 %finish.1 = f32[4,1,32,512]{3,2,1,0:T(8,128)} custom-call(f32[24,8,128]{2,1,0:T(8,128)S(1)} %starts.1.start_ref, f32[32,8,128]{2,1,0:T(8,128)S(1)} %all_to_all.17.part_ref, f32[8,32,512]{2,1,0:T(8,128)S(1)} %get-tuple-element.20.refs_0_, f32[8,32,512]{2,1,0:T(8,128)S(1)} %get-tuple-element.22.refs_1_, f32[8,32,512]{2,1,0:T(8,128)S(1)} %get-tuple-element.26.refs_2_, ...), custom_call_target="tpu_custom_call" | custom-call | flops 5000000 | bytes 2400000 | tf_op jit(solution)/shard_map/finish/pallas_call | solution.py:502
  (37 shorter events, 7.0 us)
Async XLA Ops:
  0.0 1.0 copy-start
  1.1 30.0 %copy-start.1 = (f32[1,256,512]{2,1,0:T(8,128)S(1)}, f32[1,256,512]{2,1,0:T(8,128)}, u32[]{:S(2)}) copy-start(f32[1,256,512]{2,1,0:T(8,128)} %visc_ref.1) | copy-start | bytes 1572868
  31.1 7.2 %copy-start.2 = (s32[7,8]{1,0:T(8,128)S(1)}, s32[7,8]{1,0:T(8,128)}, u32[]{:S(2)}) copy-start(s32[7,8]{1,0:T(8,128)} %order_ref.1) | copy-start | bytes 676
  31.1 7.2 %copy-start.4 = (s32[7]{0:T(128)S(1)}, s32[7]{0:T(128)}, u32[]{:S(2)}) copy-start(s32[7]{0:T(128)} %keep_ref.1) | copy-start | bytes 88
  31.1 9.9 %collective-permute-start.1 = (f32[9,40,512]{2,1,0:T(8,128)S(1)}, f32[9,40,512]{2,1,0:T(8,128)S(1)}, u32[]{:S(2)}, u32[]{:S(2)}) collective-permute-start(f32[9,40,512]{2,1,0:T(8,128)S(1)} %assemble.1.u_ref.v_ref.refs_1_.refs_4_.refs_3_.refs_6_.refs_2_.refs_5_), channel_id=1, source_target_pairs={{0,1},{1,0},{2,3},{3,2},{4,5},{5,4},{6,7},{7,6},{8,9},{9,8},{10,11... | collective-permute-start | bytes 2211848 | tf_op jit(solution)/shard_map/ppermute | solution.py:529
  35.1 12.8 %collective-permute-start = (f32[9,40,512]{2,1,0:T(8,128)S(1)}, f32[9,40,512]{2,1,0:T(8,128)S(1)}, u32[]{:S(2)}, u32[]{:S(2)}) collective-permute-start(f32[9,40,512]{2,1,0:T(8,128)S(1)} %assemble.1.u_ref.v_ref.refs_1_.refs_4_.refs_3_.refs_6_.refs_2_.refs_5_), channel_id=1, source_target_pairs={{1,2},{3,4},{5,6},{7,8},{9,10},{11,12},{13,14},{15,16},{17,18},{19... | collective-permute-start | bytes 2211848 | tf_op jit(solution)/shard_map/ppermute | solution.py:526
  38.3 0.7 copy-start.3
  39.0 0.7 copy-start.5
  39.0 0.7 copy-start.6
  41.0 14.8 %collective-permute-start.3 = (f32[9,40,512]{2,1,0:T(8,128)S(1)}, f32[9,40,512]{2,1,0:T(8,128)S(1)}, u32[]{:S(2)}, u32[]{:S(2)}) collective-permute-start(f32[9,40,512]{2,1,0:T(8,128)S(1)} %collective-permute-done.1.refs_2_.refs_5_.u_ref.v_ref.refs_1_.refs_4_), channel_id=1, source_target_pairs={{1,2},{3,4},{5,6},{7,8},{9,10},{11,12},{13,14},{15,16},{17,18},{19... | collective-permute-start | bytes 2211848 | tf_op jit(solution)/shard_map/ppermute | solution.py:526
  47.9 8.2 %collective-permute-start.2 = (f32[9,40,512]{2,1,0:T(8,128)S(1)}, f32[9,40,512]{2,1,0:T(8,128)S(1)}, u32[]{:S(2)}, u32[]{:S(2)}) collective-permute-start(f32[9,40,512]{2,1,0:T(8,128)S(1)} %collective-permute-done.refs_3_.refs_6_.u_ref.v_ref.refs_1_.refs_4_), channel_id=1, source_target_pairs={{0,1},{1,0},{2,3},{3,2},{4,5},{5,4},{6,7},{7,6},{8,9},{9,8},{10,11... | collective-permute-start | bytes 2211848 | tf_op jit(solution)/shard_map/ppermute | solution.py:529
  56.7 7.1 %collective-permute-start.5 = (f32[8,40,512]{2,1,0:T(8,128)S(1)}, f32[8,40,512]{2,1,0:T(8,128)S(1)}, u32[]{:S(2)}, u32[]{:S(2)}) collective-permute-start(f32[8,40,512]{2,1,0:T(8,128)S(1)} %get-tuple-element.23.u_ref.refs_1_.refs_3_.refs_2_), channel_id=1, source_target_pairs={{0,1},{1,0},{2,3},{3,2},{4,5},{5,4},{6,7},{7,6},{8,9},{9,8},{10,11... | collective-permute-start | bytes 1966088 | tf_op jit(solution)/shard_map/ppermute | solution.py:529
  58.6 11.9 %collective-permute-start.4 = (f32[8,40,512]{2,1,0:T(8,128)S(1)}, f32[8,40,512]{2,1,0:T(8,128)S(1)}, u32[]{:S(2)}, u32[]{:S(2)}) collective-permute-start(f32[8,40,512]{2,1,0:T(8,128)S(1)} %get-tuple-element.23.u_ref.refs_1_.refs_3_.refs_2_), channel_id=1, source_target_pairs={{1,2},{3,4},{5,6},{7,8},{9,10},{11,12},{13,14},{15,16},{17,18},{19... | collective-permute-start | bytes 1966088 | tf_op jit(solution)/shard_map/ppermute | solution.py:526
  63.8 12.3 %collective-permute-start.7 = (f32[8,32,512]{2,1,0:T(8,128)S(1)}, f32[8,32,512]{2,1,0:T(8,128)S(1)}, u32[]{:S(2)}, u32[]{:S(2)}) collective-permute-start(f32[8,32,512]{2,1,0:T(8,128)S(1)} %trim.3), channel_id=1, source_target_pairs={{1,2},{3,4},{5,6},{7,8},{9,10},{11,12},{13,14},{15,16},{17,18},{19... | collective-permute-start | bytes 1572872 | tf_op jit(solution)/shard_map/ppermute | solution.py:526
  70.5 5.9 %collective-permute-start.6 = (f32[8,32,512]{2,1,0:T(8,128)S(1)}, f32[8,32,512]{2,1,0:T(8,128)S(1)}, u32[]{:S(2)}, u32[]{:S(2)}) collective-permute-start(f32[8,32,512]{2,1,0:T(8,128)S(1)} %trim.2), channel_id=1, source_target_pairs={{0,1},{1,0},{2,3},{3,2},{4,5},{5,4},{6,7},{7,6},{8,9},{9,8},{10,11... | collective-permute-start | bytes 1572872 | tf_op jit(solution)/shard_map/ppermute | solution.py:529

commit v5 on v4

--- a/solution.py
+++ b/solution.py
@@ -451,8 +451,15 @@
     sub = sub_iota((size, 128))
     lane = lane_iota((size, 128))
     raw = jnp.where(lane < size, raw, 0.0)
-    perm = jnp.where(lane == 8 * (sub & 3) + (sub >> 2), 1.0, 0.0)
-    full = dot(perm[:, :size], raw)
+    eight = sub_iota((8, 128))
+    blocks = []
+    for m in range(STEPS):
+        block = jnp.zeros((8, 128), jnp.float32)
+        for r in range(8):
+            at = 8 * (r & 3) + 2 * m + (r >> 2)
+            block = jnp.where(eight == r, raw[at : at + 1, :], block)
+        blocks.append(block)
+    full = jnp.concatenate(blocks, axis=0)
     square = jnp.concatenate([full, jnp.zeros((128 - size, 128), jnp.float32)], axis=0)
     mirror = square.T[:size, :]
     same = ((sub & 3) == (lane & 3)) & (((lane & 16) == 0) | ((sub & 16) != 0))
@@ -473,8 +480,16 @@
         total = w if total is None else dot(total[:, :rows_now], w)
         if nodes > 1:
             half = dot(gram_now[:, :rows_now], w)
-            w_t = jnp.concatenate([w, jnp.zeros((128 - rows_now, 128), jnp.float32)], axis=0).T
-            gram_now = dot(w_t[: STEPS * nodes, :rows_now], half)
+            rows = []
+            for b in range(nodes // 2):
+                block = jnp.zeros((8, 128), jnp.float32)
+                for r in range(8):
+                    k = 2 * b + (r >> 2)
+                    column = basis[r & 3][:, k : k + 1]
+                    row = sublane_sum(column * half[8 * k : 8 * k + 8, :])
+                    block = jnp.where(eight == r, row, block)
+                rows.append(block)
+            gram_now = jnp.concatenate(rows, axis=0) if len(rows) > 1 else rows[0]
         level += 1
         nodes //= 2
     total = total * scale_col
@@ -541,8 +556,8 @@
             early = (cross1, packed, acc_own)
             cross1, packed, acc_own = lax.optimization_barrier(early)
         else:
-            early = (cross1, acc_own, start)
-            cross1, acc_own, start = lax.optimization_barrier(early)
+            early = (cross1, acc_own, acc_sib, start)
+            cross1, acc_own, acc_sib, start = lax.optimization_barrier(early)
         sib2 = swap_sib(trim(cross1) if last else cross1)
         if planes is None:
             planes = vs2, vc2 = sib2, cross2

time: 113 us -> 113 us (level)
  no operation moved by 1% of the time
where the time goes in v5:
time: 113 us
  blocking collectives  61.1 us (54%)
  starting transfers between devices  21.1 us (19%)
  Pallas kernels  15.4 us (14%)
  waiting for transfers between devices  13 us (12%)
  local copies, waits for them, and re-layouts  1.71 us (2%)
    all_to_all x1, blocking collectives, local(): blocks = lax.all_to_all(row_blocks(start_field), 'run', 0, 0)  29.9 us
    all_to_all x1, blocking collectives, local(): parts = spread(lax.all_to_all(parts, ('y', 'core'), 0, 0))  17.1 us
    all_to_all x1, blocking collectives, local(): parts = lax.all_to_all(parts, ('run', 'x'), 0, 0)  14 us
    ppermute x4, waiting for transfers between devices, swap_cross(): return lax.ppermute(a, SPACE, crossing)  13 us
    ppermute x4, starting transfers between devices, swap_cross(): return lax.ppermute(a, SPACE, crossing)  11.1 us
    ppermute x4, starting transfers between devices, swap_sib(): return lax.ppermute(a, SPACE, sibling)  9.95 us
    pallas_call x8, Pallas kernels, interior(): pl.pallas_call(interior_kernel, out_shape=jax.ShapeDtypeStruct((RUNS, EXT...  5.43 us
    pallas_call x1, Pallas kernels, finish(): pl.pallas_call(finish_kernel, out_shape=jax.ShapeDtypeStruct((STEPS, 1, B...  3.05 us
  transfers between devices with their start and end apart: 8, of which 4 were waited for; matrix products, arithmetic and copies ran while one was open for 0% of the time, Pallas kernels for 9%

profile of v5, /device:TPU:1, one launch (start us, length us, event | category | flops | bytes accessed | tf_op | source)
XLA Modules:
  0.0 112.6 jit_solution(250944515909304856)
XLA Ops:
  0.0 1.0 copy-done
  1.1 29.9 %all_to_all.15.state_ref = f32[8,40,512]{2,1,0:T(8,128)S(1)} all-to-all(f32[8,40,512]{2,1,0:T(8,128)S(1)} %row_blocks.1), channel_id=1, replica_groups=mesh['run'=8,'x'=4,'y'=8,'core'=2] {'run'}, dimensions={0} | all-to-all | bytes 1310720 | tf_op jit(solution)/shard_map/all_to_all | solution.py:532
  31.1 4.0 %collective-permute-start.1 = (f32[9,40,512]{2,1,0:T(8,128)S(1)}, f32[9,40,512]{2,1,0:T(8,128)S(1)}, u32[]{:S(2)}, u32[]{:S(2)}) collective-permute-start(f32[9,40,512]{2,1,0:T(8,128)S(1)} %assemble.1.u_ref.v_ref.refs_1_.refs_4_.refs_3_.refs_6_.refs_2_.refs_5_), channel_id=1, source_target_pairs={{0,1},{1,0},{2,3},{3,2},{4,5},{5,4},{6,7},{7,6},{8,9},{9,8},{10,11... | collective-permute-start | bytes 2211848 | tf_op jit(solution)/shard_map/ppermute | solution.py:544
  35.1 3.1 %collective-permute-start = (f32[9,40,512]{2,1,0:T(8,128)S(1)}, f32[9,40,512]{2,1,0:T(8,128)S(1)}, u32[]{:S(2)}, u32[]{:S(2)}) collective-permute-start(f32[9,40,512]{2,1,0:T(8,128)S(1)} %assemble.1.u_ref.v_ref.refs_1_.refs_4_.refs_3_.refs_6_.refs_2_.refs_5_), channel_id=1, source_target_pairs={{1,2},{3,4},{5,6},{7,8},{9,10},{11,12},{13,14},{15,16},{17,18},{19... | collective-permute-start | bytes 2211848 | tf_op jit(solution)/shard_map/ppermute | solution.py:541
  38.3 0.7 starts.1.start_ref
  40.3 0.7 interior.8.refs_0_
  41.0 2.5 %collective-permute-start.3 = (f32[9,40,512]{2,1,0:T(8,128)S(1)}, f32[9,40,512]{2,1,0:T(8,128)S(1)}, u32[]{:S(2)}, u32[]{:S(2)}) collective-permute-start(f32[9,40,512]{2,1,0:T(8,128)S(1)} %collective-permute-done.1.u_ref.v_ref.refs_2_.refs_5_.refs_1_.refs_4_), channel_id=1, source_target_pairs={{1,2},{3,4},{5,6},{7,8},{9,10},{11,12},{13,14},{15,16},{17,18},{19... | collective-permute-start | bytes 2211848 | tf_op jit(solution)/shard_map/ppermute | solution.py:541
  43.5 0.7 interior.9.refs_0_
  44.1 3.8 %collective-permute-done.refs_3_.refs_6_.u_ref.v_ref.refs_1_.refs_4_ = f32[9,40,512]{2,1,0:T(8,128)S(1)} collective-permute-done((f32[9,40,512]{2,1,0:T(8,128)S(1)}, f32[9,40,512]{2,1,0:T(8,128)S(1)}, u32[]{:S(2)}, u32[]{:S(2)}) %collective-permute-start) | collective-permute-done | bytes 737312 | tf_op jit(solution)/shard_map/ppermute | solution.py:541
  47.9 1.9 %collective-permute-start.2 = (f32[9,40,512]{2,1,0:T(8,128)S(1)}, f32[9,40,512]{2,1,0:T(8,128)S(1)}, u32[]{:S(2)}, u32[]{:S(2)}) collective-permute-start(f32[9,40,512]{2,1,0:T(8,128)S(1)} %collective-permute-done.refs_3_.refs_6_.u_ref.v_ref.refs_1_.refs_4_), channel_id=1, source_target_pairs={{0,1},{1,0},{2,3},{3,2},{4,5},{5,4},{6,7},{7,6},{8,9},{9,8},{10,11... | collective-permute-start | bytes 2211848 | tf_op jit(solution)/shard_map/ppermute | solution.py:544
  50.2 0.7 interior.10.refs_0_
  50.8 0.7 interior.11.refs_0_
  51.5 4.3 %collective-permute-done.3.refs_3_.refs_6_ = f32[9,40,512]{2,1,0:T(8,128)S(1)} collective-permute-done((f32[9,40,512]{2,1,0:T(8,128)S(1)}, f32[9,40,512]{2,1,0:T(8,128)S(1)}, u32[]{:S(2)}, u32[]{:S(2)}) %collective-permute-start.3) | collective-permute-done | bytes 737312 | tf_op jit(solution)/shard_map/ppermute | solution.py:541
  56.7 1.9 %collective-permute-start.5 = (f32[8,40,512]{2,1,0:T(8,128)S(1)}, f32[8,40,512]{2,1,0:T(8,128)S(1)}, u32[]{:S(2)}, u32[]{:S(2)}) collective-permute-start(f32[8,40,512]{2,1,0:T(8,128)S(1)} %get-tuple-element.25.u_ref.refs_1_.refs_3_.refs_2_), channel_id=1, source_target_pairs={{0,1},{1,0},{2,3},{3,2},{4,5},{5,4},{6,7},{7,6},{8,9},{9,8},{10,11... | collective-permute-start | bytes 1966088 | tf_op jit(solution)/shard_map/ppermute | solution.py:544
  58.6 3.6 %collective-permute-start.4 = (f32[8,40,512]{2,1,0:T(8,128)S(1)}, f32[8,40,512]{2,1,0:T(8,128)S(1)}, u32[]{:S(2)}, u32[]{:S(2)}) collective-permute-start(f32[8,40,512]{2,1,0:T(8,128)S(1)} %get-tuple-element.25.u_ref.refs_1_.refs_3_.refs_2_), channel_id=1, source_target_pairs={{1,2},{3,4},{5,6},{7,8},{9,10},{11,12},{13,14},{15,16},{17,18},{19... | collective-permute-start | bytes 1966088 | tf_op jit(solution)/shard_map/ppermute | solution.py:541
  63.8 2.0 %collective-permute-start.7 = (f32[8,32,512]{2,1,0:T(8,128)S(1)}, f32[8,32,512]{2,1,0:T(8,128)S(1)}, u32[]{:S(2)}, u32[]{:S(2)}) collective-permute-start(f32[8,32,512]{2,1,0:T(8,128)S(1)} %trim.3), channel_id=1, source_target_pairs={{1,2},{3,4},{5,6},{7,8},{9,10},{11,12},{13,14},{15,16},{17,18},{19... | collective-permute-start | bytes 1572872 | tf_op jit(solution)/shard_map/ppermute | solution.py:541
  65.8 4.7 %collective-permute-done.4.refs_3_.in_ref.u_ref.refs_1_ = f32[8,40,512]{2,1,0:T(8,128)S(1)} collective-permute-done((f32[8,40,512]{2,1,0:T(8,128)S(1)}, f32[8,40,512]{2,1,0:T(8,128)S(1)}, u32[]{:S(2)}, u32[]{:S(2)}) %collective-permute-start.4) | collective-permute-done | bytes 655392 | tf_op jit(solution)/shard_map/ppermute | solution.py:541
  70.5 2.1 %collective-permute-start.6 = (f32[8,32,512]{2,1,0:T(8,128)S(1)}, f32[8,32,512]{2,1,0:T(8,128)S(1)}, u32[]{:S(2)}, u32[]{:S(2)}) collective-permute-start(f32[8,32,512]{2,1,0:T(8,128)S(1)} %trim.2), channel_id=1, source_target_pairs={{0,1},{1,0},{2,3},{3,2},{4,5},{5,4},{6,7},{7,6},{8,9},{9,8},{10,11... | collective-permute-start | bytes 1572872 | tf_op jit(solution)/shard_map/ppermute | solution.py:544
  72.9 0.7 interior.13.refs_0_
  75.0 0.9 gram2.1.refs_4_
  77.1 1.2 %gram3.1 = f32[16,8,128]{2,1,0:T(8,128)S(1)} custom-call(f32[8,32,512]{2,1,0:T(8,128)S(1)} %get-tuple-element.21.refs_0_, f32[8,32,512]{2,1,0:T(8,128)S(1)} %get-tuple-element.24.refs_1_, f32[8,32,512]{2,1,0:T(8,128)S(1)} %get-tuple-element.28.refs_2_, f32[8,32,512]{2,1,0:T(8,128)S(1)} %close_core.1.refs_3_, f32[8,128]{1,0:T(8,128)S(1)} %gram2.1.refs_4_), custom_call_target="tpu_custom_call" | custom-call | flops 8800000 | bytes 2400000 | tf_op jit(solution)/shard_map/gram3/pallas_call | solution.py:293
  78.3 17.1 %all_to_all.16.in_ref = f32[16,8,128]{2,1,0:T(8,128)S(1)} all-to-all(f32[16,8,128]{2,1,0:T(8,128)S(1)} %gram3.1), channel_id=1, replica_groups=mesh['run'=8,'x'=4,'y'=8,'core'=2] {'y','core'}, dimensions={0} | all-to-all | bytes 131072 | tf_op jit(solution)/shard_map/all_to_all | solution.py:578
  95.5 14.0 %all_to_all.17.part_ref = f32[32,8,128]{2,1,0:T(8,128)S(1)} all-to-all(f32[32,8,128]{2,1,0:T(8,128)S(1)} %spread.1), channel_id=1, replica_groups=mesh['run'=8,'x'=4,'y'=8,'core'=2] {'run','x'}, dimensions={0} | all-to-all | bytes 262144 | tf_op jit(solution)/shard_map/all_to_all | solution.py:579
  109.5 3.0 %finish.1 = f32[4,1,32,512]{3,2,1,0:T(8,128)} custom-call(f32[24,8,128]{2,1,0:T(8,128)S(1)} %starts.1.start_ref, f32[32,8,128]{2,1,0:T(8,128)S(1)} %all_to_all.17.part_ref, f32[8,32,512]{2,1,0:T(8,128)S(1)} %get-tuple-element.21.refs_0_, f32[8,32,512]{2,1,0:T(8,128)S(1)} %get-tuple-element.24.refs_1_, f32[8,32,512]{2,1,0:T(8,128)S(1)} %get-tuple-element.28.refs_2_, ...), custom_call_target="tpu_custom_call" | custom-call | flops 5000000 | bytes 2400000 | tf_op jit(solution)/shard_map/finish/pallas_call | solution.py:517
  (37 shorter events, 7.0 us)
Async XLA Ops:
  0.0 1.0 copy-start
  1.1 30.0 %copy-start.1 = (f32[1,256,512]{2,1,0:T(8,128)S(1)}, f32[1,256,512]{2,1,0:T(8,128)}, u32[]{:S(2)}) copy-start(f32[1,256,512]{2,1,0:T(8,128)} %visc_ref.1) | copy-start | bytes 1572868
  31.1 7.2 %copy-start.2 = (s32[7,8]{1,0:T(8,128)S(1)}, s32[7,8]{1,0:T(8,128)}, u32[]{:S(2)}) copy-start(s32[7,8]{1,0:T(8,128)} %order_ref.1) | copy-start | bytes 676
  31.1 7.2 %copy-start.4 = (s32[7]{0:T(128)S(1)}, s32[7]{0:T(128)}, u32[]{:S(2)}) copy-start(s32[7]{0:T(128)} %keep_ref.1) | copy-start | bytes 88
  31.1 9.9 %collective-permute-start.1 = (f32[9,40,512]{2,1,0:T(8,128)S(1)}, f32[9,40,512]{2,1,0:T(8,128)S(1)}, u32[]{:S(2)}, u32[]{:S(2)}) collective-permute-start(f32[9,40,512]{2,1,0:T(8,128)S(1)} %assemble.1.u_ref.v_ref.refs_1_.refs_4_.refs_3_.refs_6_.refs_2_.refs_5_), channel_id=1, source_target_pairs={{0,1},{1,0},{2,3},{3,2},{4,5},{5,4},{6,7},{7,6},{8,9},{9,8},{10,11... | collective-permute-start | bytes 2211848 | tf_op jit(solution)/shard_map/ppermute | solution.py:544
  35.1 12.8 %collective-permute-start = (f32[9,40,512]{2,1,0:T(8,128)S(1)}, f32[9,40,512]{2,1,0:T(8,128)S(1)}, u32[]{:S(2)}, u32[]{:S(2)}) collective-permute-start(f32[9,40,512]{2,1,0:T(8,128)S(1)} %assemble.1.u_ref.v_ref.refs_1_.refs_4_.refs_3_.refs_6_.refs_2_.refs_5_), channel_id=1, source_target_pairs={{1,2},{3,4},{5,6},{7,8},{9,10},{11,12},{13,14},{15,16},{17,18},{19... | collective-permute-start | bytes 2211848 | tf_op jit(solution)/shard_map/ppermute | solution.py:541
  38.3 0.7 copy-start.3
  39.0 0.7 copy-start.5
  39.0 0.7 copy-start.6
  41.0 14.8 %collective-permute-start.3 = (f32[9,40,512]{2,1,0:T(8,128)S(1)}, f32[9,40,512]{2,1,0:T(8,128)S(1)}, u32[]{:S(2)}, u32[]{:S(2)}) collective-permute-start(f32[9,40,512]{2,1,0:T(8,128)S(1)} %collective-permute-done.1.u_ref.v_ref.refs_2_.refs_5_.refs_1_.refs_4_), channel_id=1, source_target_pairs={{1,2},{3,4},{5,6},{7,8},{9,10},{11,12},{13,14},{15,16},{17,18},{19... | collective-permute-start | bytes 2211848 | tf_op jit(solution)/shard_map/ppermute | solution.py:541
  47.9 8.2 %collective-permute-start.2 = (f32[9,40,512]{2,1,0:T(8,128)S(1)}, f32[9,40,512]{2,1,0:T(8,128)S(1)}, u32[]{:S(2)}, u32[]{:S(2)}) collective-permute-start(f32[9,40,512]{2,1,0:T(8,128)S(1)} %collective-permute-done.refs_3_.refs_6_.u_ref.v_ref.refs_1_.refs_4_), channel_id=1, source_target_pairs={{0,1},{1,0},{2,3},{3,2},{4,5},{5,4},{6,7},{7,6},{8,9},{9,8},{10,11... | collective-permute-start | bytes 2211848 | tf_op jit(solution)/shard_map/ppermute | solution.py:544
  56.7 7.1 %collective-permute-start.5 = (f32[8,40,512]{2,1,0:T(8,128)S(1)}, f32[8,40,512]{2,1,0:T(8,128)S(1)}, u32[]{:S(2)}, u32[]{:S(2)}) collective-permute-start(f32[8,40,512]{2,1,0:T(8,128)S(1)} %get-tuple-element.25.u_ref.refs_1_.refs_3_.refs_2_), channel_id=1, source_target_pairs={{0,1},{1,0},{2,3},{3,2},{4,5},{5,4},{6,7},{7,6},{8,9},{9,8},{10,11... | collective-permute-start | bytes 1966088 | tf_op jit(solution)/shard_map/ppermute | solution.py:544
  58.6 11.9 %collective-permute-start.4 = (f32[8,40,512]{2,1,0:T(8,128)S(1)}, f32[8,40,512]{2,1,0:T(8,128)S(1)}, u32[]{:S(2)}, u32[]{:S(2)}) collective-permute-start(f32[8,40,512]{2,1,0:T(8,128)S(1)} %get-tuple-element.25.u_ref.refs_1_.refs_3_.refs_2_), channel_id=1, source_target_pairs={{1,2},{3,4},{5,6},{7,8},{9,10},{11,12},{13,14},{15,16},{17,18},{19... | collective-permute-start | bytes 1966088 | tf_op jit(solution)/shard_map/ppermute | solution.py:541
  63.8 12.3 %collective-permute-start.7 = (f32[8,32,512]{2,1,0:T(8,128)S(1)}, f32[8,32,512]{2,1,0:T(8,128)S(1)}, u32[]{:S(2)}, u32[]{:S(2)}) collective-permute-start(f32[8,32,512]{2,1,0:T(8,128)S(1)} %trim.3), channel_id=1, source_target_pairs={{1,2},{3,4},{5,6},{7,8},{9,10},{11,12},{13,14},{15,16},{17,18},{19... | collective-permute-start | bytes 1572872 | tf_op jit(solution)/shard_map/ppermute | solution.py:541
  70.5 5.9 %collective-permute-start.6 = (f32[8,32,512]{2,1,0:T(8,128)S(1)}, f32[8,32,512]{2,1,0:T(8,128)S(1)}, u32[]{:S(2)}, u32[]{:S(2)}) collective-permute-start(f32[8,32,512]{2,1,0:T(8,128)S(1)} %trim.2), channel_id=1, source_target_pairs={{0,1},{1,0},{2,3},{3,2},{4,5},{5,4},{6,7},{7,6},{8,9},{9,8},{10,11... | collective-permute-start | bytes 1572872 | tf_op jit(solution)/shard_map/ppermute | solution.py:544

commit v6 on v5

--- a/solution.py
+++ b/solution.py
@@ -551,10 +551,10 @@
         acc_own = interior(own, v, table)
         acc_sib = interior(sib1, vs1, table)
         last = turn == STEPS // 2 - 1
-        cross2 = swap_cross(trim(sib1) if last else sib1)
+        cross2 = swap_cross(sib1)
         if cores:
-            early = (cross1, packed, acc_own)
-            cross1, packed, acc_own = lax.optimization_barrier(early)
+            early = (cross1, packed, acc_own, acc_sib)
+            cross1, packed, acc_own, acc_sib = lax.optimization_barrier(early)
         else:
             early = (cross1, acc_own, acc_sib, start)
             cross1, acc_own, acc_sib, start = lax.optimization_barrier(early)

time: 113 us -> 114 us (level)
  no operation moved by 1% of the time
where the time goes in v6:
time: 114 us
  blocking collectives  61.1 us (54%)
  starting transfers between devices  21.1 us (19%)
  Pallas kernels  15.2 us (13%)
  waiting for transfers between devices  14.1 us (12%)
  local copies, waits for them, and re-layouts  1.71 us (2%)
    all_to_all x1, blocking collectives, local(): blocks = lax.all_to_all(row_blocks(start_field), 'run', 0, 0)  29.9 us
    all_to_all x1, blocking collectives, local(): parts = spread(lax.all_to_all(parts, ('y', 'core'), 0, 0))  17.1 us
    ppermute x4, waiting for transfers between devices, swap_cross(): return lax.ppermute(a, SPACE, crossing)  14.1 us
    all_to_all x1, blocking collectives, local(): parts = lax.all_to_all(parts, ('run', 'x'), 0, 0)  14 us
    ppermute x4, starting transfers between devices, swap_cross(): return lax.ppermute(a, SPACE, crossing)  11.1 us
    ppermute x4, starting transfers between devices, swap_sib(): return lax.ppermute(a, SPACE, sibling)  9.95 us
    pallas_call x8, Pallas kernels, interior(): pl.pallas_call(interior_kernel, out_shape=jax.ShapeDtypeStruct((RUNS, EXT...  5.43 us
    pallas_call x1, Pallas kernels, finish(): pl.pallas_call(finish_kernel, out_shape=jax.ShapeDtypeStruct((STEPS, 1, B...  3.05 us
  transfers between devices with their start and end apart: 8, of which 4 were waited for; matrix products, arithmetic and copies ran while one was open for 0% of the time, Pallas kernels for 9%

profile of v6, /device:TPU:1, one launch (start us, length us, event | category | flops | bytes accessed | tf_op | source)
XLA Modules:
  0.0 113.5 jit_solution(1823434865977961378)
XLA Ops:
  0.0 1.0 copy-done
  1.1 29.9 %all_to_all.15.state_ref = f32[8,40,512]{2,1,0:T(8,128)S(1)} all-to-all(f32[8,40,512]{2,1,0:T(8,128)S(1)} %row_blocks.1), channel_id=1, replica_groups=mesh['run'=8,'x'=4,'y'=8,'core'=2] {'run'}, dimensions={0} | all-to-all | bytes 1310720 | tf_op jit(solution)/shard_map/all_to_all | solution.py:532
  31.1 4.0 %collective-permute-start.1 = (f32[9,40,512]{2,1,0:T(8,128)S(1)}, f32[9,40,512]{2,1,0:T(8,128)S(1)}, u32[]{:S(2)}, u32[]{:S(2)}) collective-permute-start(f32[9,40,512]{2,1,0:T(8,128)S(1)} %assemble.1.u_ref.v_ref.refs_1_.refs_4_.refs_3_.refs_6_.refs_2_.refs_5_), channel_id=1, source_target_pairs={{0,1},{1,0},{2,3},{3,2},{4,5},{5,4},{6,7},{7,6},{8,9},{9,8},{10,11... | collective-permute-start | bytes 2211848 | tf_op jit(solution)/shard_map/ppermute | solution.py:544
  35.1 3.1 %collective-permute-start = (f32[9,40,512]{2,1,0:T(8,128)S(1)}, f32[9,40,512]{2,1,0:T(8,128)S(1)}, u32[]{:S(2)}, u32[]{:S(2)}) collective-permute-start(f32[9,40,512]{2,1,0:T(8,128)S(1)} %assemble.1.u_ref.v_ref.refs_1_.refs_4_.refs_3_.refs_6_.refs_2_.refs_5_), channel_id=1, source_target_pairs={{1,2},{3,4},{5,6},{7,8},{9,10},{11,12},{13,14},{15,16},{17,18},{19... | collective-permute-start | bytes 2211848 | tf_op jit(solution)/shard_map/ppermute | solution.py:541
  38.3 0.7 starts.1.start_ref
  40.3 0.7 interior.8.refs_0_
  41.0 2.5 %collective-permute-start.3 = (f32[9,40,512]{2,1,0:T(8,128)S(1)}, f32[9,40,512]{2,1,0:T(8,128)S(1)}, u32[]{:S(2)}, u32[]{:S(2)}) collective-permute-start(f32[9,40,512]{2,1,0:T(8,128)S(1)} %collective-permute-done.1.u_ref.v_ref.refs_2_.refs_5_.refs_1_.refs_4_), channel_id=1, source_target_pairs={{1,2},{3,4},{5,6},{7,8},{9,10},{11,12},{13,14},{15,16},{17,18},{19... | collective-permute-start | bytes 2211848 | tf_op jit(solution)/shard_map/ppermute | solution.py:541
  43.5 0.7 interior.9.refs_0_
  44.1 3.8 %collective-permute-done.refs_3_.refs_6_.u_ref.v_ref.refs_1_.refs_4_ = f32[9,40,512]{2,1,0:T(8,128)S(1)} collective-permute-done((f32[9,40,512]{2,1,0:T(8,128)S(1)}, f32[9,40,512]{2,1,0:T(8,128)S(1)}, u32[]{:S(2)}, u32[]{:S(2)}) %collective-permute-start) | collective-permute-done | bytes 737312 | tf_op jit(solution)/shard_map/ppermute | solution.py:541
  47.9 1.9 %collective-permute-start.2 = (f32[9,40,512]{2,1,0:T(8,128)S(1)}, f32[9,40,512]{2,1,0:T(8,128)S(1)}, u32[]{:S(2)}, u32[]{:S(2)}) collective-permute-start(f32[9,40,512]{2,1,0:T(8,128)S(1)} %collective-permute-done.refs_3_.refs_6_.u_ref.v_ref.refs_1_.refs_4_), channel_id=1, source_target_pairs={{0,1},{1,0},{2,3},{3,2},{4,5},{5,4},{6,7},{7,6},{8,9},{9,8},{10,11... | collective-permute-start | bytes 2211848 | tf_op jit(solution)/shard_map/ppermute | solution.py:544
  50.2 0.7 interior.10.refs_0_
  50.8 0.7 interior.11.refs_0_
  51.5 4.3 %collective-permute-done.3.refs_3_.refs_6_ = f32[9,40,512]{2,1,0:T(8,128)S(1)} collective-permute-done((f32[9,40,512]{2,1,0:T(8,128)S(1)}, f32[9,40,512]{2,1,0:T(8,128)S(1)}, u32[]{:S(2)}, u32[]{:S(2)}) %collective-permute-start.3) | collective-permute-done | bytes 737312 | tf_op jit(solution)/shard_map/ppermute | solution.py:541
  56.7 1.9 %collective-permute-start.5 = (f32[8,40,512]{2,1,0:T(8,128)S(1)}, f32[8,40,512]{2,1,0:T(8,128)S(1)}, u32[]{:S(2)}, u32[]{:S(2)}) collective-permute-start(f32[8,40,512]{2,1,0:T(8,128)S(1)} %get-tuple-element.26.u_ref.refs_1_.refs_3_.refs_2_), channel_id=1, source_target_pairs={{0,1},{1,0},{2,3},{3,2},{4,5},{5,4},{6,7},{7,6},{8,9},{9,8},{10,11... | collective-permute-start | bytes 1966088 | tf_op jit(solution)/shard_map/ppermute | solution.py:544
  58.6 3.6 %collective-permute-start.4 = (f32[8,40,512]{2,1,0:T(8,128)S(1)}, f32[8,40,512]{2,1,0:T(8,128)S(1)}, u32[]{:S(2)}, u32[]{:S(2)}) collective-permute-start(f32[8,40,512]{2,1,0:T(8,128)S(1)} %get-tuple-element.26.u_ref.refs_1_.refs_3_.refs_2_), channel_id=1, source_target_pairs={{1,2},{3,4},{5,6},{7,8},{9,10},{11,12},{13,14},{15,16},{17,18},{19... | collective-permute-start | bytes 1966088 | tf_op jit(solution)/shard_map/ppermute | solution.py:541
  62.2 2.0 %collective-permute-start.7 = (f32[8,40,512]{2,1,0:T(8,128)S(1)}, f32[8,40,512]{2,1,0:T(8,128)S(1)}, u32[]{:S(2)}, u32[]{:S(2)}) collective-permute-start(f32[8,40,512]{2,1,0:T(8,128)S(1)} %collective-permute-done.5.u_ref.refs_2_.refs_1_), channel_id=1, source_target_pairs={{1,2},{3,4},{5,6},{7,8},{9,10},{11,12},{13,14},{15,16},{17,18},{19... | collective-permute-start | bytes 1966088 | tf_op jit(solution)/shard_map/ppermute | solution.py:541
  66.4 4.1 %collective-permute-done.4.refs_3_.in_ref.u_ref.refs_1_ = f32[8,40,512]{2,1,0:T(8,128)S(1)} collective-permute-done((f32[8,40,512]{2,1,0:T(8,128)S(1)}, f32[8,40,512]{2,1,0:T(8,128)S(1)}, u32[]{:S(2)}, u32[]{:S(2)}) %collective-permute-start.4) | collective-permute-done | bytes 655392 | tf_op jit(solution)/shard_map/ppermute | solution.py:541
  70.5 2.1 %collective-permute-start.6 = (f32[8,32,512]{2,1,0:T(8,128)S(1)}, f32[8,32,512]{2,1,0:T(8,128)S(1)}, u32[]{:S(2)}, u32[]{:S(2)}) collective-permute-start(f32[8,32,512]{2,1,0:T(8,128)S(1)} %trim.1), channel_id=1, source_target_pairs={{0,1},{1,0},{2,3},{3,2},{4,5},{5,4},{6,7},{7,6},{8,9},{9,8},{10,11... | collective-permute-start | bytes 1572872 | tf_op jit(solution)/shard_map/ppermute | solution.py:544
  74.3 0.9 gram2.1.refs_4_
  75.5 2.0 %collective-permute-done.7.refs_3_ = f32[8,40,512]{2,1,0:T(8,128)S(1)} collective-permute-done((f32[8,40,512]{2,1,0:T(8,128)S(1)}, f32[8,40,512]{2,1,0:T(8,128)S(1)}, u32[]{:S(2)}, u32[]{:S(2)}) %collective-permute-start.7) | collective-permute-done | bytes 655392 | tf_op jit(solution)/shard_map/ppermute | solution.py:541
  78.1 1.2 %gram3.1 = f32[16,8,128]{2,1,0:T(8,128)S(1)} custom-call(f32[8,32,512]{2,1,0:T(8,128)S(1)} %get-tuple-element.22.refs_0_, f32[8,32,512]{2,1,0:T(8,128)S(1)} %get-tuple-element.25.refs_1_, f32[8,32,512]{2,1,0:T(8,128)S(1)} %get-tuple-element.29.refs_2_, f32[8,32,512]{2,1,0:T(8,128)S(1)} %close_core.1.refs_3_, f32[8,128]{1,0:T(8,128)S(1)} %gram2.1.refs_4_), custom_call_target="tpu_custom_call" | custom-call | flops 8800000 | bytes 2400000 | tf_op jit(solution)/shard_map/gram3/pallas_call | solution.py:293
  79.3 17.1 %all_to_all.16.in_ref = f32[16,8,128]{2,1,0:T(8,128)S(1)} all-to-all(f32[16,8,128]{2,1,0:T(8,128)S(1)} %gram3.1), channel_id=1, replica_groups=mesh['run'=8,'x'=4,'y'=8,'core'=2] {'y','core'}, dimensions={0} | all-to-all | bytes 131072 | tf_op jit(solution)/shard_map/all_to_all | solution.py:578
  96.5 14.0 %all_to_all.17.part_ref = f32[32,8,128]{2,1,0:T(8,128)S(1)} all-to-all(f32[32,8,128]{2,1,0:T(8,128)S(1)} %spread.1), channel_id=1, replica_groups=mesh['run'=8,'x'=4,'y'=8,'core'=2] {'run','x'}, dimensions={0} | all-to-all | bytes 262144 | tf_op jit(solution)/shard_map/all_to_all | solution.py:579
  110.5 3.0 %finish.1 = f32[4,1,32,512]{3,2,1,0:T(8,128)} custom-call(f32[24,8,128]{2,1,0:T(8,128)S(1)} %starts.1.start_ref, f32[32,8,128]{2,1,0:T(8,128)S(1)} %all_to_all.17.part_ref, f32[8,32,512]{2,1,0:T(8,128)S(1)} %get-tuple-element.22.refs_0_, f32[8,32,512]{2,1,0:T(8,128)S(1)} %get-tuple-element.25.refs_1_, f32[8,32,512]{2,1,0:T(8,128)S(1)} %get-tuple-element.29.refs_2_, ...), custom_call_target="tpu_custom_call" | custom-call | flops 5000000 | bytes 2400000 | tf_op jit(solution)/shard_map/finish/pallas_call | solution.py:517
  (36 shorter events, 7.3 us)
Async XLA Ops:
  0.0 1.0 copy-start
  1.1 30.0 %copy-start.1 = (f32[1,256,512]{2,1,0:T(8,128)S(1)}, f32[1,256,512]{2,1,0:T(8,128)}, u32[]{:S(2)}) copy-start(f32[1,256,512]{2,1,0:T(8,128)} %visc_ref.1) | copy-start | bytes 1572868
  31.1 7.2 %copy-start.2 = (s32[7,8]{1,0:T(8,128)S(1)}, s32[7,8]{1,0:T(8,128)}, u32[]{:S(2)}) copy-start(s32[7,8]{1,0:T(8,128)} %order_ref.1) | copy-start | bytes 676
  31.1 7.2 %copy-start.4 = (s32[7]{0:T(128)S(1)}, s32[7]{0:T(128)}, u32[]{:S(2)}) copy-start(s32[7]{0:T(128)} %keep_ref.1) | copy-start | bytes 88
  31.1 9.9 %collective-permute-start.1 = (f32[9,40,512]{2,1,0:T(8,128)S(1)}, f32[9,40,512]{2,1,0:T(8,128)S(1)}, u32[]{:S(2)}, u32[]{:S(2)}) collective-permute-start(f32[9,40,512]{2,1,0:T(8,128)S(1)} %assemble.1.u_ref.v_ref.refs_1_.refs_4_.refs_3_.refs_6_.refs_2_.refs_5_), channel_id=1, source_target_pairs={{0,1},{1,0},{2,3},{3,2},{4,5},{5,4},{6,7},{7,6},{8,9},{9,8},{10,11... | collective-permute-start | bytes 2211848 | tf_op jit(solution)/shard_map/ppermute | solution.py:544
  35.1 12.8 %collective-permute-start = (f32[9,40,512]{2,1,0:T(8,128)S(1)}, f32[9,40,512]{2,1,0:T(8,128)S(1)}, u32[]{:S(2)}, u32[]{:S(2)}) collective-permute-start(f32[9,40,512]{2,1,0:T(8,128)S(1)} %assemble.1.u_ref.v_ref.refs_1_.refs_4_.refs_3_.refs_6_.refs_2_.refs_5_), channel_id=1, source_target_pairs={{1,2},{3,4},{5,6},{7,8},{9,10},{11,12},{13,14},{15,16},{17,18},{19... | collective-permute-start | bytes 2211848 | tf_op jit(solution)/shard_map/ppermute | solution.py:541
  38.3 0.7 copy-start.3
  39.0 0.7 copy-start.5
  39.0 0.7 copy-start.6
  41.0 14.8 %collective-permute-start.3 = (f32[9,40,512]{2,1,0:T(8,128)S(1)}, f32[9,40,512]{2,1,0:T(8,128)S(1)}, u32[]{:S(2)}, u32[]{:S(2)}) collective-permute-start(f32[9,40,512]{2,1,0:T(8,128)S(1)} %collective-permute-done.1.u_ref.v_ref.refs_2_.refs_5_.refs_1_.refs_4_), channel_id=1, source_target_pairs={{1,2},{3,4},{5,6},{7,8},{9,10},{11,12},{13,14},{15,16},{17,18},{19... | collective-permute-start | bytes 2211848 | tf_op jit(solution)/shard_map/ppermute | solution.py:541
  47.9 8.2 %collective-permute-start.2 = (f32[9,40,512]{2,1,0:T(8,128)S(1)}, f32[9,40,512]{2,1,0:T(8,128)S(1)}, u32[]{:S(2)}, u32[]{:S(2)}) collective-permute-start(f32[9,40,512]{2,1,0:T(8,128)S(1)} %collective-permute-done.refs_3_.refs_6_.u_ref.v_ref.refs_1_.refs_4_), channel_id=1, source_target_pairs={{0,1},{1,0},{2,3},{3,2},{4,5},{5,4},{6,7},{7,6},{8,9},{9,8},{10,11... | collective-permute-start | bytes 2211848 | tf_op jit(solution)/shard_map/ppermute | solution.py:544
  56.7 5.5 %collective-permute-start.5 = (f32[8,40,512]{2,1,0:T(8,128)S(1)}, f32[8,40,512]{2,1,0:T(8,128)S(1)}, u32[]{:S(2)}, u32[]{:S(2)}) collective-permute-start(f32[8,40,512]{2,1,0:T(8,128)S(1)} %get-tuple-element.26.u_ref.refs_1_.refs_3_.refs_2_), channel_id=1, source_target_pairs={{0,1},{1,0},{2,3},{3,2},{4,5},{5,4},{6,7},{7,6},{8,9},{9,8},{10,11... | collective-permute-start | bytes 1966088 | tf_op jit(solution)/shard_map/ppermute | solution.py:544
  58.6 11.9 %collective-permute-start.4 = (f32[8,40,512]{2,1,0:T(8,128)S(1)}, f32[8,40,512]{2,1,0:T(8,128)S(1)}, u32[]{:S(2)}, u32[]{:S(2)}) collective-permute-start(f32[8,40,512]{2,1,0:T(8,128)S(1)} %get-tuple-element.26.u_ref.refs_1_.refs_3_.refs_2_), channel_id=1, source_target_pairs={{1,2},{3,4},{5,6},{7,8},{9,10},{11,12},{13,14},{15,16},{17,18},{19... | collective-permute-start | bytes 1966088 | tf_op jit(solution)/shard_map/ppermute | solution.py:541
  62.2 15.3 %collective-permute-start.7 = (f32[8,40,512]{2,1,0:T(8,128)S(1)}, f32[8,40,512]{2,1,0:T(8,128)S(1)}, u32[]{:S(2)}, u32[]{:S(2)}) collective-permute-start(f32[8,40,512]{2,1,0:T(8,128)S(1)} %collective-permute-done.5.u_ref.refs_2_.refs_1_), channel_id=1, source_target_pairs={{1,2},{3,4},{5,6},{7,8},{9,10},{11,12},{13,14},{15,16},{17,18},{19... | collective-permute-start | bytes 1966088 | tf_op jit(solution)/shard_map/ppermute | solution.py:541
  70.5 4.7 %collective-permute-start.6 = (f32[8,32,512]{2,1,0:T(8,128)S(1)}, f32[8,32,512]{2,1,0:T(8,128)S(1)}, u32[]{:S(2)}, u32[]{:S(2)}) collective-permute-start(f32[8,32,512]{2,1,0:T(8,128)S(1)} %trim.1), channel_id=1, source_target_pairs={{0,1},{1,0},{2,3},{3,2},{4,5},{5,4},{6,7},{7,6},{8,9},{9,8},{10,11... | collective-permute-start | bytes 1572872 | tf_op jit(solution)/shard_map/ppermute | solution.py:544
